TPU v7x, 32 devices: a whole 2x2x4 slice. The times are simulated.
32 devices in a mesh: dp: 4 (over x, core), expert: 8 (over z, y).
Axes of the slice: x: 2, y: 2, z: 4, core: 2. Of those that a mesh axis runs over, the one named last changes fastest.
Arguments:
- tokens: bfloat16 [1024, 2048], P('dp', 'expert'), may hold values from -6 to 6
- out_grad: bfloat16 [1024, 2048], P('dp', 'expert'), may hold values from -6 to 6
- expert_out: bfloat16 [1024, 2048], P('dp', 'expert'), may hold values from -0.119628906 to 0.119628906
- router_probs: float32 [1024, 8], P('dp'), may hold values from 0 to 1, as said below
- expert_index: int32 [1024, 1], P('dp'), may hold values from 0 to 7; in each aligned block of 256 rows (0 to 255, 256 to 511, ...) at most 40 rows name the same one
- in_weight: bfloat16 [8, 2, 5120, 2048], P('expert', None, 'dp'), may hold values from -0.125 to 0.125
- down_weight: bfloat16 [8, 5120, 2048], P('expert', 'dp'), may hold values from -0.078125 to 0.078125
- router_weight: bfloat16 [2048, 8], P('expert'), may hold values from -6 to 6
Outputs:
- token_grad: bfloat16 [1024, 2048], P('dp', 'expert')
- in_weight_grad: bfloat16 [8, 2, 5120, 2048], P('expert', None, 'dp')
- router_grad: float32 [2048, 8], P('expert')
Inputs may be any that keep to these rules, and one draw needn't show every extreme that they name: `expert_index`: in each aligned block of 256 tokens (one group) no expert is chosen more than 40 times, so no token is dropped. `router_probs`: each row is positive and sums to one.
All inputs are finite; a program needn't handle non-finite values.
Results may differ from a plain program's by a relative error of at most 0.0057.
Values may be sent and summed in bfloat16 or wider, within the bound.
No kernel may reach another device: no remote copies, remote signals or barrier semaphores. Data moves between devices by JAX's collectives and lax.ppermute only.
A program may use at most 64 MiB of HBM per device.

v0:
```python
import math
from functools import partial

import jax
import jax.numpy as jnp
from jax import lax
from jax.experimental import pallas as pl
from jax.experimental.pallas import tpu as pltpu
from jax.sharding import PartitionSpec as P


aux_coef = 0.2
contract_last = (((1,), (1,)), ((), ()))
contract_first = (((0,), (0,)), ((), ()))


def slot_numbers(routes):
    width = routes.shape[1]
    same_expert = routes[:, :, None] == routes[:, None, :]
    position = jnp.arange(width, dtype=jnp.int32)
    before = position[None, :] < position[:, None]
    return jnp.sum((same_expert & before[None]).astype(jnp.int32), axis=2)


def one_hot(routes, slot_ids, experts, capacity):
    expert_hit = routes[..., None] == jnp.arange(experts, dtype=jnp.int32)
    slot_hit = slot_ids[..., None] == jnp.arange(capacity, dtype=jnp.int32)
    return (expert_hit[..., :, None] & slot_hit[..., None, :]).astype(jnp.float32)


def gelu_parts(pre_act, upstream):
    gelu_value, pullback = jax.vjp(partial(jax.nn.gelu, approximate=True), pre_act)
    return (gelu_value, pullback(upstream)[0])


def swap(value, distance):
    size = lax.axis_size("dp")
    return lax.ppermute(value, "dp", [(i, i ^ distance) for i in range(size)])


def distances():
    found, distance = [], lax.axis_size("dp") // 2
    while distance:
        found.append(distance)
        distance //= 2
    return found


def gather_groups(block, given=()):
    for distance in given or distances():
        block = jnp.concatenate([block, swap(block, distance)], axis=0)
    return block


def reduce_groups(total, first=1):
    order = [distance for distance in distances()[::-1] if distance >= first]
    for distance in order:
        half = total.shape[0] // 2
        away = swap(total[half:].astype(jnp.bfloat16), distance)
        total = total[:half] + away.astype(jnp.float32)
    return total


def weight_grad_kernel(gate_ref, up_ref, rows_ref, out_ref):
    rows = rows_ref[...]
    out_ref[0, 0] = lax.dot_general(
        gate_ref[...], rows, contract_first, preferred_element_type=jnp.float32
    ).astype(jnp.bfloat16)
    out_ref[0, 1] = lax.dot_general(
        up_ref[...], rows, contract_first, preferred_element_type=jnp.float32
    ).astype(jnp.bfloat16)


def weight_grads(gate_grad, up_grad, rows):
    count, hidden = gate_grad.shape
    width = rows.shape[1]
    block = 256 if hidden % 256 == 0 else hidden
    return pl.pallas_call(
        weight_grad_kernel,
        grid=(hidden // block,),
        in_specs=[
            pl.BlockSpec((count, block), lambda j: (0, j)),
            pl.BlockSpec((count, block), lambda j: (0, j)),
            pl.BlockSpec((count, width), lambda j: (0, 0)),
        ],
        out_specs=pl.BlockSpec((1, 2, block, width), lambda j: (0, 0, j, 0)),
        out_shape=jax.ShapeDtypeStruct((1, 2, hidden, width), jnp.bfloat16),
        cost_estimate=pl.CostEstimate(
            flops=4 * count * hidden * width,
            bytes_accessed=4 * hidden * width,
            transcendentals=0,
        ),
        name="weight_grads",
    )(gate_grad, up_grad, rows)


def split_float(value):
    high = lax.reduce_precision(value, 8, 7)
    middle = lax.reduce_precision(value - high, 8, 7)
    return jnp.stack([high, middle, value - high - middle]).astype(jnp.bfloat16)


def general_device(
    tokens, out_grad, expert_out, router_probs, expert_index, in_weight, down_weight, router_weight
):
    token_count, feature_width = tokens.shape
    experts = router_probs.shape[1]
    capacity = (5 * token_count + 4 * experts - 1) // (4 * experts)
    groups = lax.axis_size("dp")
    routes = expert_index[:, 0]
    slot_ids = slot_numbers(routes[None, :])[0]
    dispatch_mask = one_hot(routes, slot_ids, experts, capacity)
    mask_half = dispatch_mask.astype(jnp.bfloat16)
    chosen = jnp.sum(dispatch_mask, axis=2)

    def exchange(value):
        return lax.all_to_all(value, "expert", split_axis=0, concat_axis=2, tiled=True)[0]

    send_tokens = jnp.einsum(
        "tec,tf->ecf", mask_half, tokens, preferred_element_type=jnp.float32
    ).astype(jnp.bfloat16)
    got_tokens = exchange(send_tokens)

    gate = jnp.sum(router_probs * chosen, axis=1)
    gated_dy = (gate[:, None] * out_grad.astype(jnp.float32)).astype(jnp.bfloat16)
    send_grads = jnp.einsum(
        "tec,tf->ecf", mask_half, gated_dy, preferred_element_type=jnp.float32
    ).astype(jnp.bfloat16)
    partial_dot = jnp.sum(out_grad.astype(jnp.float32) * expert_out.astype(jnp.float32), axis=1)
    dot_rows = token_count // feature_width
    pieces = split_float(partial_dot).reshape(3 * dot_rows, feature_width)
    local_counts = jnp.sum(chosen, axis=0)
    count_row = jnp.pad(local_counts.astype(jnp.bfloat16)[None], ((0, 0), (0, feature_width - experts)))
    side = jnp.concatenate([pieces, count_row], axis=0)
    side_rows = -(-(capacity + side.shape[0]) // 8) * 8 - capacity
    side = jnp.pad(side, ((0, side_rows - side.shape[0]), (0, 0)))
    send_grads = jnp.concatenate(
        [send_grads, jnp.broadcast_to(side[None], (experts, side_rows, feature_width))], axis=1
    )
    got_grads = exchange(send_grads)

    row_tokens = gather_groups(got_tokens)
    all_grads = gather_groups(got_grads).reshape(groups, capacity + side_rows, -1)
    row_grads = all_grads[:, :capacity].reshape(groups * capacity, -1)
    own_side = got_grads[capacity:].astype(jnp.float32)
    gate_dot = jnp.sum(
        own_side[: 3 * dot_rows].reshape(3, dot_rows, experts, feature_width), axis=(0, 2)
    ).reshape(token_count)
    counts = jnp.sum(all_grads[:, capacity + 3 * dot_rows, :experts].astype(jnp.float32), axis=0)

    gate_weight = in_weight[0, 0]
    up_weight = in_weight[0, 1]
    gate_pre = lax.dot_general(
        row_tokens, gate_weight, contract_last, preferred_element_type=jnp.float32
    )
    up_pre = lax.dot_general(
        row_tokens, up_weight, contract_last, preferred_element_type=jnp.float32
    )
    hidden_grad = lax.dot_general(
        row_grads, down_weight[0], contract_last, preferred_element_type=jnp.float32
    )
    gate_act, gate_back = gelu_parts(gate_pre, hidden_grad * up_pre)
    gate_grad = gate_back.astype(jnp.bfloat16)
    up_grad = (hidden_grad * gate_act).astype(jnp.bfloat16)
    term = jnp.dot(gate_grad, gate_weight, preferred_element_type=jnp.float32)
    term = term + jnp.dot(up_grad, up_weight, preferred_element_type=jnp.float32)
    summed = reduce_groups(term)
    going = summed.astype(jnp.bfloat16).reshape(capacity, experts, feature_width)
    returned = lax.all_to_all(
        going.transpose(1, 0, 2), "expert", split_axis=0, concat_axis=0, tiled=True
    )
    weight_grad = weight_grads(gate_grad, up_grad, row_tokens)

    prob_grad = chosen * gate_dot[:, None] + aux_coef * experts * counts[None, :] / (
        token_count * groups
    )
    logit_grad = router_probs * (
        prob_grad - jnp.sum(router_probs * prob_grad, axis=1, keepdims=True)
    )
    logit_grad = logit_grad.astype(jnp.bfloat16)
    router_grad = lax.dot_general(
        tokens, logit_grad, contract_first, preferred_element_type=jnp.float32
    )
    for distance in distances():
        router_grad = router_grad + swap(router_grad, distance)
    router_term = lax.dot_general(
        logit_grad, router_weight, contract_last, preferred_element_type=jnp.float32
    )
    combined = jnp.einsum(
        "tec,ecf->tf", mask_half, returned, preferred_element_type=jnp.float32
    )
    token_grad = (combined + router_term).astype(jnp.bfloat16)
    return (token_grad, weight_grad, router_grad)


def prelude_kernel(
    capacity,
    route_hbm,
    probs_hbm,
    tokens_hbm,
    grads_hbm,
    expert_out_hbm,
    send_ref,
    place_ref,
    route_ref,
    probs_ref,
    tokens_ref,
    grads_ref,
    expert_out_ref,
    sems,
):
    sources = (route_hbm, probs_hbm, tokens_hbm, grads_hbm, expert_out_hbm)
    targets = (route_ref, probs_ref, tokens_ref, grads_ref, expert_out_ref)
    copies = [
        pltpu.make_async_copy(source, target, sems.at[number])
        for number, (source, target) in enumerate(zip(sources, targets))
    ]
    for copy in copies:
        copy.start()
    experts, count = probs_ref.shape
    width = tokens_ref.shape[1]
    half, full = jnp.bfloat16, jnp.float32
    iota = lambda shape, axis: lax.broadcasted_iota(jnp.int32, shape, axis)
    dot = partial(lax.dot_general, preferred_element_type=full)
    plain = (((1,), (0,)), ((), ()))
    square = (count, count)
    earlier = (iota(square, 0) < iota(square, 1)).astype(full).astype(half)
    copies[0].wait()
    route = route_ref[...]
    hit = iota((experts, count), 0) == route
    before = dot(hit.astype(full).astype(half), earlier, plain)
    slot = jnp.sum(jnp.where(hit, before, 0.0), axis=0, keepdims=True)
    place = iota((experts * capacity, count), 0) == route * capacity + slot.astype(jnp.int32)
    mask = place.astype(full).astype(half)
    place_ref[...] = mask
    copies[1].wait()
    gate = jnp.sum(jnp.where(hit, probs_ref[...], 0.0), axis=0, keepdims=True)
    row_gate = jnp.sum(jnp.where(place, gate, 0.0), axis=1, keepdims=True)
    copies[2].wait()
    rows_x = dot(mask, tokens_ref[...], plain)
    copies[3].wait()
    rows_dy = dot(mask, grads_ref[...], plain) * row_gate
    copies[4].wait()
    product = grads_ref[...].astype(full) * expert_out_ref[...].astype(full)
    high = product.astype(half)
    low = (product - high.astype(full)).astype(half)
    ones = jnp.ones((8, width), half)
    part = dot(ones, high, contract_last) + dot(ones, low, contract_last)
    first = part.astype(half).astype(full)
    second = (part - first).astype(half).astype(full)
    third = part - first - second
    listed = (iota((width, count), 0) == route).astype(full).astype(half)
    counts = dot(jnp.ones((8, count), half), listed, contract_last)
    line = iota((8, width), 0)
    side = jnp.where(line == 3, counts, 0.0)
    for number, piece in enumerate((first, second, third)):
        side = jnp.where(line == number, piece, side)
    side = side.astype(half)
    for expert in range(experts):
        rows = slice(expert * capacity, (expert + 1) * capacity)
        send_ref[expert, :capacity] = rows_x[rows].astype(half)
        send_ref[expert, capacity : 2 * capacity] = rows_dy[rows].astype(half)
        send_ref[expert, 2 * capacity :] = side


def far(value):
    return pltpu.with_memory_space_constraint(value, pltpu.HBM)


def near(value):
    return pltpu.with_memory_space_constraint(value, pltpu.VMEM)


def prelude(capacity, *args):
    experts, count = args[1].shape
    width = args[2].shape[1]
    return pl.pallas_call(
        partial(prelude_kernel, capacity),
        in_specs=[pl.BlockSpec(memory_space=pl.ANY)] * len(args),
        out_shape=(
            jax.ShapeDtypeStruct((experts, 2 * capacity + 8, width), jnp.bfloat16),
            jax.ShapeDtypeStruct((experts * capacity, count), jnp.bfloat16),
        ),
        scratch_shapes=[pltpu.VMEM(value.shape, value.dtype) for value in args]
        + [pltpu.SemaphoreType.DMA((len(args),))],
        compiler_params=pltpu.CompilerParams(vmem_limit_bytes=8 << 20),
        name="prelude",
    )(*[far(value) for value in args])


def fetch_kernel(pieces, source_ref, after_ref, target_ref, sems):
    planes, hidden = source_ref.shape[1:3]
    size = hidden // pieces
    copies = []
    for plane in range(planes):
        for piece in range(pieces):
            where = (0, plane, pl.ds(piece * size, size))
            copies.append(
                pltpu.make_async_copy(
                    source_ref.at[where], target_ref.at[where], sems.at[len(copies)]
                )
            )
    for copy in copies:
        copy.start()
    for copy in copies:
        copy.wait()


def fetch(weight, after):
    pieces = 4
    return pl.pallas_call(
        partial(fetch_kernel, pieces),
        in_specs=[pl.BlockSpec(memory_space=pl.ANY)] * 2,
        out_specs=pl.BlockSpec(memory_space=pltpu.VMEM),
        out_shape=pltpu.VMEM(weight.shape, weight.dtype),
        scratch_shapes=[pltpu.SemaphoreType.DMA((weight.shape[1] * pieces,))],
        compiler_params=pltpu.CompilerParams(vmem_limit_bytes=1 << 20),
        cost_estimate=pl.CostEstimate(
            flops=0, bytes_accessed=2 * weight.size, transcendentals=0
        ),
        name="fetch",
    )(far(weight), after)


def hidden_pre_kernel(which, rows_ref, in_ref, down_hbm, out_ref, down_ref, sems):
    size = down_ref.shape[0]
    piece = size // sems.shape[0]
    copies = [
        pltpu.make_async_copy(
            down_hbm.at[0, pl.ds(which * size + number * piece, piece)],
            down_ref.at[pl.ds(number * piece, piece)],
            sems.at[number],
        )
        for number in range(sems.shape[0])
    ]
    for copy in copies:
        copy.start()
    rows = rows_ref[...]
    for start in range(0, 2 * size, size):
        part = slice(start, start + size)
        out_ref[part] = lax.dot_general(
            in_ref[0, which, part], rows, contract_last, preferred_element_type=jnp.float32
        )
    for copy in copies:
        copy.wait()


def hidden_pre(which, rows, in_near, down_weight):
    count, width = rows.shape
    hidden = in_near.shape[2]
    near_spec = pl.BlockSpec(memory_space=pltpu.VMEM)
    return pl.pallas_call(
        partial(hidden_pre_kernel, which),
        in_specs=[near_spec] * 2 + [pl.BlockSpec(memory_space=pl.ANY)],
        out_specs=[near_spec] * 2,
        out_shape=(
            pltpu.VMEM((hidden, count), jnp.float32),
            pltpu.VMEM((hidden // 2, width), down_weight.dtype),
        ),
        scratch_shapes=[pltpu.SemaphoreType.DMA((4,))],
        compiler_params=pltpu.CompilerParams(vmem_limit_bytes=8 << 20),
        cost_estimate=pl.CostEstimate(
            flops=2 * count * hidden * width, bytes_accessed=2 * hidden * width, transcendentals=0
        ),
        name="hidden_pre",
    )(rows, near(in_near), far(down_weight))


def block_of(size, wanted):
    return wanted if size % wanted == 0 else size


def hidden_back_kernel(
    block,
    rows_ref,
    gate_pre_ref,
    up_pre_ref,
    in_ref,
    down_ref,
    other_ref,
    gate_ref,
    up_ref,
    kept_ref,
    away_ref,
):
    size, width = down_ref.shape
    rows = rows_ref[...]
    half = rows.shape[0] // 2
    scale, cubic = math.sqrt(2 / math.pi), 0.044715
    for number, weight_ref in enumerate((down_ref, other_ref)):
        part = slice(number * size, (number + 1) * size)
        grad = lax.dot_general(
            weight_ref[...], rows, contract_last, preferred_element_type=jnp.float32
        )
        value, up = gate_pre_ref[part], up_pre_ref[part]
        square = value * value
        bend = jnp.tanh(scale * (value + cubic * (square * value)))
        cdf = 0.5 * (1.0 + bend)
        slope = cdf + (0.5 * scale) * value * (1.0 - bend * bend) * (1.0 + 3 * cubic * square)
        gate_ref[part] = (grad * up * slope).astype(jnp.bfloat16)
        up_ref[part] = (grad * (value * cdf)).astype(jnp.bfloat16)
    gate_grad, up_grad = gate_ref[...].T, up_ref[...].T
    for start in range(0, width, block):
        part = slice(start, start + block)
        total = jnp.dot(gate_grad, in_ref[0, 0, :, part], preferred_element_type=jnp.float32)
        total += jnp.dot(up_grad, in_ref[0, 1, :, part], preferred_element_type=jnp.float32)
        kept_ref[:, part] = total[:half]
        away_ref[:, part] = total[half:].astype(jnp.bfloat16)


def hidden_back(rows, gate_pre, up_pre, in_near, downs):
    count, width = rows.shape
    hidden = in_near.shape[2]
    near_spec = pl.BlockSpec(memory_space=pltpu.VMEM)
    return pl.pallas_call(
        partial(hidden_back_kernel, block_of(width, 1024)),
        in_specs=[near_spec] * 6,
        out_specs=[near_spec] * 4,
        out_shape=(
            pltpu.VMEM((hidden, count), jnp.bfloat16),
            pltpu.VMEM((hidden, count), jnp.bfloat16),
            pltpu.VMEM((count // 2, width), jnp.float32),
            pltpu.VMEM((count // 2, width), jnp.bfloat16),
        ),
        compiler_params=pltpu.CompilerParams(vmem_limit_bytes=12 << 20),
        cost_estimate=pl.CostEstimate(
            flops=6 * count * hidden * width,
            bytes_accessed=6 * hidden * width,
            transcendentals=count * hidden,
        ),
        name="hidden_back",
    )(rows, near(gate_pre), near(up_pre), near(in_near), *map(near, downs))


def half_kernel(grad_ref, rows_ref, *refs):
    refs[-1][0, 0] = jnp.dot(
        grad_ref[...], rows_ref[...], preferred_element_type=jnp.float32
    ).astype(jnp.bfloat16)


def half_weight_grad(which, grad, rows, partly=None):
    hidden, count = grad.shape
    width = rows.shape[1]
    block = block_of(hidden, 640)
    given = [] if partly is None else [partly]
    return pl.pallas_call(
        half_kernel,
        grid=(hidden // block,),
        in_specs=[
            pl.BlockSpec((block, count), lambda j: (j, 0)),
            pl.BlockSpec((count, width), lambda j: (0, 0)),
        ]
        + [pl.BlockSpec(memory_space=pl.ANY)] * len(given),
        out_specs=pl.BlockSpec((1, 1, block, width), lambda j: (0, which, j, 0)),
        out_shape=jax.ShapeDtypeStruct((1, 2, hidden, width), jnp.bfloat16),
        input_output_aliases={2: 0} if given else {},
        compiler_params=pltpu.CompilerParams(vmem_limit_bytes=20 << 20),
        cost_estimate=pl.CostEstimate(
            flops=2 * count * hidden * width, bytes_accessed=2 * hidden * width, transcendentals=0
        ),
        name="weight_grad_half",
    )(grad, rows, *given)


def aligned_device(
    tokens, out_grad, expert_out, router_probs, expert_index, in_weight, down_weight, router_weight
):
    token_count, width = tokens.shape
    experts = router_probs.shape[1]
    capacity = (5 * token_count + 4 * experts - 1) // (4 * experts)
    groups = lax.axis_size("dp")
    full_width = experts * width
    probs = router_probs.T
    route = expert_index.reshape(1, token_count)
    send, mask = prelude(capacity, route, probs, tokens, out_grad, expert_out)
    got = lax.all_to_all(send, "expert", split_axis=0, concat_axis=0, tiled=True)
    in_near = fetch(in_weight, got)

    def as_rows(value):
        return value.transpose(1, 0, 2).reshape(value.shape[1], full_width)

    row_tokens, all_grads = as_rows(got[:, :capacity]), as_rows(got[:, capacity:])
    first, last = distances()[:-1], distances()[-1:]
    row_tokens = gather_groups(row_tokens, first)
    all_grads = gather_groups(all_grads, first)
    row_tokens = gather_groups(row_tokens, last)
    all_grads = gather_groups(all_grads, last).reshape(groups, capacity + 8, full_width)
    gate_pre, first_down = hidden_pre(0, row_tokens, in_near, down_weight)
    up_pre, second_down = hidden_pre(1, row_tokens, in_near, down_weight)
    row_grads = all_grads[:, :capacity].reshape(groups * capacity, full_width)
    gate_dot = jnp.sum(got[:, 2 * capacity : 2 * capacity + 3].astype(jnp.float32), axis=(0, 1))
    counts = jnp.sum(all_grads[:, capacity + 3, :experts].astype(jnp.float32), axis=0)

    gate_grad, up_grad, kept, away = hidden_back(
        row_grads, gate_pre, up_pre, in_near, (first_down, second_down)
    )
    summed = kept + swap(away, 1).astype(jnp.float32)
    summed = reduce_groups(summed, 2)
    going = summed.astype(jnp.bfloat16).reshape(capacity, experts, width).transpose(1, 0, 2)
    returned = lax.all_to_all(going, "expert", split_axis=0, concat_axis=0, tiled=True)
    weight_grad = half_weight_grad(0, gate_grad, row_tokens)
    weight_grad = half_weight_grad(1, up_grad, row_tokens, weight_grad)

    chosen = (lax.broadcasted_iota(jnp.int32, (experts, token_count), 0) == route).astype(jnp.float32)
    prob_grad = chosen * gate_dot[None, :] + aux_coef * experts * counts[:, None] / (
        token_count * groups
    )
    logit_grad = probs * (prob_grad - jnp.sum(probs * prob_grad, axis=0, keepdims=True))
    logit_grad = logit_grad.astype(jnp.bfloat16)
    router_grad = jnp.dot(logit_grad, tokens, preferred_element_type=jnp.float32)
    for distance in distances():
        router_grad = router_grad + swap(router_grad, distance)
    router_term = lax.dot_general(
        logit_grad, router_weight, (((0,), (1,)), ((), ())), preferred_element_type=jnp.float32
    )
    combined = lax.dot_general(
        mask,
        returned.reshape(experts * capacity, width),
        contract_first,
        preferred_element_type=jnp.float32,
    )
    token_grad = (combined + router_term).astype(jnp.bfloat16)
    return (token_grad, weight_grad, router_grad.T)


def per_device(tokens, out_grad, expert_out, router_probs, *rest):
    token_count, width = tokens.shape
    experts = router_probs.shape[1]
    capacity = (5 * token_count + 4 * experts - 1) // (4 * experts)
    aligned = token_count == width and width % 128 == 0 and capacity % 8 == 0 and experts % 8 == 0
    if not aligned:
        return general_device(tokens, out_grad, expert_out, router_probs, *rest)
    return aligned_device(tokens, out_grad, expert_out, router_probs, *rest)


def solution(mesh):
    in_specs = (
        P("dp", "expert"),
        P("dp", "expert"),
        P("dp", "expert"),
        P("dp", None),
        P("dp", None),
        P("expert", None, "dp", None),
        P("expert", "dp", None),
        P("expert", None),
    )
    out_specs = (P("dp", "expert"), P("expert", None, "dp", None), P("expert", None))
    return jax.shard_map(
        per_device, mesh=mesh, in_specs=in_specs, out_specs=out_specs, check_vma=False
    )
```

profile of v0, /device:TPU:0, one launch (start us, length us, event | category | flops | bytes accessed | tf_op | source)
XLA Modules:
  0.0 61.5 jit_solution(209952251796297923)
XLA Ops:
  0.6 0.0 copy-start
  0.6 1.8 %prelude.1 = (bf16[8,88,256]{2,1,0:T(8,128)(2,1)S(1)}, bf16[320,256]{1,0:T(8,128)(2,1)S(1)}) custom-call(s32[1,256]{1,0:T(1,128)} %bitcast.43, f32[8,256]{1,0:T(8,128)} %bitcast.42, bf16[256,256]{1,0:T(8,128)(2,1)} %tokens_hbm.1, bf16[256,256]{1,0:T(8,128)(2,1)} %grads_hbm.1, bf16[256,256]{1,0:T(8,128)(2,1)} %expert_out_hbm.1), custom_call_target="tpu_custom_call" | custom-call | tf_op jit(solution)/shard_map/prelude/pallas_call | solution.py:277
  2.5 18.6 %all_to_all.10.after_ref = bf16[8,88,256]{2,1,0:T(8,128)(2,1)S(1)} all-to-all(bf16[8,88,256]{2,1,0:T(8,128)(2,1)S(1)} %get-tuple-element.14), channel_id=1, replica_groups=mesh['dp'=4,'expert'=8] {'expert'}, dimensions={0} | all-to-all | bytes 720896 | tf_op jit(solution)/shard_map/all_to_all | solution.py:476
  21.1 1.6 %collective-permute-start.2 = (bf16[40,2048]{1,0:T(8,128)(2,1)S(1)}, bf16[40,2048]{1,0:T(8,128)(2,1)S(1)}, u32[]{:S(2)}, u32[]{:S(2)}) collective-permute-start(bf16[40,2048]{1,0:T(8,128)(2,1)S(1)} %bitcast.37), channel_id=1, source_target_pairs={{0,16},{8,24},{16,0},{24,8},{1,17},{9,25},{17,1},{25,9},{2,18},{10... | collective-permute-start | bytes 491528 | tf_op jit(solution)/shard_map/ppermute | solution.py:38
  22.7 0.6 collective-permute-start
  23.3 4.1 %fetch.1.in_ref = bf16[1,2,1280,2048]{3,2,1,0:T(8,128)(2,1)S(1)} custom-call(bf16[1,2,1280,2048]{3,2,1,0:T(8,128)(2,1)} %source_ref.1, bf16[8,88,256]{2,1,0:T(8,128)(2,1)S(1)} %all_to_all.10.after_ref), custom_call_target="tpu_custom_call" | custom-call | bytes 10485760 | tf_op jit(solution)/shard_map/fetch/pallas_call | solution.py:311
  27.5 0.1 collective-permute-start.3
  27.6 1.4 %collective-permute-done = bf16[48,2048]{1,0:T(8,128)(2,1)S(1)} collective-permute-done((bf16[48,2048]{1,0:T(8,128)(2,1)S(1)}, bf16[48,2048]{1,0:T(8,128)(2,1)S(1)}, u32[]{:S(2)}, u32[]{:S(2)}) %collective-permute-start) | collective-permute-done | bytes 196640 | tf_op jit(solution)/shard_map/ppermute | solution.py:38
  29.0 0.1 collective-permute-start.1
  29.1 0.0 collective-permute-done.3
  29.2 1.7 %hidden_pre.2 = (f32[1280,160]{1,0:T(8,128)S(1)}, bf16[640,2048]{1,0:T(8,128)(2,1)S(1)}) custom-call(bf16[160,2048]{1,0:T(8,128)(2,1)S(1)} %constant_dynamic-update-slice_fusion.rows_ref, bf16[1,2,1280,2048]{3,2,1,0:T(8,128)(2,1)S(1)} %fetch.1.in_ref, bf16[1,1280,2048]{2,1,0:T(8,128)(2,1)} %down_hbm.3), custom_call_target="tpu_custom_call" | custom-call | flops 838860800 | bytes 5242880 | tf_op jit(solution)/shard_map/hidden_pre/pallas_call | solution.py:352
  30.9 2.5 %hidden_pre.3 = (f32[1280,160]{1,0:T(8,128)S(1)}, bf16[640,2048]{1,0:T(8,128)(2,1)S(1)}) custom-call(bf16[160,2048]{1,0:T(8,128)(2,1)S(1)} %constant_dynamic-update-slice_fusion.rows_ref, bf16[1,2,1280,2048]{3,2,1,0:T(8,128)(2,1)S(1)} %fetch.1.in_ref, bf16[1,1280,2048]{2,1,0:T(8,128)(2,1)} %down_hbm.3), custom_call_target="tpu_custom_call" | custom-call | flops 838860800 | bytes 5242880 | tf_op jit(solution)/shard_map/hidden_pre/pallas_call | solution.py:352
  33.5 0.1 pad_maximum_fusion
  33.6 0.1 slice.30
  33.7 0.0 copy-start.2
  33.7 4.1 %hidden_back.1 = (bf16[1280,160]{1,0:T(8,128)(2,1)S(1)}, bf16[1280,160]{1,0:T(8,128)(2,1)S(1)}, f32[80,2048]{1,0:T(8,128)S(1)}, bf16[80,2048]{1,0:T(8,128)(2,1)S(1)}) custom-call(bf16[160,2048]{1,0:T(8,128)(2,1)S(1)} %bitcast.31, f32[1280,160]{1,0:T(8,128)S(1)} %get-tuple-element.15.gate_pre_ref, f32[1280,160]{1,0:T(8,128)S(1)} %get-tuple-element.16.up_pre_ref, ...), custom_call_target="tpu_custom_call" | custom-call | flops 2516582400 | bytes 15728640 | tf_op jit(solution)/shard_map/hidden_back/pallas_call | solution.py:415
  37.8 0.5 collective-permute-start.4
  38.3 0.1 multiply_reduce_fusion
  38.4 0.3 fusion.4
  38.7 0.9 %collective-permute-done.4 = bf16[80,2048]{1,0:T(8,128)(2,1)S(1)} collective-permute-done((bf16[80,2048]{1,0:T(8,128)(2,1)S(1)}, bf16[80,2048]{1,0:T(8,128)(2,1)S(1)}, u32[]{:S(2)}, u32[]{:S(2)}) %collective-permute-start.4) | collective-permute-done | bytes 327712 | tf_op jit(solution)/shard_map/ppermute | solution.py:38
  39.6 0.1 convert_add_fusion
  39.7 1.6 %collective-permute-start.5 = (bf16[40,2048]{1,0:T(8,128)(2,1)S(1)}, bf16[40,2048]{1,0:T(8,128)(2,1)S(1)}, u32[]{:S(2)}, u32[]{:S(2)}) collective-permute-start(bf16[40,2048]{1,0:T(8,128)(2,1)S(1)} %slice.46), channel_id=1, source_target_pairs={{0,16},{8,24},{16,0},{24,8},{1,17},{9,25},{17,1},{25,9},{2,18},{10... | collective-permute-start | bytes 491528 | tf_op jit(solution)/shard_map/ppermute | solution.py:38
  41.2 0.2 fusion.3
  41.4 0.5 collective-permute-start.6
  41.9 3.2 %weight_grad_half.2.refs_0_ = bf16[1,2,1280,2048]{3,2,1,0:T(8,128)(2,1)} custom-call(bf16[1280,160]{1,0:T(8,128)(2,1)S(1)} %get-tuple-element.22.grad_ref, bf16[160,2048]{1,0:T(8,128)(2,1)S(1)} %constant_dynamic-update-slice_fusion.rows_ref), custom_call_target="tpu_custom_call" | custom-call | flops 838860800 | bytes 5242880 | tf_op jit(solution)/shard_map/weight_grad_half/pallas_call | solution.py:446
  45.1 1.2 %collective-permute-done.6 = f32[8,256]{1,0:T(8,128)S(1)} collective-permute-done((f32[8,256]{1,0:T(8,128)S(1)}, f32[8,256]{1,0:T(8,128)S(1)}, u32[]{:S(2)}, u32[]{:S(2)}) %collective-permute-start.6) | collective-permute-done | bytes 8224 | tf_op jit(solution)/shard_map/ppermute | solution.py:38
  46.4 0.7 %copy.20 = bf16[5,8,8,256]{3,2,0,1:T(8,128)(2,1)} copy(bf16[5,8,8,256]{3,2,1,0:T(8,128)(2,1)S(1)} %bitcast.40) | data formatting | bytes 327680 | tf_op jit(solution)/shard_map/reshape | solution.py:499
  47.1 5.3 %all-to-all-start.1 = ((bf16[8,40,256]{2,1,0:T(8,128)(2,1)}), bf16[8,40,256]{2,1,0:T(8,128)(2,1)S(1)}, u32[]{:S(2)}, u32[]{:S(2)}) async-start(bf16[8,40,256]{2,1,0:T(8,128)(2,1)} %bitcast.30), calls=%async_computation.1 | async-start | bytes 327680 | tf_op jit(solution)/shard_map/all_to_all | solution.py:500
  52.4 3.2 %weight_grad_half.3 = bf16[1,2,1280,2048]{3,2,1,0:T(8,128)(2,1)} custom-call(bf16[1280,160]{1,0:T(8,128)(2,1)S(1)} %get-tuple-element.21.grad_ref, bf16[160,2048]{1,0:T(8,128)(2,1)S(1)} %constant_dynamic-update-slice_fusion.rows_ref, bf16[1,2,1280,2048]{3,2,1,0:T(8,128)(2,1)} %weight_grad_half.2.refs_0_), custom_call_target="tpu_custom_call", output_to_operand_aliasing={{}: (2, {})} | custom-call | flops 838860800 | bytes 5242880 | tf_op jit(solution)/shard_map/weight_grad_half/pallas_call | solution.py:446
  55.6 0.6 add_bitcast_fusion
  56.2 4.3 %all-to-all-done.1 = bf16[8,40,256]{2,1,0:T(8,128)(2,1)S(1)} async-done(((bf16[8,40,256]{2,1,0:T(8,128)(2,1)}), bf16[8,40,256]{2,1,0:T(8,128)(2,1)S(1)}, u32[]{:S(2)}, u32[]{:S(2)}) %all-to-all-start.1) | async-done | bytes 163872 | tf_op jit(solution)/shard_map/all_to_all | solution.py:500
  60.6 0.9 %fusion = bf16[256,256]{1,0:T(8,128)(2,1)} fusion(f32[256,256]{1,0:T(8,128)S(1)} %fusion.4, bf16[320,256]{1,0:T(8,128)(2,1)S(1)} %get-tuple-element.13, bf16[320,256]{1,0:T(8,128)(2,1)S(1)} %bitcast.41), kind=kOutput, calls=%fused_computation.1 | convolution fusion | flops 42074112 | bytes 720896 | tf_op jit(solution)/shard_map/dot_general | solution.py:516
  (26 shorter events, 0.3 us)
Async XLA Ops:
  0.6 37.8 %copy-start = (bf16[256,8]{0,1:T(8,128)(2,1)S(1)}, bf16[256,8]{0,1:T(8,128)(2,1)}, u32[]{:S(2)}) copy-start(bf16[256,8]{0,1:T(8,128)(2,1)} %param.15) | copy-start | bytes 12292
  21.1 6.3 %collective-permute-start.2 = (bf16[40,2048]{1,0:T(8,128)(2,1)S(1)}, bf16[40,2048]{1,0:T(8,128)(2,1)S(1)}, u32[]{:S(2)}, u32[]{:S(2)}) collective-permute-start(bf16[40,2048]{1,0:T(8,128)(2,1)S(1)} %bitcast.37), channel_id=1, source_target_pairs={{0,16},{8,24},{16,0},{24,8},{1,17},{9,25},{17,1},{25,9},{2,18},{10... | collective-permute-start | bytes 491528 | tf_op jit(solution)/shard_map/ppermute | solution.py:38
  22.7 6.3 %collective-permute-start = (bf16[48,2048]{1,0:T(8,128)(2,1)S(1)}, bf16[48,2048]{1,0:T(8,128)(2,1)S(1)}, u32[]{:S(2)}, u32[]{:S(2)}) collective-permute-start(bf16[48,2048]{1,0:T(8,128)(2,1)S(1)} %bitcast.34), channel_id=1, source_target_pairs={{0,16},{8,24},{16,0},{24,8},{1,17},{9,25},{17,1},{25,9},{2,18},{10... | collective-permute-start | bytes 589832 | tf_op jit(solution)/shard_map/ppermute | solution.py:38
  27.5 1.7 %collective-permute-start.3 = (bf16[80,2048]{1,0:T(8,128)(2,1)S(1)}, bf16[80,2048]{1,0:T(8,128)(2,1)S(1)}, u32[]{:S(2)}, u32[]{:S(2)}) collective-permute-start(bf16[80,2048]{1,0:T(8,128)(2,1)S(1)} %pad_maximum_fusion.2), channel_id=1, source_target_pairs={{0,8},{8,0},{16,24},{24,16},{1,9},{9,1},{17,25},{25,17},{2,10},{10... | collective-permute-start | bytes 983048 | tf_op jit(solution)/shard_map/ppermute | solution.py:38
  29.0 4.4 %collective-permute-start.1 = (bf16[96,2048]{1,0:T(8,128)(2,1)S(1)}, bf16[96,2048]{1,0:T(8,128)(2,1)S(1)}, u32[]{:S(2)}, u32[]{:S(2)}) collective-permute-start(bf16[96,2048]{1,0:T(8,128)(2,1)S(1)} %pad_maximum_fusion.1), channel_id=1, source_target_pairs={{0,8},{8,0},{16,24},{24,16},{1,9},{9,1},{17,25},{25,17},{2,10},{10... | collective-permute-start | bytes 1179656 | tf_op jit(solution)/shard_map/ppermute | solution.py:38
  33.7 4.7 %copy-start.2 = (f32[256,8]{0,1:T(8,128)S(1)}, f32[256,8]{0,1:T(8,128)}, u32[]{:S(2)}) copy-start(f32[256,8]{0,1:T(8,128)} %param.11) | copy-start | bytes 24580
  33.7 4.6 %copy-start.3 = (s32[256,1]{0,1:T(1,128)S(1)}, s32[256,1]{0,1:T(1,128)}, u32[]{:S(2)}) copy-start(s32[256,1]{0,1:T(1,128)} %param.12) | copy-start | bytes 3076
  33.7 7.5 %copy-start.1 = (bf16[256,256]{1,0:T(8,128)(2,1)S(1)}, bf16[256,256]{1,0:T(8,128)(2,1)}, u32[]{:S(2)}) copy-start(bf16[256,256]{1,0:T(8,128)(2,1)} %tokens_hbm.1) | copy-start | bytes 393220
  37.8 1.8 %collective-permute-start.4 = (bf16[80,2048]{1,0:T(8,128)(2,1)S(1)}, bf16[80,2048]{1,0:T(8,128)(2,1)S(1)}, u32[]{:S(2)}, u32[]{:S(2)}) collective-permute-start(bf16[80,2048]{1,0:T(8,128)(2,1)S(1)} %get-tuple-element.20), channel_id=1, source_target_pairs={{0,8},{8,0},{16,24},{24,16},{1,9},{9,1},{17,25},{25,17},{2,10},{10... | collective-permute-start | bytes 983048 | tf_op jit(solution)/shard_map/ppermute | solution.py:38
  39.7 6.7 %collective-permute-start.5 = (bf16[40,2048]{1,0:T(8,128)(2,1)S(1)}, bf16[40,2048]{1,0:T(8,128)(2,1)S(1)}, u32[]{:S(2)}, u32[]{:S(2)}) collective-permute-start(bf16[40,2048]{1,0:T(8,128)(2,1)S(1)} %slice.46), channel_id=1, source_target_pairs={{0,16},{8,24},{16,0},{24,8},{1,17},{9,25},{17,1},{25,9},{2,18},{10... | collective-permute-start | bytes 491528 | tf_op jit(solution)/shard_map/ppermute | solution.py:38
  41.4 5.0 %collective-permute-start.6 = (f32[8,256]{1,0:T(8,128)S(1)}, f32[8,256]{1,0:T(8,128)S(1)}, u32[]{:S(2)}, u32[]{:S(2)}) collective-permute-start(f32[8,256]{1,0:T(8,128)S(1)} %fusion.3), channel_id=1, source_target_pairs={{0,16},{8,24},{16,0},{24,8},{1,17},{9,25},{17,1},{25,9},{2,18},{10... | collective-permute-start | bytes 24584 | tf_op jit(solution)/shard_map/ppermute | solution.py:38
  46.4 9.3 %collective-permute-start.7 = (f32[8,256]{1,0:T(8,128)S(1)}, f32[8,256]{1,0:T(8,128)S(1)}, u32[]{:S(2)}, u32[]{:S(2)}) collective-permute-start(f32[8,256]{1,0:T(8,128)S(1)} %add.28), channel_id=1, source_target_pairs={{0,8},{8,0},{16,24},{24,16},{1,9},{9,1},{17,25},{25,17},{2,10},{10... | collective-permute-start | bytes 24584 | tf_op jit(solution)/shard_map/ppermute | solution.py:38
  47.1 13.5 %all-to-all-start.1 = ((bf16[8,40,256]{2,1,0:T(8,128)(2,1)}), bf16[8,40,256]{2,1,0:T(8,128)(2,1)S(1)}, u32[]{:S(2)}, u32[]{:S(2)}) async-start(bf16[8,40,256]{2,1,0:T(8,128)(2,1)} %bitcast.30), calls=%async_computation.1 | async-start | bytes 327680 | tf_op jit(solution)/shard_map/all_to_all | solution.py:500
where the time goes:
time: 61.8 us; the launch traced here: 61.5 us
  Pallas kernels  20.6 us (33%)
  blocking collectives  18.6 us (30%)
  starting transfers between devices  10.3 us (17%)
  waiting for transfers between devices  7.93 us (13%)
  matrix products  1.39 us (2%)
  other arithmetic  0.96 us (2%)
  local copies, waits for them, and re-layouts  0.87 us (1%)
  between operations  0.86 us (1%)
    all_to_all x1, blocking collectives, aligned_device(): lax.all_to_all(send, 'expert', split_axis=0, concat_axis=0, tiled=True)  18.6 us
    pallas_call x2, Pallas kernels, half_weight_grad(): pl.pallas_call(half_kernel, grid=(hidden // block,), in_specs=[pl.BlockSp...  6.39 us
    all_to_all x1, starting transfers between devices, aligned_device(): lax.all_to_all(going, 'expert', split_axis=0, concat_axis=0, tiled=True)  5.33 us
    ppermute x8, starting transfers between devices, swap(): return lax.ppermute(value, 'dp', [(i, i ^ distance) for i in range(size)])  4.93 us
    all_to_all x1, waiting for transfers between devices, aligned_device(): lax.all_to_all(going, 'expert', split_axis=0, concat_axis=0, tiled=True)  4.32 us
    pallas_call x2, Pallas kernels, hidden_pre(): pl.pallas_call(partial(hidden_pre_kernel, which), in_specs=[near_spec] *...  4.25 us
    pallas_call x1, Pallas kernels, fetch(): pl.pallas_call(partial(fetch_kernel, pieces), in_specs=[pl.BlockSpec(memo...  4.08 us
    pallas_call x1, Pallas kernels, hidden_back(): pl.pallas_call(partial(hidden_back_kernel, block_of(width, 1024)), in_spe...  4.08 us
  transfers between devices with their start and end apart: 9, of which 4 were waited for; matrix products, arithmetic and copies ran while one was open for 3% of the time, Pallas kernels for 24%

commit v1 on v0

--- a/solution.py
+++ b/solution.py
@@ -322,47 +322,60 @@
     )(far(weight), after)
 
 
-def hidden_pre_kernel(which, rows_ref, in_ref, down_hbm, out_ref, down_ref, sems):
-    size = down_ref.shape[0]
-    piece = size // sems.shape[0]
-    copies = [
-        pltpu.make_async_copy(
-            down_hbm.at[0, pl.ds(which * size + number * piece, piece)],
-            down_ref.at[pl.ds(number * piece, piece)],
-            sems.at[number],
-        )
-        for number in range(sems.shape[0])
-    ]
-    for copy in copies:
-        copy.start()
+def pre_activation(which, rows_ref, in_ref, out_ref):
     rows = rows_ref[...]
-    for start in range(0, 2 * size, size):
+    size = in_ref.shape[2] // 2
+    for start in (0, size):
         part = slice(start, start + size)
         out_ref[part] = lax.dot_general(
             in_ref[0, which, part], rows, contract_last, preferred_element_type=jnp.float32
         )
+
+
+def gate_pre_kernel(rows_ref, in_ref, down_hbm, out_ref, down_ref, sems):
+    pieces = sems.shape[0]
+    size = down_ref.shape[1] // pieces
+    copies = []
+    for piece in range(pieces):
+        where = (0, pl.ds(piece * size, size))
+        copies.append(
+            pltpu.make_async_copy(down_hbm.at[where], down_ref.at[where], sems.at[piece])
+        )
+    for copy in copies:
+        copy.start()
+    pre_activation(0, rows_ref, in_ref, out_ref)
     for copy in copies:
         copy.wait()
 
 
-def hidden_pre(which, rows, in_near, down_weight):
+def hidden_pre(which, rows, in_near, down_weight=None):
     count, width = rows.shape
     hidden = in_near.shape[2]
     near_spec = pl.BlockSpec(memory_space=pltpu.VMEM)
-    return pl.pallas_call(
-        partial(hidden_pre_kernel, which),
-        in_specs=[near_spec] * 2 + [pl.BlockSpec(memory_space=pl.ANY)],
-        out_specs=[near_spec] * 2,
-        out_shape=(
-            pltpu.VMEM((hidden, count), jnp.float32),
-            pltpu.VMEM((hidden // 2, width), down_weight.dtype),
-        ),
-        scratch_shapes=[pltpu.SemaphoreType.DMA((4,))],
+    out = pltpu.VMEM((hidden, count), jnp.float32)
+    settings = dict(
         compiler_params=pltpu.CompilerParams(vmem_limit_bytes=8 << 20),
         cost_estimate=pl.CostEstimate(
             flops=2 * count * hidden * width, bytes_accessed=2 * hidden * width, transcendentals=0
         ),
-        name="hidden_pre",
+    )
+    if down_weight is None:
+        return pl.pallas_call(
+            partial(pre_activation, which),
+            in_specs=[near_spec] * 2,
+            out_specs=near_spec,
+            out_shape=out,
+            name="hidden_pre",
+            **settings,
+        )(rows, near(in_near))
+    return pl.pallas_call(
+        gate_pre_kernel,
+        in_specs=[near_spec] * 2 + [pl.BlockSpec(memory_space=pl.ANY)],
+        out_specs=[near_spec] * 2,
+        out_shape=(out, pltpu.VMEM(down_weight.shape, down_weight.dtype)),
+        scratch_shapes=[pltpu.SemaphoreType.DMA((4,))],
+        name="gate_pre",
+        **settings,
     )(rows, near(in_near), far(down_weight))
 
 
@@ -377,20 +390,19 @@
     up_pre_ref,
     in_ref,
     down_ref,
-    other_ref,
     gate_ref,
     up_ref,
     kept_ref,
     away_ref,
 ):
-    size, width = down_ref.shape
+    size, width = down_ref.shape[1] // 2, down_ref.shape[2]
     rows = rows_ref[...]
     half = rows.shape[0] // 2
     scale, cubic = math.sqrt(2 / math.pi), 0.044715
-    for number, weight_ref in enumerate((down_ref, other_ref)):
-        part = slice(number * size, (number + 1) * size)
+    for start in (0, size):
+        part = slice(start, start + size)
         grad = lax.dot_general(
-            weight_ref[...], rows, contract_last, preferred_element_type=jnp.float32
+            down_ref[0, part], rows, contract_last, preferred_element_type=jnp.float32
         )
         value, up = gate_pre_ref[part], up_pre_ref[part]
         square = value * value
@@ -408,13 +420,13 @@
         away_ref[:, part] = total[half:].astype(jnp.bfloat16)
 
 
-def hidden_back(rows, gate_pre, up_pre, in_near, downs):
+def hidden_back(rows, gate_pre, up_pre, in_near, down_near):
     count, width = rows.shape
     hidden = in_near.shape[2]
     near_spec = pl.BlockSpec(memory_space=pltpu.VMEM)
     return pl.pallas_call(
         partial(hidden_back_kernel, block_of(width, 1024)),
-        in_specs=[near_spec] * 6,
+        in_specs=[near_spec] * 5,
         out_specs=[near_spec] * 4,
         out_shape=(
             pltpu.VMEM((hidden, count), jnp.bfloat16),
@@ -429,7 +441,7 @@
             transcendentals=count * hidden,
         ),
         name="hidden_back",
-    )(rows, near(gate_pre), near(up_pre), near(in_near), *map(near, downs))
+    )(rows, near(gate_pre), near(up_pre), near(in_near), near(down_near))
 
 
 def half_kernel(grad_ref, rows_ref, *refs):
@@ -485,14 +497,14 @@
     all_grads = gather_groups(all_grads, first)
     row_tokens = gather_groups(row_tokens, last)
     all_grads = gather_groups(all_grads, last).reshape(groups, capacity + 8, full_width)
-    gate_pre, first_down = hidden_pre(0, row_tokens, in_near, down_weight)
-    up_pre, second_down = hidden_pre(1, row_tokens, in_near, down_weight)
+    gate_pre, down_near = hidden_pre(0, row_tokens, in_near, down_weight)
+    up_pre = hidden_pre(1, row_tokens, in_near)
     row_grads = all_grads[:, :capacity].reshape(groups * capacity, full_width)
     gate_dot = jnp.sum(got[:, 2 * capacity : 2 * capacity + 3].astype(jnp.float32), axis=(0, 1))
     counts = jnp.sum(all_grads[:, capacity + 3, :experts].astype(jnp.float32), axis=0)
 
     gate_grad, up_grad, kept, away = hidden_back(
-        row_grads, gate_pre, up_pre, in_near, (first_down, second_down)
+        row_grads, gate_pre, up_pre, in_near, down_near
     )
     summed = kept + swap(away, 1).astype(jnp.float32)
     summed = reduce_groups(summed, 2)
@@ -508,7 +520,7 @@
     logit_grad = probs * (prob_grad - jnp.sum(probs * prob_grad, axis=0, keepdims=True))
     logit_grad = logit_grad.astype(jnp.bfloat16)
     router_grad = jnp.dot(logit_grad, tokens, preferred_element_type=jnp.float32)
-    for distance in distances():
+    for distance in distances()[::-1]:
         router_grad = router_grad + swap(router_grad, distance)
     router_term = lax.dot_general(
         logit_grad, router_weight, (((0,), (1,)), ((), ())), preferred_element_type=jnp.float32

time: 61.8 us -> 60.8 us (0.984)
  waiting for transfers between devices: 7.93 us -> 7.08 us
where the time goes in v1:
time: 60.8 us; the launch traced here: 60.5 us
  Pallas kernels  20.5 us (34%)
  blocking collectives  18.6 us (31%)
  starting transfers between devices  10.4 us (17%)
  waiting for transfers between devices  7.08 us (12%)
  matrix products  1.39 us (2%)
  other arithmetic  0.95 us (2%)
  local copies, waits for them, and re-layouts  0.87 us (1%)
  between operations  0.84 us (1%)
    all_to_all x1, blocking collectives, aligned_device(): lax.all_to_all(send, 'expert', split_axis=0, concat_axis=0, tiled=True)  18.6 us
    pallas_call x2, Pallas kernels, half_weight_grad(): pl.pallas_call(half_kernel, grid=(hidden // block,), in_specs=[pl.BlockSp...  6.4 us
    all_to_all x1, starting transfers between devices, aligned_device(): lax.all_to_all(going, 'expert', split_axis=0, concat_axis=0, tiled=True)  5.32 us
    ppermute x8, starting transfers between devices, swap(): return lax.ppermute(value, 'dp', [(i, i ^ distance) for i in range(size)])  5.03 us
    pallas_call x1, Pallas kernels, fetch(): pl.pallas_call(partial(fetch_kernel, pieces), in_specs=[pl.BlockSpec(memo...  4.08 us
    pallas_call x1, Pallas kernels, hidden_back(): pl.pallas_call(partial(hidden_back_kernel, block_of(width, 1024)), in_spe...  4.08 us
    all_to_all x1, waiting for transfers between devices, aligned_device(): lax.all_to_all(going, 'expert', split_axis=0, concat_axis=0, tiled=True)  3.75 us
    ppermute x8, waiting for transfers between devices, swap(): return lax.ppermute(value, 'dp', [(i, i ^ distance) for i in range(size)])  3.32 us
  transfers between devices with their start and end apart: 9, of which 4 were waited for; matrix products, arithmetic and copies ran while one was open for 3% of the time, Pallas kernels for 24%

profile of v1, /device:TPU:0, one launch (start us, length us, event | category | flops | bytes accessed | tf_op | source)
XLA Modules:
  0.0 60.5 jit_solution(12340774995410233724)
XLA Ops:
  0.6 0.0 copy-start
  0.6 1.8 %prelude.1 = (bf16[8,88,256]{2,1,0:T(8,128)(2,1)S(1)}, bf16[320,256]{1,0:T(8,128)(2,1)S(1)}) custom-call(s32[1,256]{1,0:T(1,128)} %bitcast.43, f32[8,256]{1,0:T(8,128)} %bitcast.42, bf16[256,256]{1,0:T(8,128)(2,1)} %tokens_hbm.1, bf16[256,256]{1,0:T(8,128)(2,1)} %grads_hbm.1, bf16[256,256]{1,0:T(8,128)(2,1)} %expert_out_hbm.1), custom_call_target="tpu_custom_call" | custom-call | tf_op jit(solution)/shard_map/prelude/pallas_call | solution.py:277
  2.5 18.6 %all_to_all.10.after_ref = bf16[8,88,256]{2,1,0:T(8,128)(2,1)S(1)} all-to-all(bf16[8,88,256]{2,1,0:T(8,128)(2,1)S(1)} %get-tuple-element.12), channel_id=1, replica_groups=mesh['dp'=4,'expert'=8] {'expert'}, dimensions={0} | all-to-all | bytes 720896 | tf_op jit(solution)/shard_map/all_to_all | solution.py:488
  21.1 1.6 %collective-permute-start.2 = (bf16[40,2048]{1,0:T(8,128)(2,1)S(1)}, bf16[40,2048]{1,0:T(8,128)(2,1)S(1)}, u32[]{:S(2)}, u32[]{:S(2)}) collective-permute-start(bf16[40,2048]{1,0:T(8,128)(2,1)S(1)} %bitcast.37), channel_id=1, source_target_pairs={{0,16},{8,24},{16,0},{24,8},{1,17},{9,25},{17,1},{25,9},{2,18},{10... | collective-permute-start | bytes 491528 | tf_op jit(solution)/shard_map/ppermute | solution.py:38
  22.7 0.6 collective-permute-start
  23.3 4.1 %fetch.1.in_ref = bf16[1,2,1280,2048]{3,2,1,0:T(8,128)(2,1)S(1)} custom-call(bf16[1,2,1280,2048]{3,2,1,0:T(8,128)(2,1)} %source_ref.1, bf16[8,88,256]{2,1,0:T(8,128)(2,1)S(1)} %all_to_all.10.after_ref), custom_call_target="tpu_custom_call" | custom-call | bytes 10485760 | tf_op jit(solution)/shard_map/fetch/pallas_call | solution.py:311
  27.5 0.1 collective-permute-start.3
  27.6 1.4 %collective-permute-done = bf16[48,2048]{1,0:T(8,128)(2,1)S(1)} collective-permute-done((bf16[48,2048]{1,0:T(8,128)(2,1)S(1)}, bf16[48,2048]{1,0:T(8,128)(2,1)S(1)}, u32[]{:S(2)}, u32[]{:S(2)}) %collective-permute-start) | collective-permute-done | bytes 196640 | tf_op jit(solution)/shard_map/ppermute | solution.py:38
  29.0 0.1 collective-permute-start.1
  29.1 0.0 collective-permute-done.3
  29.2 1.5 %hidden_pre.1.up_pre_ref = f32[1280,160]{1,0:T(8,128)S(1)} custom-call(bf16[160,2048]{1,0:T(8,128)(2,1)S(1)} %constant_dynamic-update-slice_fusion.rows_ref, bf16[1,2,1280,2048]{3,2,1,0:T(8,128)(2,1)S(1)} %fetch.1.in_ref), custom_call_target="tpu_custom_call" | custom-call | flops 838860800 | bytes 5242880 | tf_op jit(solution)/shard_map/hidden_pre/pallas_call | solution.py:363
  30.7 2.5 %gate_pre.1 = (f32[1280,160]{1,0:T(8,128)S(1)}, bf16[1,1280,2048]{2,1,0:T(8,128)(2,1)S(1)}) custom-call(bf16[160,2048]{1,0:T(8,128)(2,1)S(1)} %constant_dynamic-update-slice_fusion.rows_ref, bf16[1,2,1280,2048]{3,2,1,0:T(8,128)(2,1)S(1)} %fetch.1.in_ref, bf16[1,1280,2048]{2,1,0:T(8,128)(2,1)} %down_hbm.1), custom_call_target="tpu_custom_call" | custom-call | flops 838860800 | bytes 5242880 | tf_op jit(solution)/shard_map/gate_pre/pallas_call | solution.py:371
  33.3 0.1 pad_maximum_fusion
  33.4 0.1 slice.30
  33.5 4.1 %hidden_back.1 = (bf16[1280,160]{1,0:T(8,128)(2,1)S(1)}, bf16[1280,160]{1,0:T(8,128)(2,1)S(1)}, f32[80,2048]{1,0:T(8,128)S(1)}, bf16[80,2048]{1,0:T(8,128)(2,1)S(1)}) custom-call(bf16[160,2048]{1,0:T(8,128)(2,1)S(1)} %bitcast.31, f32[1280,160]{1,0:T(8,128)S(1)} %get-tuple-element.13.gate_pre_ref, f32[1280,160]{1,0:T(8,128)S(1)} %hidden_pre.1.up_pre_ref, ...), custom_call_target="tpu_custom_call" | custom-call | flops 2516582400 | bytes 15728640 | tf_op jit(solution)/shard_map/hidden_back/pallas_call | solution.py:427
  37.6 0.5 collective-permute-start.4
  38.1 0.1 multiply_reduce_fusion
  38.2 0.3 fusion.4
  38.5 0.9 %collective-permute-done.4 = bf16[80,2048]{1,0:T(8,128)(2,1)S(1)} collective-permute-done((bf16[80,2048]{1,0:T(8,128)(2,1)S(1)}, bf16[80,2048]{1,0:T(8,128)(2,1)S(1)}, u32[]{:S(2)}, u32[]{:S(2)}) %collective-permute-start.4) | collective-permute-done | bytes 327712 | tf_op jit(solution)/shard_map/ppermute | solution.py:38
  39.4 0.1 convert_add_fusion
  39.5 1.5 %collective-permute-start.5 = (bf16[40,2048]{1,0:T(8,128)(2,1)S(1)}, bf16[40,2048]{1,0:T(8,128)(2,1)S(1)}, u32[]{:S(2)}, u32[]{:S(2)}) collective-permute-start(bf16[40,2048]{1,0:T(8,128)(2,1)S(1)} %slice.46), channel_id=1, source_target_pairs={{0,16},{8,24},{16,0},{24,8},{1,17},{9,25},{17,1},{25,9},{2,18},{10... | collective-permute-start | bytes 491528 | tf_op jit(solution)/shard_map/ppermute | solution.py:38
  41.0 0.2 fusion.3
  41.2 0.1 collective-permute-start.6
  41.3 3.2 %weight_grad_half.2.refs_0_ = bf16[1,2,1280,2048]{3,2,1,0:T(8,128)(2,1)} custom-call(bf16[1280,160]{1,0:T(8,128)(2,1)S(1)} %get-tuple-element.18.grad_ref, bf16[160,2048]{1,0:T(8,128)(2,1)S(1)} %constant_dynamic-update-slice_fusion.rows_ref), custom_call_target="tpu_custom_call" | custom-call | flops 838860800 | bytes 5242880 | tf_op jit(solution)/shard_map/weight_grad_half/pallas_call | solution.py:458
  44.5 0.5 collective-permute-start.7
  45.0 1.0 %collective-permute-done.5 = bf16[40,2048]{1,0:T(8,128)(2,1)S(1)} collective-permute-done((bf16[40,2048]{1,0:T(8,128)(2,1)S(1)}, bf16[40,2048]{1,0:T(8,128)(2,1)S(1)}, u32[]{:S(2)}, u32[]{:S(2)}) %collective-permute-start.5) | collective-permute-done | bytes 163872 | tf_op jit(solution)/shard_map/ppermute | solution.py:38
  46.0 0.7 %copy.20 = bf16[5,8,8,256]{3,2,0,1:T(8,128)(2,1)} copy(bf16[5,8,8,256]{3,2,1,0:T(8,128)(2,1)S(1)} %bitcast.40) | data formatting | bytes 327680 | tf_op jit(solution)/shard_map/reshape | solution.py:511
  46.7 5.3 %all-to-all-start.1 = ((bf16[8,40,256]{2,1,0:T(8,128)(2,1)}), bf16[8,40,256]{2,1,0:T(8,128)(2,1)S(1)}, u32[]{:S(2)}, u32[]{:S(2)}) async-start(bf16[8,40,256]{2,1,0:T(8,128)(2,1)} %bitcast.30), calls=%async_computation.1 | async-start | bytes 327680 | tf_op jit(solution)/shard_map/all_to_all | solution.py:512
  52.0 3.2 %weight_grad_half.3 = bf16[1,2,1280,2048]{3,2,1,0:T(8,128)(2,1)} custom-call(bf16[1280,160]{1,0:T(8,128)(2,1)S(1)} %get-tuple-element.17.grad_ref, bf16[160,2048]{1,0:T(8,128)(2,1)S(1)} %constant_dynamic-update-slice_fusion.rows_ref, bf16[1,2,1280,2048]{3,2,1,0:T(8,128)(2,1)} %weight_grad_half.2.refs_0_), custom_call_target="tpu_custom_call", output_to_operand_aliasing={{}: (2, {})} | custom-call | flops 838860800 | bytes 5242880 | tf_op jit(solution)/shard_map/weight_grad_half/pallas_call | solution.py:458
  55.2 0.6 add_bitcast_fusion
  55.8 3.8 %all-to-all-done.1 = bf16[8,40,256]{2,1,0:T(8,128)(2,1)S(1)} async-done(((bf16[8,40,256]{2,1,0:T(8,128)(2,1)}), bf16[8,40,256]{2,1,0:T(8,128)(2,1)S(1)}, u32[]{:S(2)}, u32[]{:S(2)}) %all-to-all-start.1) | async-done | bytes 163872 | tf_op jit(solution)/shard_map/all_to_all | solution.py:512
  59.6 0.9 %fusion = bf16[256,256]{1,0:T(8,128)(2,1)} fusion(f32[256,256]{1,0:T(8,128)S(1)} %fusion.4, bf16[320,256]{1,0:T(8,128)(2,1)S(1)} %get-tuple-element.11, bf16[320,256]{1,0:T(8,128)(2,1)S(1)} %bitcast.41), kind=kOutput, calls=%fused_computation.1 | convolution fusion | flops 42074112 | bytes 720896 | tf_op jit(solution)/shard_map/dot_general | solution.py:528
  (26 shorter events, 0.3 us)
Async XLA Ops:
  0.6 37.6 %copy-start = (bf16[256,8]{0,1:T(8,128)(2,1)S(1)}, bf16[256,8]{0,1:T(8,128)(2,1)}, u32[]{:S(2)}) copy-start(bf16[256,8]{0,1:T(8,128)(2,1)} %param.15) | copy-start | bytes 12292
  21.1 6.3 %collective-permute-start.2 = (bf16[40,2048]{1,0:T(8,128)(2,1)S(1)}, bf16[40,2048]{1,0:T(8,128)(2,1)S(1)}, u32[]{:S(2)}, u32[]{:S(2)}) collective-permute-start(bf16[40,2048]{1,0:T(8,128)(2,1)S(1)} %bitcast.37), channel_id=1, source_target_pairs={{0,16},{8,24},{16,0},{24,8},{1,17},{9,25},{17,1},{25,9},{2,18},{10... | collective-permute-start | bytes 491528 | tf_op jit(solution)/shard_map/ppermute | solution.py:38
  22.7 6.3 %collective-permute-start = (bf16[48,2048]{1,0:T(8,128)(2,1)S(1)}, bf16[48,2048]{1,0:T(8,128)(2,1)S(1)}, u32[]{:S(2)}, u32[]{:S(2)}) collective-permute-start(bf16[48,2048]{1,0:T(8,128)(2,1)S(1)} %bitcast.34), channel_id=1, source_target_pairs={{0,16},{8,24},{16,0},{24,8},{1,17},{9,25},{17,1},{25,9},{2,18},{10... | collective-permute-start | bytes 589832 | tf_op jit(solution)/shard_map/ppermute | solution.py:38
  27.5 1.7 %collective-permute-start.3 = (bf16[80,2048]{1,0:T(8,128)(2,1)S(1)}, bf16[80,2048]{1,0:T(8,128)(2,1)S(1)}, u32[]{:S(2)}, u32[]{:S(2)}) collective-permute-start(bf16[80,2048]{1,0:T(8,128)(2,1)S(1)} %pad_maximum_fusion.2), channel_id=1, source_target_pairs={{0,8},{8,0},{16,24},{24,16},{1,9},{9,1},{17,25},{25,17},{2,10},{10... | collective-permute-start | bytes 983048 | tf_op jit(solution)/shard_map/ppermute | solution.py:38
  29.0 4.2 %collective-permute-start.1 = (bf16[96,2048]{1,0:T(8,128)(2,1)S(1)}, bf16[96,2048]{1,0:T(8,128)(2,1)S(1)}, u32[]{:S(2)}, u32[]{:S(2)}) collective-permute-start(bf16[96,2048]{1,0:T(8,128)(2,1)S(1)} %pad_maximum_fusion.1), channel_id=1, source_target_pairs={{0,8},{8,0},{16,24},{24,16},{1,9},{9,1},{17,25},{25,17},{2,10},{10... | collective-permute-start | bytes 1179656 | tf_op jit(solution)/shard_map/ppermute | solution.py:38
  33.5 4.7 %copy-start.2 = (f32[256,8]{0,1:T(8,128)S(1)}, f32[256,8]{0,1:T(8,128)}, u32[]{:S(2)}) copy-start(f32[256,8]{0,1:T(8,128)} %param.11) | copy-start | bytes 24580
  33.5 4.6 %copy-start.3 = (s32[256,1]{0,1:T(1,128)S(1)}, s32[256,1]{0,1:T(1,128)}, u32[]{:S(2)}) copy-start(s32[256,1]{0,1:T(1,128)} %param.12) | copy-start | bytes 3076
  37.6 3.4 %copy-start.1 = (bf16[256,256]{1,0:T(8,128)(2,1)S(1)}, bf16[256,256]{1,0:T(8,128)(2,1)}, u32[]{:S(2)}) copy-start(bf16[256,256]{1,0:T(8,128)(2,1)} %tokens_hbm.1) | copy-start | bytes 393220
  37.6 1.8 %collective-permute-start.4 = (bf16[80,2048]{1,0:T(8,128)(2,1)S(1)}, bf16[80,2048]{1,0:T(8,128)(2,1)S(1)}, u32[]{:S(2)}, u32[]{:S(2)}) collective-permute-start(bf16[80,2048]{1,0:T(8,128)(2,1)S(1)} %get-tuple-element.16), channel_id=1, source_target_pairs={{0,8},{8,0},{16,24},{24,16},{1,9},{9,1},{17,25},{25,17},{2,10},{10... | collective-permute-start | bytes 983048 | tf_op jit(solution)/shard_map/ppermute | solution.py:38
  39.5 6.5 %collective-permute-start.5 = (bf16[40,2048]{1,0:T(8,128)(2,1)S(1)}, bf16[40,2048]{1,0:T(8,128)(2,1)S(1)}, u32[]{:S(2)}, u32[]{:S(2)}) collective-permute-start(bf16[40,2048]{1,0:T(8,128)(2,1)S(1)} %slice.46), channel_id=1, source_target_pairs={{0,16},{8,24},{16,0},{24,8},{1,17},{9,25},{17,1},{25,9},{2,18},{10... | collective-permute-start | bytes 491528 | tf_op jit(solution)/shard_map/ppermute | solution.py:38
  41.2 3.3 %collective-permute-start.6 = (f32[8,256]{1,0:T(8,128)S(1)}, f32[8,256]{1,0:T(8,128)S(1)}, u32[]{:S(2)}, u32[]{:S(2)}) collective-permute-start(f32[8,256]{1,0:T(8,128)S(1)} %fusion.3), channel_id=1, source_target_pairs={{0,8},{8,0},{16,24},{24,16},{1,9},{9,1},{17,25},{25,17},{2,10},{10... | collective-permute-start | bytes 24584 | tf_op jit(solution)/shard_map/ppermute | solution.py:38
  44.5 10.7 %collective-permute-start.7 = (f32[8,256]{1,0:T(8,128)S(1)}, f32[8,256]{1,0:T(8,128)S(1)}, u32[]{:S(2)}, u32[]{:S(2)}) collective-permute-start(f32[8,256]{1,0:T(8,128)S(1)} %add.28), channel_id=1, source_target_pairs={{0,16},{8,24},{16,0},{24,8},{1,17},{9,25},{17,1},{25,9},{2,18},{10... | collective-permute-start | bytes 24584 | tf_op jit(solution)/shard_map/ppermute | solution.py:38
  46.7 12.9 %all-to-all-start.1 = ((bf16[8,40,256]{2,1,0:T(8,128)(2,1)}), bf16[8,40,256]{2,1,0:T(8,128)(2,1)S(1)}, u32[]{:S(2)}, u32[]{:S(2)}) async-start(bf16[8,40,256]{2,1,0:T(8,128)(2,1)} %bitcast.30), calls=%async_computation.1 | async-start | bytes 327680 | tf_op jit(solution)/shard_map/all_to_all | solution.py:512

commit v2 on v1

--- a/solution.py
+++ b/solution.py
@@ -383,6 +383,16 @@
     return wanted if size % wanted == 0 else size
 
 
+def input_grads(rows, in_ref, first, kept_ref, away_ref, block):
+    half = kept_ref.shape[0]
+    for start in range(0, kept_ref.shape[1], block):
+        part, columns = slice(start, start + block), slice(first + start, first + start + block)
+        total = jnp.dot(rows[0], in_ref[0, 0, :, columns], preferred_element_type=jnp.float32)
+        total += jnp.dot(rows[1], in_ref[0, 1, :, columns], preferred_element_type=jnp.float32)
+        kept_ref[:, part] = total[:half]
+        away_ref[:, part] = total[half:].astype(jnp.bfloat16)
+
+
 def hidden_back_kernel(
     block,
     rows_ref,
@@ -392,12 +402,13 @@
     down_ref,
     gate_ref,
     up_ref,
+    gate_rows_ref,
+    up_rows_ref,
     kept_ref,
     away_ref,
 ):
-    size, width = down_ref.shape[1] // 2, down_ref.shape[2]
+    size = down_ref.shape[1] // 2
     rows = rows_ref[...]
-    half = rows.shape[0] // 2
     scale, cubic = math.sqrt(2 / math.pi), 0.044715
     for start in (0, size):
         part = slice(start, start + size)
@@ -411,37 +422,60 @@
         slope = cdf + (0.5 * scale) * value * (1.0 - bend * bend) * (1.0 + 3 * cubic * square)
         gate_ref[part] = (grad * up * slope).astype(jnp.bfloat16)
         up_ref[part] = (grad * (value * cdf)).astype(jnp.bfloat16)
-    gate_grad, up_grad = gate_ref[...].T, up_ref[...].T
-    for start in range(0, width, block):
-        part = slice(start, start + block)
-        total = jnp.dot(gate_grad, in_ref[0, 0, :, part], preferred_element_type=jnp.float32)
-        total += jnp.dot(up_grad, in_ref[0, 1, :, part], preferred_element_type=jnp.float32)
-        kept_ref[:, part] = total[:half]
-        away_ref[:, part] = total[half:].astype(jnp.bfloat16)
+    gate_rows_ref[...] = gate_ref[...].T
+    up_rows_ref[...] = up_ref[...].T
+    input_grads((gate_rows_ref[...], up_rows_ref[...]), in_ref, 0, kept_ref, away_ref, block)
+
+
+def rest_back_kernel(block, gate_rows_ref, up_rows_ref, in_ref, kept_ref, away_ref):
+    first = in_ref.shape[3] - kept_ref.shape[1]
+    input_grads((gate_rows_ref[...], up_rows_ref[...]), in_ref, first, kept_ref, away_ref, block)
 
 
 def hidden_back(rows, gate_pre, up_pre, in_near, down_near):
     count, width = rows.shape
-    hidden = in_near.shape[2]
+    hidden = down_near.shape[1]
     near_spec = pl.BlockSpec(memory_space=pltpu.VMEM)
     return pl.pallas_call(
-        partial(hidden_back_kernel, block_of(width, 1024)),
+        partial(hidden_back_kernel, width // 2),
         in_specs=[near_spec] * 5,
-        out_specs=[near_spec] * 4,
+        out_specs=[near_spec] * 6,
         out_shape=(
             pltpu.VMEM((hidden, count), jnp.bfloat16),
             pltpu.VMEM((hidden, count), jnp.bfloat16),
-            pltpu.VMEM((count // 2, width), jnp.float32),
-            pltpu.VMEM((count // 2, width), jnp.bfloat16),
+            pltpu.VMEM((count, hidden), jnp.bfloat16),
+            pltpu.VMEM((count, hidden), jnp.bfloat16),
+            pltpu.VMEM((count // 2, width // 2), jnp.float32),
+            pltpu.VMEM((count // 2, width // 2), jnp.bfloat16),
         ),
         compiler_params=pltpu.CompilerParams(vmem_limit_bytes=12 << 20),
         cost_estimate=pl.CostEstimate(
-            flops=6 * count * hidden * width,
-            bytes_accessed=6 * hidden * width,
+            flops=4 * count * hidden * width,
+            bytes_accessed=4 * hidden * width,
             transcendentals=count * hidden,
         ),
         name="hidden_back",
     )(rows, near(gate_pre), near(up_pre), near(in_near), near(down_near))
+
+
+def rest_back(gate_rows, up_rows, in_near):
+    count, hidden = gate_rows.shape
+    width = in_near.shape[3]
+    near_spec = pl.BlockSpec(memory_space=pltpu.VMEM)
+    return pl.pallas_call(
+        partial(rest_back_kernel, width // 2),
+        in_specs=[near_spec] * 3,
+        out_specs=[near_spec] * 2,
+        out_shape=(
+            pltpu.VMEM((count // 2, width // 2), jnp.float32),
+            pltpu.VMEM((count // 2, width // 2), jnp.bfloat16),
+        ),
+        compiler_params=pltpu.CompilerParams(vmem_limit_bytes=12 << 20),
+        cost_estimate=pl.CostEstimate(
+            flops=2 * count * hidden * width, bytes_accessed=2 * hidden * width, transcendentals=0
+        ),
+        name="rest_back",
+    )(near(gate_rows), near(up_rows), near(in_near))
 
 
 def half_kernel(grad_ref, rows_ref, *refs):
@@ -503,12 +537,16 @@
     gate_dot = jnp.sum(got[:, 2 * capacity : 2 * capacity + 3].astype(jnp.float32), axis=(0, 1))
     counts = jnp.sum(all_grads[:, capacity + 3, :experts].astype(jnp.float32), axis=0)
 
-    gate_grad, up_grad, kept, away = hidden_back(
+    gate_grad, up_grad, gate_rows, up_rows, kept, away = hidden_back(
         row_grads, gate_pre, up_pre, in_near, down_near
     )
+    more_kept, more_away = rest_back(gate_rows, up_rows, in_near)
     summed = kept + swap(away, 1).astype(jnp.float32)
-    summed = reduce_groups(summed, 2)
-    going = summed.astype(jnp.bfloat16).reshape(capacity, experts, width).transpose(1, 0, 2)
+    more = more_kept + swap(more_away, 1).astype(jnp.float32)
+    summed = reduce_groups(summed, 2).astype(jnp.bfloat16)
+    more = reduce_groups(more, 2).astype(jnp.bfloat16)
+    going = jnp.concatenate([summed, more], axis=1)
+    going = going.reshape(capacity, experts, width).transpose(1, 0, 2)
     returned = lax.all_to_all(going, "expert", split_axis=0, concat_axis=0, tiled=True)
     weight_grad = half_weight_grad(0, gate_grad, row_tokens)
     weight_grad = half_weight_grad(1, up_grad, row_tokens, weight_grad)

time: 60.8 us -> 64.9 us (1.067)
  starting transfers between devices: 10.4 us -> 12.3 us
  waiting for transfers between devices: 7.08 us -> 8.95 us
    ppermute x8 -> x10, starting transfers between devices: 5.03 us -> 6.99 us  [swap(): return lax.ppermute(value, 'dp', [(i, i ^ distance) for i in range(size)])]
    ppermute x8 -> x10, waiting for transfers between devices: 3.32 us -> 5.2 us  [swap(): return lax.ppermute(value, 'dp', [(i, i ^ distance) for i in range(size)])]
    pallas_call x1 -> x2, Pallas kernels: 4.08 us -> 4.25 us  [the longest x1 3.23 us: hidden_back(): pl.pallas_call(partial(hidden_back_kernel, width // 2), in_specs=[near_sp...]
  transfers between devices with their start and end apart: 9 -> 11, of which waited for: 4 -> 4; matrix products, arithmetic and copies ran while one was open for 3% -> 3% of each run, Pallas kernels for 24% -> 23%
where the time goes in v2:
time: 64.9 us; the launch traced here: 64.6 us
  Pallas kernels  20.6 us (32%)
  blocking collectives  18.6 us (29%)
  starting transfers between devices  12.3 us (19%)
  waiting for transfers between devices  8.95 us (14%)
  matrix products  1.39 us (2%)
  other arithmetic  0.99 us (2%)
  local copies, waits for them, and re-layouts  0.88 us (1%)
  between operations  0.88 us (1%)
    all_to_all x1, blocking collectives, aligned_device(): lax.all_to_all(send, 'expert', split_axis=0, concat_axis=0, tiled=True)  18.6 us
    ppermute x10, starting transfers between devices, swap(): return lax.ppermute(value, 'dp', [(i, i ^ distance) for i in range(size)])  6.99 us
    pallas_call x2, Pallas kernels, half_weight_grad(): pl.pallas_call(half_kernel, grid=(hidden // block,), in_specs=[pl.BlockSp...  6.4 us
    all_to_all x1, starting transfers between devices, aligned_device(): lax.all_to_all(going, 'expert', split_axis=0, concat_axis=0, tiled=True)  5.31 us
    ppermute x10, waiting for transfers between devices, swap(): return lax.ppermute(value, 'dp', [(i, i ^ distance) for i in range(size)])  5.2 us
    pallas_call x1, Pallas kernels, fetch(): pl.pallas_call(partial(fetch_kernel, pieces), in_specs=[pl.BlockSpec(memo...  4.08 us
    all_to_all x1, waiting for transfers between devices, aligned_device(): lax.all_to_all(going, 'expert', split_axis=0, concat_axis=0, tiled=True)  3.75 us
    pallas_call x1, Pallas kernels, hidden_back(): pl.pallas_call(partial(hidden_back_kernel, width // 2), in_specs=[near_sp...  3.23 us
  transfers between devices with their start and end apart: 11, of which 4 were waited for; matrix products, arithmetic and copies ran while one was open for 3% of the time, Pallas kernels for 23%

profile of v2, /device:TPU:0, one launch (start us, length us, event | category | flops | bytes accessed | tf_op | source)
XLA Modules:
  0.0 64.6 jit_solution(9898120335779918097)
XLA Ops:
  0.6 1.8 %prelude.1 = (bf16[8,88,256]{2,1,0:T(8,128)(2,1)S(1)}, bf16[320,256]{1,0:T(8,128)(2,1)S(1)}) custom-call(s32[1,256]{1,0:T(1,128)} %bitcast.43, f32[8,256]{1,0:T(8,128)} %bitcast.42, bf16[256,256]{1,0:T(8,128)(2,1)} %tokens_hbm.1, bf16[256,256]{1,0:T(8,128)(2,1)} %grads_hbm.1, bf16[256,256]{1,0:T(8,128)(2,1)} %expert_out_hbm.1), custom_call_target="tpu_custom_call" | custom-call | tf_op jit(solution)/shard_map/prelude/pallas_call | solution.py:277
  2.5 18.6 %all_to_all.10.after_ref = bf16[8,88,256]{2,1,0:T(8,128)(2,1)S(1)} all-to-all(bf16[8,88,256]{2,1,0:T(8,128)(2,1)S(1)} %get-tuple-element.16), channel_id=1, replica_groups=mesh['dp'=4,'expert'=8] {'expert'}, dimensions={0} | all-to-all | bytes 720896 | tf_op jit(solution)/shard_map/all_to_all | solution.py:522
  21.1 1.6 %collective-permute-start.2 = (bf16[40,2048]{1,0:T(8,128)(2,1)S(1)}, bf16[40,2048]{1,0:T(8,128)(2,1)S(1)}, u32[]{:S(2)}, u32[]{:S(2)}) collective-permute-start(bf16[40,2048]{1,0:T(8,128)(2,1)S(1)} %bitcast.37), channel_id=1, source_target_pairs={{0,16},{8,24},{16,0},{24,8},{1,17},{9,25},{17,1},{25,9},{2,18},{10... | collective-permute-start | bytes 491528 | tf_op jit(solution)/shard_map/ppermute | solution.py:38
  22.7 0.6 collective-permute-start
  23.3 4.1 %fetch.1.in_ref = bf16[1,2,1280,2048]{3,2,1,0:T(8,128)(2,1)S(1)} custom-call(bf16[1,2,1280,2048]{3,2,1,0:T(8,128)(2,1)} %source_ref.1, bf16[8,88,256]{2,1,0:T(8,128)(2,1)S(1)} %all_to_all.10.after_ref), custom_call_target="tpu_custom_call" | custom-call | bytes 10485760 | tf_op jit(solution)/shard_map/fetch/pallas_call | solution.py:311
  27.5 0.1 collective-permute-start.3
  27.6 1.4 %collective-permute-done = bf16[48,2048]{1,0:T(8,128)(2,1)S(1)} collective-permute-done((bf16[48,2048]{1,0:T(8,128)(2,1)S(1)}, bf16[48,2048]{1,0:T(8,128)(2,1)S(1)}, u32[]{:S(2)}, u32[]{:S(2)}) %collective-permute-start) | collective-permute-done | bytes 196640 | tf_op jit(solution)/shard_map/ppermute | solution.py:38
  29.0 0.1 collective-permute-start.1
  29.2 1.5 %hidden_pre.1.up_pre_ref = f32[1280,160]{1,0:T(8,128)S(1)} custom-call(bf16[160,2048]{1,0:T(8,128)(2,1)S(1)} %constant_dynamic-update-slice_fusion.rows_ref, bf16[1,2,1280,2048]{3,2,1,0:T(8,128)(2,1)S(1)} %fetch.1.in_ref), custom_call_target="tpu_custom_call" | custom-call | flops 838860800 | bytes 5242880 | tf_op jit(solution)/shard_map/hidden_pre/pallas_call | solution.py:363
  30.7 2.5 %gate_pre.1 = (f32[1280,160]{1,0:T(8,128)S(1)}, bf16[1,1280,2048]{2,1,0:T(8,128)(2,1)S(1)}) custom-call(bf16[160,2048]{1,0:T(8,128)(2,1)S(1)} %constant_dynamic-update-slice_fusion.rows_ref, bf16[1,2,1280,2048]{3,2,1,0:T(8,128)(2,1)S(1)} %fetch.1.in_ref, bf16[1,1280,2048]{2,1,0:T(8,128)(2,1)} %down_hbm.1), custom_call_target="tpu_custom_call" | custom-call | flops 838860800 | bytes 5242880 | tf_op jit(solution)/shard_map/gate_pre/pallas_call | solution.py:371
  33.3 0.1 pad_maximum_fusion
  33.4 0.1 slice.39
  33.5 3.2 %hidden_back.1 = (bf16[1280,160]{1,0:T(8,128)(2,1)S(1)}, bf16[1280,160]{1,0:T(8,128)(2,1)S(1)}, bf16[160,1280]{1,0:T(8,128)(2,1)S(1)}, bf16[160,1280]{1,0:T(8,12...) custom-call(bf16[160,2048]{1,0:T(8,128)(2,1)S(1)} %bitcast.31, ...), custom_call_target="tpu_custom_call" | custom-call | flops 1677721600 | bytes 10485760 | tf_op jit(solution)/shard_map/hidden_back/pallas_call | solution.py:439
  36.7 1.0 %rest_back.1 = (f32[80,1024]{1,0:T(8,128)S(1)}, bf16[80,1024]{1,0:T(8,128)(2,1)S(1)}) custom-call(bf16[160,1280]{1,0:T(8,128)(2,1)S(1)} %get-tuple-element.21.gate_rows_ref, bf16[160,1280]{1,0:T(8,128)(2,1)S(1)} %get-tuple-element.22.up_rows_ref, bf16[1,2,1280,2048]{3,2,1,0:T(8,128)(2,1)S(1)} %fetch.1.in_ref), custom_call_target="tpu_custom_call" | custom-call | flops 838860800 | bytes 5242880 | tf_op jit(solution)/shard_map/rest_back/pallas_call | solution.py:465
  37.8 0.5 collective-permute-start.6
  38.3 0.1 multiply_reduce_fusion
  38.4 0.3 fusion.5
  38.7 0.2 fusion.4
  38.9 0.1 collective-permute-start.4
  38.9 0.4 collective-permute-start.8
  39.4 3.2 %weight_grad_half.2.refs_0_ = bf16[1,2,1280,2048]{3,2,1,0:T(8,128)(2,1)} custom-call(bf16[1280,160]{1,0:T(8,128)(2,1)S(1)} %get-tuple-element.26.grad_ref, bf16[160,2048]{1,0:T(8,128)(2,1)S(1)} %constant_dynamic-update-slice_fusion.rows_ref), custom_call_target="tpu_custom_call" | custom-call | flops 838860800 | bytes 5242880 | tf_op jit(solution)/shard_map/weight_grad_half/pallas_call | solution.py:492
  42.6 1.5 %collective-permute-start.9 = (f32[8,256]{1,0:T(8,128)S(1)}, f32[8,256]{1,0:T(8,128)S(1)}, u32[]{:S(2)}, u32[]{:S(2)}) collective-permute-start(f32[8,256]{1,0:T(8,128)S(1)} %add.36), channel_id=1, source_target_pairs={{0,16},{8,24},{16,0},{24,8},{1,17},{9,25},{17,1},{25,9},{2,18},{10... | collective-permute-start | bytes 24584 | tf_op jit(solution)/shard_map/ppermute | solution.py:38
  44.1 0.6 collective-permute-start.7
  44.8 1.6 %collective-permute-start.5 = (bf16[40,1024]{1,0:T(8,128)(2,1)S(1)}, bf16[40,1024]{1,0:T(8,128)(2,1)S(1)}, u32[]{:S(2)}, u32[]{:S(2)}) collective-permute-start(bf16[40,1024]{1,0:T(8,128)(2,1)S(1)} %slice.62), channel_id=1, source_target_pairs={{0,16},{8,24},{16,0},{24,8},{1,17},{9,25},{17,1},{25,9},{2,18},{10... | collective-permute-start | bytes 245768 | tf_op jit(solution)/shard_map/ppermute | solution.py:38
  46.4 2.9 %collective-permute-done.7 = bf16[40,1024]{1,0:T(8,128)(2,1)S(1)} collective-permute-done((bf16[40,1024]{1,0:T(8,128)(2,1)S(1)}, bf16[40,1024]{1,0:T(8,128)(2,1)S(1)}, u32[]{:S(2)}, u32[]{:S(2)}) %collective-permute-start.7) | collective-permute-done | bytes 81952 | tf_op jit(solution)/shard_map/ppermute | solution.py:38
  49.2 0.8 %collective-permute-done.5 = bf16[40,1024]{1,0:T(8,128)(2,1)S(1)} collective-permute-done((bf16[40,1024]{1,0:T(8,128)(2,1)S(1)}, bf16[40,1024]{1,0:T(8,128)(2,1)S(1)}, u32[]{:S(2)}, u32[]{:S(2)}) %collective-permute-start.5) | collective-permute-done | bytes 81952 | tf_op jit(solution)/shard_map/ppermute | solution.py:38
  50.1 0.7 %copy.20 = bf16[5,8,8,256]{3,2,0,1:T(8,128)(2,1)} copy(bf16[5,8,8,256]{3,2,1,0:T(8,128)(2,1)S(1)} %bitcast.40) | data formatting | bytes 327680 | tf_op jit(solution)/shard_map/reshape | solution.py:549
  50.8 5.3 %all-to-all-start.1 = ((bf16[8,40,256]{2,1,0:T(8,128)(2,1)}), bf16[8,40,256]{2,1,0:T(8,128)(2,1)S(1)}, u32[]{:S(2)}, u32[]{:S(2)}) async-start(bf16[8,40,256]{2,1,0:T(8,128)(2,1)} %bitcast.30), calls=%async_computation.1 | async-start | bytes 327680 | tf_op jit(solution)/shard_map/all_to_all | solution.py:550
  56.1 3.2 %weight_grad_half.3 = bf16[1,2,1280,2048]{3,2,1,0:T(8,128)(2,1)} custom-call(bf16[1280,160]{1,0:T(8,128)(2,1)S(1)} %get-tuple-element.25.grad_ref, bf16[160,2048]{1,0:T(8,128)(2,1)S(1)} %constant_dynamic-update-slice_fusion.rows_ref, bf16[1,2,1280,2048]{3,2,1,0:T(8,128)(2,1)} %weight_grad_half.2.refs_0_), custom_call_target="tpu_custom_call", output_to_operand_aliasing={{}: (2, {})} | custom-call | flops 838860800 | bytes 5242880 | tf_op jit(solution)/shard_map/weight_grad_half/pallas_call | solution.py:492
  59.3 0.6 add_bitcast_fusion
  59.9 3.7 %all-to-all-done.1 = bf16[8,40,256]{2,1,0:T(8,128)(2,1)S(1)} async-done(((bf16[8,40,256]{2,1,0:T(8,128)(2,1)}), bf16[8,40,256]{2,1,0:T(8,128)(2,1)S(1)}, u32[]{:S(2)}, u32[]{:S(2)}) %all-to-all-start.1) | async-done | bytes 163872 | tf_op jit(solution)/shard_map/all_to_all | solution.py:550
  63.7 0.9 %fusion = bf16[256,256]{1,0:T(8,128)(2,1)} fusion(f32[256,256]{1,0:T(8,128)S(1)} %fusion.5, bf16[320,256]{1,0:T(8,128)(2,1)S(1)} %get-tuple-element.15, bf16[320,256]{1,0:T(8,128)(2,1)S(1)} %bitcast.41), kind=kOutput, calls=%fused_computation.1 | convolution fusion | flops 42074112 | bytes 720896 | tf_op jit(solution)/shard_map/dot_general | solution.py:566
  (35 shorter events, 0.4 us)
Async XLA Ops:
  0.6 37.7 %copy-start = (bf16[256,8]{0,1:T(8,128)(2,1)S(1)}, bf16[256,8]{0,1:T(8,128)(2,1)}, u32[]{:S(2)}) copy-start(bf16[256,8]{0,1:T(8,128)(2,1)} %param.15) | copy-start | bytes 12292
  21.1 6.3 %collective-permute-start.2 = (bf16[40,2048]{1,0:T(8,128)(2,1)S(1)}, bf16[40,2048]{1,0:T(8,128)(2,1)S(1)}, u32[]{:S(2)}, u32[]{:S(2)}) collective-permute-start(bf16[40,2048]{1,0:T(8,128)(2,1)S(1)} %bitcast.37), channel_id=1, source_target_pairs={{0,16},{8,24},{16,0},{24,8},{1,17},{9,25},{17,1},{25,9},{2,18},{10... | collective-permute-start | bytes 491528 | tf_op jit(solution)/shard_map/ppermute | solution.py:38
  22.7 6.3 %collective-permute-start = (bf16[48,2048]{1,0:T(8,128)(2,1)S(1)}, bf16[48,2048]{1,0:T(8,128)(2,1)S(1)}, u32[]{:S(2)}, u32[]{:S(2)}) collective-permute-start(bf16[48,2048]{1,0:T(8,128)(2,1)S(1)} %bitcast.34), channel_id=1, source_target_pairs={{0,16},{8,24},{16,0},{24,8},{1,17},{9,25},{17,1},{25,9},{2,18},{10... | collective-permute-start | bytes 589832 | tf_op jit(solution)/shard_map/ppermute | solution.py:38
  27.5 1.7 %collective-permute-start.3 = (bf16[80,2048]{1,0:T(8,128)(2,1)S(1)}, bf16[80,2048]{1,0:T(8,128)(2,1)S(1)}, u32[]{:S(2)}, u32[]{:S(2)}) collective-permute-start(bf16[80,2048]{1,0:T(8,128)(2,1)S(1)} %pad_maximum_fusion.2), channel_id=1, source_target_pairs={{0,8},{8,0},{16,24},{24,16},{1,9},{9,1},{17,25},{25,17},{2,10},{10... | collective-permute-start | bytes 983048 | tf_op jit(solution)/shard_map/ppermute | solution.py:38
  29.0 4.2 %collective-permute-start.1 = (bf16[96,2048]{1,0:T(8,128)(2,1)S(1)}, bf16[96,2048]{1,0:T(8,128)(2,1)S(1)}, u32[]{:S(2)}, u32[]{:S(2)}) collective-permute-start(bf16[96,2048]{1,0:T(8,128)(2,1)S(1)} %pad_maximum_fusion.1), channel_id=1, source_target_pairs={{0,8},{8,0},{16,24},{24,16},{1,9},{9,1},{17,25},{25,17},{2,10},{10... | collective-permute-start | bytes 1179656 | tf_op jit(solution)/shard_map/ppermute | solution.py:38
  36.7 1.6 %copy-start.2 = (f32[256,8]{0,1:T(8,128)S(1)}, f32[256,8]{0,1:T(8,128)}, u32[]{:S(2)}) copy-start(f32[256,8]{0,1:T(8,128)} %param.11) | copy-start | bytes 24580
  36.7 1.6 %copy-start.3 = (s32[256,1]{0,1:T(1,128)S(1)}, s32[256,1]{0,1:T(1,128)}, u32[]{:S(2)}) copy-start(s32[256,1]{0,1:T(1,128)} %param.12) | copy-start | bytes 3076
  36.7 1.9 %copy-start.1 = (bf16[256,256]{1,0:T(8,128)(2,1)S(1)}, bf16[256,256]{1,0:T(8,128)(2,1)}, u32[]{:S(2)}) copy-start(bf16[256,256]{1,0:T(8,128)(2,1)} %tokens_hbm.1) | copy-start | bytes 393220
  37.8 6.3 %collective-permute-start.6 = (bf16[80,1024]{1,0:T(8,128)(2,1)S(1)}, bf16[80,1024]{1,0:T(8,128)(2,1)S(1)}, u32[]{:S(2)}, u32[]{:S(2)}) collective-permute-start(bf16[80,1024]{1,0:T(8,128)(2,1)S(1)} %get-tuple-element.24), channel_id=1, source_target_pairs={{0,8},{8,0},{16,24},{24,16},{1,9},{9,1},{17,25},{25,17},{2,10},{10... | collective-permute-start | bytes 491528 | tf_op jit(solution)/shard_map/ppermute | solution.py:38
  38.9 5.9 %collective-permute-start.4 = (bf16[80,1024]{1,0:T(8,128)(2,1)S(1)}, bf16[80,1024]{1,0:T(8,128)(2,1)S(1)}, u32[]{:S(2)}, u32[]{:S(2)}) collective-permute-start(bf16[80,1024]{1,0:T(8,128)(2,1)S(1)} %get-tuple-element.20), channel_id=1, source_target_pairs={{0,8},{8,0},{16,24},{24,16},{1,9},{9,1},{17,25},{25,17},{2,10},{10... | collective-permute-start | bytes 491528 | tf_op jit(solution)/shard_map/ppermute | solution.py:38
  38.9 3.6 %collective-permute-start.8 = (f32[8,256]{1,0:T(8,128)S(1)}, f32[8,256]{1,0:T(8,128)S(1)}, u32[]{:S(2)}, u32[]{:S(2)}) collective-permute-start(f32[8,256]{1,0:T(8,128)S(1)} %fusion.4), channel_id=1, source_target_pairs={{0,8},{8,0},{16,24},{24,16},{1,9},{9,1},{17,25},{25,17},{2,10},{10... | collective-permute-start | bytes 24584 | tf_op jit(solution)/shard_map/ppermute | solution.py:38
  42.6 16.7 %collective-permute-start.9 = (f32[8,256]{1,0:T(8,128)S(1)}, f32[8,256]{1,0:T(8,128)S(1)}, u32[]{:S(2)}, u32[]{:S(2)}) collective-permute-start(f32[8,256]{1,0:T(8,128)S(1)} %add.36), channel_id=1, source_target_pairs={{0,16},{8,24},{16,0},{24,8},{1,17},{9,25},{17,1},{25,9},{2,18},{10... | collective-permute-start | bytes 24584 | tf_op jit(solution)/shard_map/ppermute | solution.py:38
  44.1 5.1 %collective-permute-start.7 = (bf16[40,1024]{1,0:T(8,128)(2,1)S(1)}, bf16[40,1024]{1,0:T(8,128)(2,1)S(1)}, u32[]{:S(2)}, u32[]{:S(2)}) collective-permute-start(bf16[40,1024]{1,0:T(8,128)(2,1)S(1)} %slice.61), channel_id=1, source_target_pairs={{0,16},{8,24},{16,0},{24,8},{1,17},{9,25},{17,1},{25,9},{2,18},{10... | collective-permute-start | bytes 245768 | tf_op jit(solution)/shard_map/ppermute | solution.py:38
  44.8 5.3 %collective-permute-start.5 = (bf16[40,1024]{1,0:T(8,128)(2,1)S(1)}, bf16[40,1024]{1,0:T(8,128)(2,1)S(1)}, u32[]{:S(2)}, u32[]{:S(2)}) collective-permute-start(bf16[40,1024]{1,0:T(8,128)(2,1)S(1)} %slice.62), channel_id=1, source_target_pairs={{0,16},{8,24},{16,0},{24,8},{1,17},{9,25},{17,1},{25,9},{2,18},{10... | collective-permute-start | bytes 245768 | tf_op jit(solution)/shard_map/ppermute | solution.py:38
  50.8 12.9 %all-to-all-start.1 = ((bf16[8,40,256]{2,1,0:T(8,128)(2,1)}), bf16[8,40,256]{2,1,0:T(8,128)(2,1)S(1)}, u32[]{:S(2)}, u32[]{:S(2)}) async-start(bf16[8,40,256]{2,1,0:T(8,128)(2,1)} %bitcast.30), calls=%async_computation.1 | async-start | bytes 327680 | tf_op jit(solution)/shard_map/all_to_all | solution.py:550

commit v3 on v2

--- a/solution.py
+++ b/solution.py
@@ -200,8 +200,10 @@
     tokens_hbm,
     grads_hbm,
     expert_out_hbm,
+    down_hbm,
     send_ref,
     place_ref,
+    down_ref,
     route_ref,
     probs_ref,
     tokens_ref,
@@ -215,6 +217,13 @@
         pltpu.make_async_copy(source, target, sems.at[number])
         for number, (source, target) in enumerate(zip(sources, targets))
     ]
+    pieces = sems.shape[0] - len(copies)
+    size = down_ref.shape[0] // pieces
+    for piece in range(pieces):
+        rows = pl.ds(piece * size, size)
+        copies.append(
+            pltpu.make_async_copy(down_hbm.at[0, rows], down_ref.at[rows], sems.at[len(copies)])
+        )
     for copy in copies:
         copy.start()
     experts, count = probs_ref.shape
@@ -261,6 +270,8 @@
         send_ref[expert, :capacity] = rows_x[rows].astype(half)
         send_ref[expert, capacity : 2 * capacity] = rows_dy[rows].astype(half)
         send_ref[expert, 2 * capacity :] = side
+    for copy in copies[5:]:
+        copy.wait()
 
 
 def far(value):
@@ -271,21 +282,23 @@
     return pltpu.with_memory_space_constraint(value, pltpu.VMEM)
 
 
-def prelude(capacity, *args):
+def prelude(capacity, down_weight, *args):
     experts, count = args[1].shape
     width = args[2].shape[1]
     return pl.pallas_call(
         partial(prelude_kernel, capacity),
-        in_specs=[pl.BlockSpec(memory_space=pl.ANY)] * len(args),
+        in_specs=[pl.BlockSpec(memory_space=pl.ANY)] * (len(args) + 1),
+        out_specs=[pl.BlockSpec(memory_space=pltpu.VMEM)] * 3,
         out_shape=(
             jax.ShapeDtypeStruct((experts, 2 * capacity + 8, width), jnp.bfloat16),
             jax.ShapeDtypeStruct((experts * capacity, count), jnp.bfloat16),
+            pltpu.VMEM((down_weight.shape[1] // 2, down_weight.shape[2]), down_weight.dtype),
         ),
         scratch_shapes=[pltpu.VMEM(value.shape, value.dtype) for value in args]
-        + [pltpu.SemaphoreType.DMA((len(args),))],
+        + [pltpu.SemaphoreType.DMA((len(args) + 2,))],
         compiler_params=pltpu.CompilerParams(vmem_limit_bytes=8 << 20),
         name="prelude",
-    )(*[far(value) for value in args])
+    )(*[far(value) for value in args], far(down_weight))
 
 
 def fetch_kernel(pieces, source_ref, after_ref, target_ref, sems):
@@ -334,13 +347,16 @@
 
 def gate_pre_kernel(rows_ref, in_ref, down_hbm, out_ref, down_ref, sems):
     pieces = sems.shape[0]
-    size = down_ref.shape[1] // pieces
-    copies = []
-    for piece in range(pieces):
-        where = (0, pl.ds(piece * size, size))
-        copies.append(
-            pltpu.make_async_copy(down_hbm.at[where], down_ref.at[where], sems.at[piece])
+    half = down_ref.shape[0]
+    size = half // pieces
+    copies = [
+        pltpu.make_async_copy(
+            down_hbm.at[0, pl.ds(half + piece * size, size)],
+            down_ref.at[pl.ds(piece * size, size)],
+            sems.at[piece],
         )
+        for piece in range(pieces)
+    ]
     for copy in copies:
         copy.start()
     pre_activation(0, rows_ref, in_ref, out_ref)
@@ -372,7 +388,7 @@
         gate_pre_kernel,
         in_specs=[near_spec] * 2 + [pl.BlockSpec(memory_space=pl.ANY)],
         out_specs=[near_spec] * 2,
-        out_shape=(out, pltpu.VMEM(down_weight.shape, down_weight.dtype)),
+        out_shape=(out, pltpu.VMEM((hidden // 2, width), down_weight.dtype)),
         scratch_shapes=[pltpu.SemaphoreType.DMA((4,))],
         name="gate_pre",
         **settings,
@@ -400,6 +416,7 @@
     up_pre_ref,
     in_ref,
     down_ref,
+    other_ref,
     gate_ref,
     up_ref,
     gate_rows_ref,
@@ -407,13 +424,13 @@
     kept_ref,
     away_ref,
 ):
-    size = down_ref.shape[1] // 2
+    size = down_ref.shape[0]
     rows = rows_ref[...]
     scale, cubic = math.sqrt(2 / math.pi), 0.044715
-    for start in (0, size):
-        part = slice(start, start + size)
+    for number, weight_ref in enumerate((down_ref, other_ref)):
+        part = slice(number * size, (number + 1) * size)
         grad = lax.dot_general(
-            down_ref[0, part], rows, contract_last, preferred_element_type=jnp.float32
+            weight_ref[...], rows, contract_last, preferred_element_type=jnp.float32
         )
         value, up = gate_pre_ref[part], up_pre_ref[part]
         square = value * value
@@ -432,13 +449,13 @@
     input_grads((gate_rows_ref[...], up_rows_ref[...]), in_ref, first, kept_ref, away_ref, block)
 
 
-def hidden_back(rows, gate_pre, up_pre, in_near, down_near):
+def hidden_back(rows, gate_pre, up_pre, in_near, downs):
     count, width = rows.shape
-    hidden = down_near.shape[1]
+    hidden = in_near.shape[2]
     near_spec = pl.BlockSpec(memory_space=pltpu.VMEM)
     return pl.pallas_call(
         partial(hidden_back_kernel, width // 2),
-        in_specs=[near_spec] * 5,
+        in_specs=[near_spec] * 6,
         out_specs=[near_spec] * 6,
         out_shape=(
             pltpu.VMEM((hidden, count), jnp.bfloat16),
@@ -455,7 +472,7 @@
             transcendentals=count * hidden,
         ),
         name="hidden_back",
-    )(rows, near(gate_pre), near(up_pre), near(in_near), near(down_near))
+    )(rows, near(gate_pre), near(up_pre), near(in_near), *map(near, downs))
 
 
 def rest_back(gate_rows, up_rows, in_near):
@@ -518,7 +535,9 @@
     full_width = experts * width
     probs = router_probs.T
     route = expert_index.reshape(1, token_count)
-    send, mask = prelude(capacity, route, probs, tokens, out_grad, expert_out)
+    send, mask, first_down = prelude(
+        capacity, down_weight, route, probs, tokens, out_grad, expert_out
+    )
     got = lax.all_to_all(send, "expert", split_axis=0, concat_axis=0, tiled=True)
     in_near = fetch(in_weight, got)
 
@@ -531,14 +550,14 @@
     all_grads = gather_groups(all_grads, first)
     row_tokens = gather_groups(row_tokens, last)
     all_grads = gather_groups(all_grads, last).reshape(groups, capacity + 8, full_width)
-    gate_pre, down_near = hidden_pre(0, row_tokens, in_near, down_weight)
+    gate_pre, second_down = hidden_pre(0, row_tokens, in_near, down_weight)
     up_pre = hidden_pre(1, row_tokens, in_near)
     row_grads = all_grads[:, :capacity].reshape(groups * capacity, full_width)
     gate_dot = jnp.sum(got[:, 2 * capacity : 2 * capacity + 3].astype(jnp.float32), axis=(0, 1))
     counts = jnp.sum(all_grads[:, capacity + 3, :experts].astype(jnp.float32), axis=0)
 
     gate_grad, up_grad, gate_rows, up_rows, kept, away = hidden_back(
-        row_grads, gate_pre, up_pre, in_near, down_near
+        row_grads, gate_pre, up_pre, in_near, (first_down, second_down)
     )
     more_kept, more_away = rest_back(gate_rows, up_rows, in_near)
     summed = kept + swap(away, 1).astype(jnp.float32)

time: 64.9 us -> 65.1 us (level)
  transfers between devices with their start and end apart: 11 -> 11, of which waited for: 4 -> 4; matrix products, arithmetic and copies ran while one was open for 3% -> 3% of each run, Pallas kernels for 23% -> 22%
where the time goes in v3:
time: 65.1 us; the launch traced here: 64.8 us
  Pallas kernels  20.8 us (32%)
  blocking collectives  18.6 us (29%)
  starting transfers between devices  12.3 us (19%)
  waiting for transfers between devices  8.95 us (14%)
  matrix products  1.39 us (2%)
  other arithmetic  0.99 us (2%)
  local copies, waits for them, and re-layouts  0.88 us (1%)
  between operations  0.88 us (1%)
    all_to_all x1, blocking collectives, aligned_device(): lax.all_to_all(send, 'expert', split_axis=0, concat_axis=0, tiled=True)  18.6 us
    ppermute x10, starting transfers between devices, swap(): return lax.ppermute(value, 'dp', [(i, i ^ distance) for i in range(size)])  6.99 us
    pallas_call x2, Pallas kernels, half_weight_grad(): pl.pallas_call(half_kernel, grid=(hidden // block,), in_specs=[pl.BlockSp...  6.4 us
    all_to_all x1, starting transfers between devices, aligned_device(): lax.all_to_all(going, 'expert', split_axis=0, concat_axis=0, tiled=True)  5.3 us
    ppermute x10, waiting for transfers between devices, swap(): return lax.ppermute(value, 'dp', [(i, i ^ distance) for i in range(size)])  5.2 us
    pallas_call x1, Pallas kernels, fetch(): pl.pallas_call(partial(fetch_kernel, pieces), in_specs=[pl.BlockSpec(memo...  4.08 us
    all_to_all x1, waiting for transfers between devices, aligned_device(): lax.all_to_all(going, 'expert', split_axis=0, concat_axis=0, tiled=True)  3.75 us
    pallas_call x1, Pallas kernels, hidden_back(): pl.pallas_call(partial(hidden_back_kernel, width // 2), in_specs=[near_sp...  3.23 us
  transfers between devices with their start and end apart: 11, of which 4 were waited for; matrix products, arithmetic and copies ran while one was open for 3% of the time, Pallas kernels for 22%

profile of v3, /device:TPU:0, one launch (start us, length us, event | category | flops | bytes accessed | tf_op | source)
XLA Modules:
  0.0 64.8 jit_solution(12932579101160121510)
XLA Ops:
  0.6 2.0 %prelude.1 = (bf16[8,88,256]{2,1,0:T(8,128)(2,1)S(1)}, bf16[320,256]{1,0:T(8,128)(2,1)S(1)}, bf16[640,2048]{1,0:T(8,128)(2,1)S(1)}) custom-call(s32[1,256]{1,0:T(1,128)} %bitcast.43, f32[8,256]{1,0:T(8,128)} %bitcast.42, bf16[256,256]{1,0:T(8,128)(2,1)} %tokens_hbm.1, bf16[256,256]{1,0:T(8,128)(2,1)} %grads_hbm.1, bf16[256,256]{1,0:T(8,128)(2,1)} %expert_out_hbm.1, ...), custom_call_target="tpu_custom_call" | custom-call | tf_op jit(solution)/shard_map/prelude/pallas_call | solution.py:288
  2.7 18.6 %all_to_all.10.after_ref = bf16[8,88,256]{2,1,0:T(8,128)(2,1)S(1)} all-to-all(bf16[8,88,256]{2,1,0:T(8,128)(2,1)S(1)} %get-tuple-element.17), channel_id=1, replica_groups=mesh['dp'=4,'expert'=8] {'expert'}, dimensions={0} | all-to-all | bytes 720896 | tf_op jit(solution)/shard_map/all_to_all | solution.py:541
  21.3 1.6 %collective-permute-start.2 = (bf16[40,2048]{1,0:T(8,128)(2,1)S(1)}, bf16[40,2048]{1,0:T(8,128)(2,1)S(1)}, u32[]{:S(2)}, u32[]{:S(2)}) collective-permute-start(bf16[40,2048]{1,0:T(8,128)(2,1)S(1)} %bitcast.37), channel_id=1, source_target_pairs={{0,16},{8,24},{16,0},{24,8},{1,17},{9,25},{17,1},{25,9},{2,18},{10... | collective-permute-start | bytes 491528 | tf_op jit(solution)/shard_map/ppermute | solution.py:38
  22.9 0.6 collective-permute-start
  23.5 4.1 %fetch.1.in_ref = bf16[1,2,1280,2048]{3,2,1,0:T(8,128)(2,1)S(1)} custom-call(bf16[1,2,1280,2048]{3,2,1,0:T(8,128)(2,1)} %source_ref.1, bf16[8,88,256]{2,1,0:T(8,128)(2,1)S(1)} %all_to_all.10.after_ref), custom_call_target="tpu_custom_call" | custom-call | bytes 10485760 | tf_op jit(solution)/shard_map/fetch/pallas_call | solution.py:324
  27.7 0.1 collective-permute-start.3
  27.7 1.4 %collective-permute-done = bf16[48,2048]{1,0:T(8,128)(2,1)S(1)} collective-permute-done((bf16[48,2048]{1,0:T(8,128)(2,1)S(1)}, bf16[48,2048]{1,0:T(8,128)(2,1)S(1)}, u32[]{:S(2)}, u32[]{:S(2)}) %collective-permute-start) | collective-permute-done | bytes 196640 | tf_op jit(solution)/shard_map/ppermute | solution.py:38
  29.2 0.1 collective-permute-start.1
  29.3 0.0 collective-permute-done.3
  29.4 2.5 %gate_pre.1 = (f32[1280,160]{1,0:T(8,128)S(1)}, bf16[640,2048]{1,0:T(8,128)(2,1)S(1)}) custom-call(bf16[160,2048]{1,0:T(8,128)(2,1)S(1)} %constant_dynamic-update-slice_fusion.rows_ref, bf16[1,2,1280,2048]{3,2,1,0:T(8,128)(2,1)S(1)} %fetch.1.in_ref, bf16[1,1280,2048]{2,1,0:T(8,128)(2,1)} %down_hbm.3), custom_call_target="tpu_custom_call" | custom-call | flops 838860800 | bytes 5242880 | tf_op jit(solution)/shard_map/gate_pre/pallas_call | solution.py:387
  31.9 1.5 %hidden_pre.1.up_pre_ref = f32[1280,160]{1,0:T(8,128)S(1)} custom-call(bf16[160,2048]{1,0:T(8,128)(2,1)S(1)} %constant_dynamic-update-slice_fusion.rows_ref, bf16[1,2,1280,2048]{3,2,1,0:T(8,128)(2,1)S(1)} %fetch.1.in_ref), custom_call_target="tpu_custom_call" | custom-call | flops 838860800 | bytes 5242880 | tf_op jit(solution)/shard_map/hidden_pre/pallas_call | solution.py:379
  33.5 0.1 pad_maximum_fusion
  33.6 0.1 slice.39
  33.6 3.2 %hidden_back.1 = (bf16[1280,160]{1,0:T(8,128)(2,1)S(1)}, bf16[1280,160]{1,0:T(8,128)(2,1)S(1)}, bf16[160,1280]{1,0:T(8,128)(2,1)S(1)}, bf16[160,1280]{1,0:T(8,12...) custom-call(bf16[160,2048]{1,0:T(8,128)(2,1)S(1)} %bitcast.31, ...), custom_call_target="tpu_custom_call" | custom-call | flops 1677721600 | bytes 10485760 | tf_op jit(solution)/shard_map/hidden_back/pallas_call | solution.py:456
  36.9 1.0 %rest_back.1 = (f32[80,1024]{1,0:T(8,128)S(1)}, bf16[80,1024]{1,0:T(8,128)(2,1)S(1)}) custom-call(bf16[160,1280]{1,0:T(8,128)(2,1)S(1)} %get-tuple-element.23.gate_rows_ref, bf16[160,1280]{1,0:T(8,128)(2,1)S(1)} %get-tuple-element.24.up_rows_ref, bf16[1,2,1280,2048]{3,2,1,0:T(8,128)(2,1)S(1)} %fetch.1.in_ref), custom_call_target="tpu_custom_call" | custom-call | flops 838860800 | bytes 5242880 | tf_op jit(solution)/shard_map/rest_back/pallas_call | solution.py:482
  37.9 0.5 collective-permute-start.6
  38.5 0.1 multiply_reduce_fusion
  38.6 0.3 fusion.5
  38.9 0.2 fusion.4
  39.1 0.5 collective-permute-start.8
  39.6 3.2 %weight_grad_half.2.refs_0_ = bf16[1,2,1280,2048]{3,2,1,0:T(8,128)(2,1)} custom-call(bf16[1280,160]{1,0:T(8,128)(2,1)S(1)} %get-tuple-element.28.grad_ref, bf16[160,2048]{1,0:T(8,128)(2,1)S(1)} %constant_dynamic-update-slice_fusion.rows_ref), custom_call_target="tpu_custom_call" | custom-call | flops 838860800 | bytes 5242880 | tf_op jit(solution)/shard_map/weight_grad_half/pallas_call | solution.py:509
  42.8 1.5 %collective-permute-start.9 = (f32[8,256]{1,0:T(8,128)S(1)}, f32[8,256]{1,0:T(8,128)S(1)}, u32[]{:S(2)}, u32[]{:S(2)}) collective-permute-start(f32[8,256]{1,0:T(8,128)S(1)} %add.36), channel_id=1, source_target_pairs={{0,16},{8,24},{16,0},{24,8},{1,17},{9,25},{17,1},{25,9},{2,18},{10... | collective-permute-start | bytes 24584 | tf_op jit(solution)/shard_map/ppermute | solution.py:38
  44.3 0.6 collective-permute-start.7
  45.0 1.5 %collective-permute-start.5 = (bf16[40,1024]{1,0:T(8,128)(2,1)S(1)}, bf16[40,1024]{1,0:T(8,128)(2,1)S(1)}, u32[]{:S(2)}, u32[]{:S(2)}) collective-permute-start(bf16[40,1024]{1,0:T(8,128)(2,1)S(1)} %slice.62), channel_id=1, source_target_pairs={{0,16},{8,24},{16,0},{24,8},{1,17},{9,25},{17,1},{25,9},{2,18},{10... | collective-permute-start | bytes 245768 | tf_op jit(solution)/shard_map/ppermute | solution.py:38
  46.5 2.9 %collective-permute-done.7 = bf16[40,1024]{1,0:T(8,128)(2,1)S(1)} collective-permute-done((bf16[40,1024]{1,0:T(8,128)(2,1)S(1)}, bf16[40,1024]{1,0:T(8,128)(2,1)S(1)}, u32[]{:S(2)}, u32[]{:S(2)}) %collective-permute-start.7) | collective-permute-done | bytes 81952 | tf_op jit(solution)/shard_map/ppermute | solution.py:38
  49.4 0.8 %collective-permute-done.5 = bf16[40,1024]{1,0:T(8,128)(2,1)S(1)} collective-permute-done((bf16[40,1024]{1,0:T(8,128)(2,1)S(1)}, bf16[40,1024]{1,0:T(8,128)(2,1)S(1)}, u32[]{:S(2)}, u32[]{:S(2)}) %collective-permute-start.5) | collective-permute-done | bytes 81952 | tf_op jit(solution)/shard_map/ppermute | solution.py:38
  50.3 0.7 %copy.20 = bf16[5,8,8,256]{3,2,0,1:T(8,128)(2,1)} copy(bf16[5,8,8,256]{3,2,1,0:T(8,128)(2,1)S(1)} %bitcast.40) | data formatting | bytes 327680 | tf_op jit(solution)/shard_map/reshape | solution.py:568
  51.0 5.3 %all-to-all-start.1 = ((bf16[8,40,256]{2,1,0:T(8,128)(2,1)}), bf16[8,40,256]{2,1,0:T(8,128)(2,1)S(1)}, u32[]{:S(2)}, u32[]{:S(2)}) async-start(bf16[8,40,256]{2,1,0:T(8,128)(2,1)} %bitcast.30), calls=%async_computation.1 | async-start | bytes 327680 | tf_op jit(solution)/shard_map/all_to_all | solution.py:569
  56.3 3.2 %weight_grad_half.3 = bf16[1,2,1280,2048]{3,2,1,0:T(8,128)(2,1)} custom-call(bf16[1280,160]{1,0:T(8,128)(2,1)S(1)} %get-tuple-element.27.grad_ref, bf16[160,2048]{1,0:T(8,128)(2,1)S(1)} %constant_dynamic-update-slice_fusion.rows_ref, bf16[1,2,1280,2048]{3,2,1,0:T(8,128)(2,1)} %weight_grad_half.2.refs_0_), custom_call_target="tpu_custom_call", output_to_operand_aliasing={{}: (2, {})} | custom-call | flops 838860800 | bytes 5242880 | tf_op jit(solution)/shard_map/weight_grad_half/pallas_call | solution.py:509
  59.5 0.6 add_bitcast_fusion
  60.1 3.7 %all-to-all-done.1 = bf16[8,40,256]{2,1,0:T(8,128)(2,1)S(1)} async-done(((bf16[8,40,256]{2,1,0:T(8,128)(2,1)}), bf16[8,40,256]{2,1,0:T(8,128)(2,1)S(1)}, u32[]{:S(2)}, u32[]{:S(2)}) %all-to-all-start.1) | async-done | bytes 163872 | tf_op jit(solution)/shard_map/all_to_all | solution.py:569
  63.8 0.9 %fusion = bf16[256,256]{1,0:T(8,128)(2,1)} fusion(f32[256,256]{1,0:T(8,128)S(1)} %fusion.5, bf16[320,256]{1,0:T(8,128)(2,1)S(1)} %get-tuple-element.16, bf16[320,256]{1,0:T(8,128)(2,1)S(1)} %bitcast.41), kind=kOutput, calls=%fused_computation.1 | convolution fusion | flops 42074112 | bytes 720896 | tf_op jit(solution)/shard_map/dot_general | solution.py:585
  (35 shorter events, 0.4 us)
Async XLA Ops:
  0.6 37.9 %copy-start = (bf16[256,8]{0,1:T(8,128)(2,1)S(1)}, bf16[256,8]{0,1:T(8,128)(2,1)}, u32[]{:S(2)}) copy-start(bf16[256,8]{0,1:T(8,128)(2,1)} %param.15) | copy-start | bytes 12292
  21.3 6.3 %collective-permute-start.2 = (bf16[40,2048]{1,0:T(8,128)(2,1)S(1)}, bf16[40,2048]{1,0:T(8,128)(2,1)S(1)}, u32[]{:S(2)}, u32[]{:S(2)}) collective-permute-start(bf16[40,2048]{1,0:T(8,128)(2,1)S(1)} %bitcast.37), channel_id=1, source_target_pairs={{0,16},{8,24},{16,0},{24,8},{1,17},{9,25},{17,1},{25,9},{2,18},{10... | collective-permute-start | bytes 491528 | tf_op jit(solution)/shard_map/ppermute | solution.py:38
  22.9 6.3 %collective-permute-start = (bf16[48,2048]{1,0:T(8,128)(2,1)S(1)}, bf16[48,2048]{1,0:T(8,128)(2,1)S(1)}, u32[]{:S(2)}, u32[]{:S(2)}) collective-permute-start(bf16[48,2048]{1,0:T(8,128)(2,1)S(1)} %bitcast.34), channel_id=1, source_target_pairs={{0,16},{8,24},{16,0},{24,8},{1,17},{9,25},{17,1},{25,9},{2,18},{10... | collective-permute-start | bytes 589832 | tf_op jit(solution)/shard_map/ppermute | solution.py:38
  27.7 1.7 %collective-permute-start.3 = (bf16[80,2048]{1,0:T(8,128)(2,1)S(1)}, bf16[80,2048]{1,0:T(8,128)(2,1)S(1)}, u32[]{:S(2)}, u32[]{:S(2)}) collective-permute-start(bf16[80,2048]{1,0:T(8,128)(2,1)S(1)} %pad_maximum_fusion.2), channel_id=1, source_target_pairs={{0,8},{8,0},{16,24},{24,16},{1,9},{9,1},{17,25},{25,17},{2,10},{10... | collective-permute-start | bytes 983048 | tf_op jit(solution)/shard_map/ppermute | solution.py:38
  29.2 4.2 %collective-permute-start.1 = (bf16[96,2048]{1,0:T(8,128)(2,1)S(1)}, bf16[96,2048]{1,0:T(8,128)(2,1)S(1)}, u32[]{:S(2)}, u32[]{:S(2)}) collective-permute-start(bf16[96,2048]{1,0:T(8,128)(2,1)S(1)} %pad_maximum_fusion.1), channel_id=1, source_target_pairs={{0,8},{8,0},{16,24},{24,16},{1,9},{9,1},{17,25},{25,17},{2,10},{10... | collective-permute-start | bytes 1179656 | tf_op jit(solution)/shard_map/ppermute | solution.py:38
  36.9 1.6 %copy-start.2 = (f32[256,8]{0,1:T(8,128)S(1)}, f32[256,8]{0,1:T(8,128)}, u32[]{:S(2)}) copy-start(f32[256,8]{0,1:T(8,128)} %param.11) | copy-start | bytes 24580
  36.9 1.6 %copy-start.3 = (s32[256,1]{0,1:T(1,128)S(1)}, s32[256,1]{0,1:T(1,128)}, u32[]{:S(2)}) copy-start(s32[256,1]{0,1:T(1,128)} %param.12) | copy-start | bytes 3076
  36.9 2.0 %copy-start.1 = (bf16[256,256]{1,0:T(8,128)(2,1)S(1)}, bf16[256,256]{1,0:T(8,128)(2,1)}, u32[]{:S(2)}) copy-start(bf16[256,256]{1,0:T(8,128)(2,1)} %tokens_hbm.1) | copy-start | bytes 393220
  37.9 6.3 %collective-permute-start.6 = (bf16[80,1024]{1,0:T(8,128)(2,1)S(1)}, bf16[80,1024]{1,0:T(8,128)(2,1)S(1)}, u32[]{:S(2)}, u32[]{:S(2)}) collective-permute-start(bf16[80,1024]{1,0:T(8,128)(2,1)S(1)} %get-tuple-element.26), channel_id=1, source_target_pairs={{0,8},{8,0},{16,24},{24,16},{1,9},{9,1},{17,25},{25,17},{2,10},{10... | collective-permute-start | bytes 491528 | tf_op jit(solution)/shard_map/ppermute | solution.py:38
  39.1 5.9 %collective-permute-start.4 = (bf16[80,1024]{1,0:T(8,128)(2,1)S(1)}, bf16[80,1024]{1,0:T(8,128)(2,1)S(1)}, u32[]{:S(2)}, u32[]{:S(2)}) collective-permute-start(bf16[80,1024]{1,0:T(8,128)(2,1)S(1)} %get-tuple-element.22), channel_id=1, source_target_pairs={{0,8},{8,0},{16,24},{24,16},{1,9},{9,1},{17,25},{25,17},{2,10},{10... | collective-permute-start | bytes 491528 | tf_op jit(solution)/shard_map/ppermute | solution.py:38
  39.1 3.7 %collective-permute-start.8 = (f32[8,256]{1,0:T(8,128)S(1)}, f32[8,256]{1,0:T(8,128)S(1)}, u32[]{:S(2)}, u32[]{:S(2)}) collective-permute-start(f32[8,256]{1,0:T(8,128)S(1)} %fusion.4), channel_id=1, source_target_pairs={{0,8},{8,0},{16,24},{24,16},{1,9},{9,1},{17,25},{25,17},{2,10},{10... | collective-permute-start | bytes 24584 | tf_op jit(solution)/shard_map/ppermute | solution.py:38
  42.8 16.7 %collective-permute-start.9 = (f32[8,256]{1,0:T(8,128)S(1)}, f32[8,256]{1,0:T(8,128)S(1)}, u32[]{:S(2)}, u32[]{:S(2)}) collective-permute-start(f32[8,256]{1,0:T(8,128)S(1)} %add.36), channel_id=1, source_target_pairs={{0,16},{8,24},{16,0},{24,8},{1,17},{9,25},{17,1},{25,9},{2,18},{10... | collective-permute-start | bytes 24584 | tf_op jit(solution)/shard_map/ppermute | solution.py:38
  44.3 5.1 %collective-permute-start.7 = (bf16[40,1024]{1,0:T(8,128)(2,1)S(1)}, bf16[40,1024]{1,0:T(8,128)(2,1)S(1)}, u32[]{:S(2)}, u32[]{:S(2)}) collective-permute-start(bf16[40,1024]{1,0:T(8,128)(2,1)S(1)} %slice.61), channel_id=1, source_target_pairs={{0,16},{8,24},{16,0},{24,8},{1,17},{9,25},{17,1},{25,9},{2,18},{10... | collective-permute-start | bytes 245768 | tf_op jit(solution)/shard_map/ppermute | solution.py:38
  45.0 5.3 %collective-permute-start.5 = (bf16[40,1024]{1,0:T(8,128)(2,1)S(1)}, bf16[40,1024]{1,0:T(8,128)(2,1)S(1)}, u32[]{:S(2)}, u32[]{:S(2)}) collective-permute-start(bf16[40,1024]{1,0:T(8,128)(2,1)S(1)} %slice.62), channel_id=1, source_target_pairs={{0,16},{8,24},{16,0},{24,8},{1,17},{9,25},{17,1},{25,9},{2,18},{10... | collective-permute-start | bytes 245768 | tf_op jit(solution)/shard_map/ppermute | solution.py:38
  51.0 12.9 %all-to-all-start.1 = ((bf16[8,40,256]{2,1,0:T(8,128)(2,1)}), bf16[8,40,256]{2,1,0:T(8,128)(2,1)S(1)}, u32[]{:S(2)}, u32[]{:S(2)}) async-start(bf16[8,40,256]{2,1,0:T(8,128)(2,1)} %bitcast.30), calls=%async_computation.1 | async-start | bytes 327680 | tf_op jit(solution)/shard_map/all_to_all | solution.py:569

commit v4 on v3

--- a/solution.py
+++ b/solution.py
@@ -241,7 +241,9 @@
     slot = jnp.sum(jnp.where(hit, before, 0.0), axis=0, keepdims=True)
     place = iota((experts * capacity, count), 0) == route * capacity + slot.astype(jnp.int32)
     mask = place.astype(full).astype(half)
-    place_ref[...] = mask
+    own = lax.axis_index("expert")
+    turned = iota((experts * capacity, count), 0) == (route ^ own) * capacity + slot.astype(jnp.int32)
+    place_ref[...] = turned.astype(full).astype(half)
     copies[1].wait()
     gate = jnp.sum(jnp.where(hit, probs_ref[...], 0.0), axis=0, keepdims=True)
     row_gate = jnp.sum(jnp.where(place, gate, 0.0), axis=1, keepdims=True)
@@ -495,6 +497,40 @@
     )(near(gate_rows), near(up_rows), near(in_near))
 
 
+def pack_kernel(rows_ref, own_ref, odd_ref, even_ref):
+    own = lax.axis_index("expert")
+    width = own_ref.shape[1]
+    for step in range(rows_ref.shape[1] // width):
+        block = pl.ds(pl.multiple_of((own ^ step) * width, width), width)
+        target = own_ref if step == 0 else (odd_ref if step % 2 else even_ref).at[(step - 1) // 2]
+        target[...] = rows_ref[:, block]
+
+
+def pack(rows, experts):
+    capacity, width = rows.shape[0], rows.shape[1] // experts
+    near_spec = pl.BlockSpec(memory_space=pltpu.VMEM)
+    return pl.pallas_call(
+        pack_kernel,
+        in_specs=[near_spec],
+        out_specs=[near_spec] * 3,
+        out_shape=(
+            pltpu.VMEM((capacity, width), rows.dtype),
+            pltpu.VMEM((experts // 2, capacity, width), rows.dtype),
+            pltpu.VMEM((experts // 2 - 1, capacity, width), rows.dtype),
+        ),
+        compiler_params=pltpu.CompilerParams(vmem_limit_bytes=4 << 20),
+        cost_estimate=pl.CostEstimate(
+            flops=0, bytes_accessed=4 * rows.size, transcendentals=0
+        ),
+        name="pack",
+    )(near(rows))
+
+
+def across(value, distance):
+    size = lax.axis_size("expert")
+    return lax.ppermute(value, "expert", [(i, i ^ distance) for i in range(size)])
+
+
 def half_kernel(grad_ref, rows_ref, *refs):
     refs[-1][0, 0] = jnp.dot(
         grad_ref[...], rows_ref[...], preferred_element_type=jnp.float32
@@ -565,8 +601,12 @@
     summed = reduce_groups(summed, 2).astype(jnp.bfloat16)
     more = reduce_groups(more, 2).astype(jnp.bfloat16)
     going = jnp.concatenate([summed, more], axis=1)
-    going = going.reshape(capacity, experts, width).transpose(1, 0, 2)
-    returned = lax.all_to_all(going, "expert", split_axis=0, concat_axis=0, tiled=True)
+    own, odd, even = pack(going, experts)
+    neighbours = across(odd, 1)
+    returned = [jnp.stack([own, neighbours[0]])]
+    for step in range(1, experts // 2):
+        returned.append(across(jnp.stack([even[step - 1], neighbours[step]]), 2 * step))
+    returned = jnp.concatenate(returned, axis=0)
     weight_grad = half_weight_grad(0, gate_grad, row_tokens)
     weight_grad = half_weight_grad(1, up_grad, row_tokens, weight_grad)
 
@@ -577,7 +617,7 @@
     logit_grad = probs * (prob_grad - jnp.sum(probs * prob_grad, axis=0, keepdims=True))
     logit_grad = logit_grad.astype(jnp.bfloat16)
     router_grad = jnp.dot(logit_grad, tokens, preferred_element_type=jnp.float32)
-    for distance in distances()[::-1]:
+    for distance in distances():
         router_grad = router_grad + swap(router_grad, distance)
     router_term = lax.dot_general(
         logit_grad, router_weight, (((0,), (1,)), ((), ())), preferred_element_type=jnp.float32
@@ -596,7 +636,8 @@
     token_count, width = tokens.shape
     experts = router_probs.shape[1]
     capacity = (5 * token_count + 4 * experts - 1) // (4 * experts)
-    aligned = token_count == width and width % 128 == 0 and capacity % 8 == 0 and experts % 8 == 0
+    aligned = token_count == width and width % 128 == 0 and capacity % 8 == 0
+    aligned = aligned and experts % 8 == 0 and experts & (experts - 1) == 0
     if not aligned:
         return general_device(tokens, out_grad, expert_out, router_probs, *rest)
     return aligned_device(tokens, out_grad, expert_out, router_probs, *rest)

time: 65.1 us -> 70.1 us (1.077)
  waiting for transfers between devices: 8.95 us -> 12.9 us
  starting transfers between devices: 12.3 us -> 13.4 us
    ppermute x0 -> x4, waiting for transfers between devices: none -> 7.14 us  [across(): lax.ppermute(value, 'expert', [(i, i ^ distance) for i in range(size)])]
    ppermute x0 -> x4, starting transfers between devices: none -> 6.74 us  [across(): lax.ppermute(value, 'expert', [(i, i ^ distance) for i in range(size)])]
    all_to_all x1 -> x0, starting transfers between devices: 5.3 us -> none  [aligned_device(): lax.all_to_all(going, 'expert', split_axis=0, concat_axis=0, tiled=True)]
    all_to_all x1 -> x0, waiting for transfers between devices: 3.75 us -> none  [aligned_device(): lax.all_to_all(going, 'expert', split_axis=0, concat_axis=0, tiled=True)]
  transfers between devices with their start and end apart: 11 -> 14, of which waited for: 4 -> 6; matrix products, arithmetic and copies ran while one was open for 3% -> 1% of each run, Pallas kernels for 22% -> 21%
where the time goes in v4:
time: 70.1 us; the launch traced here: 69.9 us
  Pallas kernels  20.8 us (30%)
  blocking collectives  18.6 us (27%)
  starting transfers between devices  13.4 us (19%)
  waiting for transfers between devices  12.9 us (18%)
  matrix products  1.4 us (2%)
  other arithmetic  1 us (1%)
  between operations  0.89 us (1%)
  local copies, waits for them, and re-layouts  0.86 us (1%)
    all_to_all x1, blocking collectives, aligned_device(): lax.all_to_all(send, 'expert', split_axis=0, concat_axis=0, tiled=True)  18.6 us
    ppermute x4, waiting for transfers between devices, across(): lax.ppermute(value, 'expert', [(i, i ^ distance) for i in range(size)])  7.14 us
    ppermute x4, starting transfers between devices, across(): lax.ppermute(value, 'expert', [(i, i ^ distance) for i in range(size)])  6.74 us
    ppermute x10, starting transfers between devices, swap(): return lax.ppermute(value, 'dp', [(i, i ^ distance) for i in range(size)])  6.7 us
    pallas_call x2, Pallas kernels, half_weight_grad(): pl.pallas_call(half_kernel, grid=(hidden // block,), in_specs=[pl.BlockSp...  6.37 us
    ppermute x10, waiting for transfers between devices, swap(): return lax.ppermute(value, 'dp', [(i, i ^ distance) for i in range(size)])  5.79 us
    pallas_call x1, Pallas kernels, fetch(): pl.pallas_call(partial(fetch_kernel, pieces), in_specs=[pl.BlockSpec(memo...  4.08 us
    pallas_call x1, Pallas kernels, hidden_back(): pl.pallas_call(partial(hidden_back_kernel, width // 2), in_specs=[near_sp...  3.22 us
  transfers between devices with their start and end apart: 14, of which 6 were waited for; matrix products, arithmetic and copies ran while one was open for 1% of the time, Pallas kernels for 21%

profile of v4, /device:TPU:0, one launch (start us, length us, event | category | flops | bytes accessed | tf_op | source)
XLA Modules:
  0.0 69.9 jit_solution(1657568423276226983)
XLA Ops:
  0.6 2.0 %prelude.1 = (bf16[8,88,256]{2,1,0:T(8,128)(2,1)S(1)}, bf16[320,256]{1,0:T(8,128)(2,1)S(1)}, bf16[640,2048]{1,0:T(8,128)(2,1)S(1)}) custom-call(s32[1,256]{1,0:T(1,128)} %bitcast.37, f32[8,256]{1,0:T(8,128)} %bitcast.36, bf16[256,256]{1,0:T(8,128)(2,1)} %tokens_hbm.1, bf16[256,256]{1,0:T(8,128)(2,1)} %grads_hbm.1, bf16[256,256]{1,0:T(8,128)(2,1)} %expert_out_hbm.1, ...), custom_call_target="tpu_custom_call" | custom-call | tf_op jit(solution)/shard_map/prelude/pallas_call | solution.py:290
  2.7 18.6 %all_to_all.5.after_ref = bf16[8,88,256]{2,1,0:T(8,128)(2,1)S(1)} all-to-all(bf16[8,88,256]{2,1,0:T(8,128)(2,1)S(1)} %get-tuple-element.20), channel_id=1, replica_groups=mesh['dp'=4,'expert'=8] {'expert'}, dimensions={0} | all-to-all | bytes 720896 | tf_op jit(solution)/shard_map/all_to_all | solution.py:577
  21.3 1.6 %collective-permute-start.2 = (bf16[40,2048]{1,0:T(8,128)(2,1)S(1)}, bf16[40,2048]{1,0:T(8,128)(2,1)S(1)}, u32[]{:S(2)}, u32[]{:S(2)}) collective-permute-start(bf16[40,2048]{1,0:T(8,128)(2,1)S(1)} %bitcast.32), channel_id=1, source_target_pairs={{0,16},{8,24},{16,0},{24,8},{1,17},{9,25},{17,1},{25,9},{2,18},{10... | collective-permute-start | bytes 491528 | tf_op jit(solution)/shard_map/ppermute | solution.py:38
  22.9 0.6 collective-permute-start
  23.5 4.1 %fetch.1.in_ref = bf16[1,2,1280,2048]{3,2,1,0:T(8,128)(2,1)S(1)} custom-call(bf16[1,2,1280,2048]{3,2,1,0:T(8,128)(2,1)} %source_ref.1, bf16[8,88,256]{2,1,0:T(8,128)(2,1)S(1)} %all_to_all.5.after_ref), custom_call_target="tpu_custom_call" | custom-call | bytes 10485760 | tf_op jit(solution)/shard_map/fetch/pallas_call | solution.py:326
  27.7 1.4 %collective-permute-done = bf16[48,2048]{1,0:T(8,128)(2,1)S(1)} collective-permute-done((bf16[48,2048]{1,0:T(8,128)(2,1)S(1)}, bf16[48,2048]{1,0:T(8,128)(2,1)S(1)}, u32[]{:S(2)}, u32[]{:S(2)}) %collective-permute-start) | collective-permute-done | bytes 196640 | tf_op jit(solution)/shard_map/ppermute | solution.py:38
  29.4 2.5 %gate_pre.1 = (f32[1280,160]{1,0:T(8,128)S(1)}, bf16[640,2048]{1,0:T(8,128)(2,1)S(1)}) custom-call(bf16[160,2048]{1,0:T(8,128)(2,1)S(1)} %constant_dynamic-update-slice_fusion.rows_ref, bf16[1,2,1280,2048]{3,2,1,0:T(8,128)(2,1)S(1)} %fetch.1.in_ref, bf16[1,1280,2048]{2,1,0:T(8,128)(2,1)} %down_hbm.3), custom_call_target="tpu_custom_call" | custom-call | flops 838860800 | bytes 5242880 | tf_op jit(solution)/shard_map/gate_pre/pallas_call | solution.py:389
  31.9 1.5 %hidden_pre.1.up_pre_ref = f32[1280,160]{1,0:T(8,128)S(1)} custom-call(bf16[160,2048]{1,0:T(8,128)(2,1)S(1)} %constant_dynamic-update-slice_fusion.rows_ref, bf16[1,2,1280,2048]{3,2,1,0:T(8,128)(2,1)S(1)} %fetch.1.in_ref), custom_call_target="tpu_custom_call" | custom-call | flops 838860800 | bytes 5242880 | tf_op jit(solution)/shard_map/hidden_pre/pallas_call | solution.py:381
  33.7 0.5 copy-done.2
  34.2 0.2 copy-done.1
  34.4 0.2 fusion.4
  34.6 0.3 fusion.5
  34.9 3.2 %hidden_back.1 = (bf16[1280,160]{1,0:T(8,128)(2,1)S(1)}, bf16[1280,160]{1,0:T(8,128)(2,1)S(1)}, bf16[160,1280]{1,0:T(8,128)(2,1)S(1)}, bf16[160,1280]{1,0:T(8,12...) custom-call(bf16[160,2048]{1,0:T(8,128)(2,1)S(1)} %bitcast.26, ...), custom_call_target="tpu_custom_call" | custom-call | flops 1677721600 | bytes 10485760 | tf_op jit(solution)/shard_map/hidden_back/pallas_call | solution.py:458
  38.1 1.0 %rest_back.1 = (f32[80,1024]{1,0:T(8,128)S(1)}, bf16[80,1024]{1,0:T(8,128)(2,1)S(1)}) custom-call(bf16[160,1280]{1,0:T(8,128)(2,1)S(1)} %get-tuple-element.26.gate_rows_ref, bf16[160,1280]{1,0:T(8,128)(2,1)S(1)} %get-tuple-element.27.up_rows_ref, bf16[1,2,1280,2048]{3,2,1,0:T(8,128)(2,1)S(1)} %fetch.1.in_ref), custom_call_target="tpu_custom_call" | custom-call | flops 838860800 | bytes 5242880 | tf_op jit(solution)/shard_map/rest_back/pallas_call | solution.py:484
  39.1 0.5 collective-permute-start.6
  39.8 1.5 %collective-permute-start.12 = (f32[8,256]{1,0:T(8,128)S(1)}, f32[8,256]{1,0:T(8,128)S(1)}, u32[]{:S(2)}, u32[]{:S(2)}) collective-permute-start(f32[8,256]{1,0:T(8,128)S(1)} %fusion.4), channel_id=1, source_target_pairs={{0,16},{8,24},{16,0},{24,8},{1,17},{9,25},{17,1},{25,9},{2,18},{10... | collective-permute-start | bytes 24584 | tf_op jit(solution)/shard_map/ppermute | solution.py:38
  41.2 3.2 %weight_grad_half.2.refs_0_ = bf16[1,2,1280,2048]{3,2,1,0:T(8,128)(2,1)} custom-call(bf16[1280,160]{1,0:T(8,128)(2,1)S(1)} %get-tuple-element.34.grad_ref, bf16[160,2048]{1,0:T(8,128)(2,1)S(1)} %constant_dynamic-update-slice_fusion.rows_ref), custom_call_target="tpu_custom_call" | custom-call | flops 838860800 | bytes 5242880 | tf_op jit(solution)/shard_map/weight_grad_half/pallas_call | solution.py:545
  44.4 0.2 collective-permute-start.13
  44.6 3.2 %weight_grad_half.3 = bf16[1,2,1280,2048]{3,2,1,0:T(8,128)(2,1)} custom-call(bf16[1280,160]{1,0:T(8,128)(2,1)S(1)} %get-tuple-element.33.grad_ref, bf16[160,2048]{1,0:T(8,128)(2,1)S(1)} %constant_dynamic-update-slice_fusion.rows_ref, bf16[1,2,1280,2048]{3,2,1,0:T(8,128)(2,1)} %weight_grad_half.2.refs_0_), custom_call_target="tpu_custom_call", output_to_operand_aliasing={{}: (2, {})} | custom-call | flops 838860800 | bytes 5242880 | tf_op jit(solution)/shard_map/weight_grad_half/pallas_call | solution.py:545
  47.8 0.6 add_bitcast_fusion
  48.4 0.6 collective-permute-start.7
  49.1 1.5 %collective-permute-start.5 = (bf16[40,1024]{1,0:T(8,128)(2,1)S(1)}, bf16[40,1024]{1,0:T(8,128)(2,1)S(1)}, u32[]{:S(2)}, u32[]{:S(2)}) collective-permute-start(bf16[40,1024]{1,0:T(8,128)(2,1)S(1)} %slice.95), channel_id=1, source_target_pairs={{0,16},{8,24},{16,0},{24,8},{1,17},{9,25},{17,1},{25,9},{2,18},{10... | collective-permute-start | bytes 245768 | tf_op jit(solution)/shard_map/ppermute | solution.py:38
  50.6 3.2 %collective-permute-done.7 = bf16[40,1024]{1,0:T(8,128)(2,1)S(1)} collective-permute-done((bf16[40,1024]{1,0:T(8,128)(2,1)S(1)}, bf16[40,1024]{1,0:T(8,128)(2,1)S(1)}, u32[]{:S(2)}, u32[]{:S(2)}) %collective-permute-start.7) | collective-permute-done | bytes 81952 | tf_op jit(solution)/shard_map/ppermute | solution.py:38
  53.8 1.1 %collective-permute-done.5 = bf16[40,1024]{1,0:T(8,128)(2,1)S(1)} collective-permute-done((bf16[40,1024]{1,0:T(8,128)(2,1)S(1)}, bf16[40,1024]{1,0:T(8,128)(2,1)S(1)}, u32[]{:S(2)}, u32[]{:S(2)}) %collective-permute-start.5) | collective-permute-done | bytes 81952 | tf_op jit(solution)/shard_map/ppermute | solution.py:38
  55.0 2.3 %collective-permute-start.8 = (bf16[4,40,256]{2,1,0:T(8,128)(2,1)S(1)}, bf16[4,40,256]{2,1,0:T(8,128)(2,1)S(1)}, u32[]{:S(2)}, u32[]{:S(2)}) collective-permute-start(bf16[4,40,256]{2,1,0:T(8,128)(2,1)S(1)} %get-tuple-element.31), channel_id=1, source_target_pairs={{0,1},{1,0},{2,3},{3,2},{4,5},{5,4},{6,7},{7,6},{8,9},{9,8},{10,11... | collective-permute-start | bytes 245768 | tf_op jit(solution)/shard_map/ppermute | solution.py:531
  57.3 2.4 %collective-permute-done.8 = bf16[4,40,256]{2,1,0:T(8,128)(2,1)S(1)} collective-permute-done((bf16[4,40,256]{2,1,0:T(8,128)(2,1)S(1)}, bf16[4,40,256]{2,1,0:T(8,128)(2,1)S(1)}, u32[]{:S(2)}, u32[]{:S(2)}) %collective-permute-start.8) | collective-permute-done | bytes 81952 | tf_op jit(solution)/shard_map/ppermute | solution.py:531
  59.8 0.7 %collective-permute-start.9 = (bf16[2,40,256]{2,1,0:T(8,128)(2,1)S(1)}, bf16[2,40,256]{2,1,0:T(8,128)(2,1)S(1)}, u32[]{:S(2)}, u32[]{:S(2)}) collective-permute-start(bf16[2,40,256]{2,1,0:T(8,128)(2,1)S(1)} %pad_maximum_fusion.4), channel_id=1, source_target_pairs={{0,2},{1,3},{2,0},{3,1},{4,6},{5,7},{6,4},{7,5},{8,10},{9,11},{10,... | collective-permute-start | bytes 122888 | tf_op jit(solution)/shard_map/ppermute | solution.py:531
  60.5 2.6 %collective-permute-start.10 = (bf16[2,40,256]{2,1,0:T(8,128)(2,1)S(1)}, bf16[2,40,256]{2,1,0:T(8,128)(2,1)S(1)}, u32[]{:S(2)}, u32[]{:S(2)}) collective-permute-start(bf16[2,40,256]{2,1,0:T(8,128)(2,1)S(1)} %pad_maximum_fusion.5), channel_id=1, source_target_pairs={{0,4},{1,5},{2,6},{3,7},{4,0},{5,1},{6,2},{7,3},{8,12},{9,13},{10,... | collective-permute-start | bytes 122888 | tf_op jit(solution)/shard_map/ppermute | solution.py:531
  63.2 1.1 %collective-permute-start.11 = (bf16[2,40,256]{2,1,0:T(8,128)(2,1)S(1)}, bf16[2,40,256]{2,1,0:T(8,128)(2,1)S(1)}, u32[]{:S(2)}, u32[]{:S(2)}) collective-permute-start(bf16[2,40,256]{2,1,0:T(8,128)(2,1)S(1)} %pad_maximum_fusion.6), channel_id=1, source_target_pairs={{0,6},{1,7},{2,4},{3,5},{4,2},{5,3},{6,0},{7,1},{8,14},{9,15},{10,... | collective-permute-start | bytes 122888 | tf_op jit(solution)/shard_map/ppermute | solution.py:531
  64.2 1.2 %collective-permute-done.10 = bf16[2,40,256]{2,1,0:T(8,128)(2,1)S(1)} collective-permute-done((bf16[2,40,256]{2,1,0:T(8,128)(2,1)S(1)}, bf16[2,40,256]{2,1,0:T(8,128)(2,1)S(1)}, u32[]{:S(2)}, u32[]{:S(2)}) %collective-permute-start.10) | collective-permute-done | bytes 40992 | tf_op jit(solution)/shard_map/ppermute | solution.py:531
  65.5 3.5 %collective-permute-done.11 = bf16[2,40,256]{2,1,0:T(8,128)(2,1)S(1)} collective-permute-done((bf16[2,40,256]{2,1,0:T(8,128)(2,1)S(1)}, bf16[2,40,256]{2,1,0:T(8,128)(2,1)S(1)}, u32[]{:S(2)}, u32[]{:S(2)}) %collective-permute-start.11) | collective-permute-done | bytes 40992 | tf_op jit(solution)/shard_map/ppermute | solution.py:531
  69.0 0.9 %fusion = bf16[256,256]{1,0:T(8,128)(2,1)} fusion(f32[256,256]{1,0:T(8,128)S(1)} %fusion.5, bf16[320,256]{1,0:T(8,128)(2,1)S(1)} %get-tuple-element.19, bf16[320,256]{1,0:T(8,128)(2,1)S(1)} %bitcast.35), kind=kOutput, calls=%fused_computation.1 | convolution fusion | flops 42074112 | bytes 720896 | tf_op jit(solution)/shard_map/dot_general | solution.py:625
  (49 shorter events, 0.9 us)
Async XLA Ops:
  0.6 33.9 %copy-start = (bf16[256,8]{0,1:T(8,128)(2,1)S(1)}, bf16[256,8]{0,1:T(8,128)(2,1)}, u32[]{:S(2)}) copy-start(bf16[256,8]{0,1:T(8,128)(2,1)} %param.15) | copy-start | bytes 12292
  21.3 6.3 %collective-permute-start.2 = (bf16[40,2048]{1,0:T(8,128)(2,1)S(1)}, bf16[40,2048]{1,0:T(8,128)(2,1)S(1)}, u32[]{:S(2)}, u32[]{:S(2)}) collective-permute-start(bf16[40,2048]{1,0:T(8,128)(2,1)S(1)} %bitcast.32), channel_id=1, source_target_pairs={{0,16},{8,24},{16,0},{24,8},{1,17},{9,25},{17,1},{25,9},{2,18},{10... | collective-permute-start | bytes 491528 | tf_op jit(solution)/shard_map/ppermute | solution.py:38
  22.9 6.3 %collective-permute-start = (bf16[48,2048]{1,0:T(8,128)(2,1)S(1)}, bf16[48,2048]{1,0:T(8,128)(2,1)S(1)}, u32[]{:S(2)}, u32[]{:S(2)}) collective-permute-start(bf16[48,2048]{1,0:T(8,128)(2,1)S(1)} %bitcast.29), channel_id=1, source_target_pairs={{0,16},{8,24},{16,0},{24,8},{1,17},{9,25},{17,1},{25,9},{2,18},{10... | collective-permute-start | bytes 589832 | tf_op jit(solution)/shard_map/ppermute | solution.py:38
  27.7 1.7 %collective-permute-start.3 = (bf16[80,2048]{1,0:T(8,128)(2,1)S(1)}, bf16[80,2048]{1,0:T(8,128)(2,1)S(1)}, u32[]{:S(2)}, u32[]{:S(2)}) collective-permute-start(bf16[80,2048]{1,0:T(8,128)(2,1)S(1)} %pad_maximum_fusion.2), channel_id=1, source_target_pairs={{0,8},{8,0},{16,24},{24,16},{1,9},{9,1},{17,25},{25,17},{2,10},{10... | collective-permute-start | bytes 983048 | tf_op jit(solution)/shard_map/ppermute | solution.py:38
  29.2 4.3 %collective-permute-start.1 = (bf16[96,2048]{1,0:T(8,128)(2,1)S(1)}, bf16[96,2048]{1,0:T(8,128)(2,1)S(1)}, u32[]{:S(2)}, u32[]{:S(2)}) collective-permute-start(bf16[96,2048]{1,0:T(8,128)(2,1)S(1)} %pad_maximum_fusion.1), channel_id=1, source_target_pairs={{0,8},{8,0},{16,24},{24,16},{1,9},{9,1},{17,25},{25,17},{2,10},{10... | collective-permute-start | bytes 1179656 | tf_op jit(solution)/shard_map/ppermute | solution.py:38
  33.4 0.7 %copy-start.2 = (f32[256,8]{0,1:T(8,128)S(1)}, f32[256,8]{0,1:T(8,128)}, u32[]{:S(2)}) copy-start(f32[256,8]{0,1:T(8,128)} %param.11) | copy-start | bytes 24580
  33.5 0.7 copy-start.3
  33.5 0.9 %copy-start.1 = (bf16[256,256]{1,0:T(8,128)(2,1)S(1)}, bf16[256,256]{1,0:T(8,128)(2,1)}, u32[]{:S(2)}) copy-start(bf16[256,256]{1,0:T(8,128)(2,1)} %tokens_hbm.1) | copy-start | bytes 393220
  39.1 9.2 %collective-permute-start.6 = (bf16[80,1024]{1,0:T(8,128)(2,1)S(1)}, bf16[80,1024]{1,0:T(8,128)(2,1)S(1)}, u32[]{:S(2)}, u32[]{:S(2)}) collective-permute-start(bf16[80,1024]{1,0:T(8,128)(2,1)S(1)} %get-tuple-element.29), channel_id=1, source_target_pairs={{0,8},{8,0},{16,24},{24,16},{1,9},{9,1},{17,25},{25,17},{2,10},{10... | collective-permute-start | bytes 491528 | tf_op jit(solution)/shard_map/ppermute | solution.py:38
  39.7 9.4 %collective-permute-start.4 = (bf16[80,1024]{1,0:T(8,128)(2,1)S(1)}, bf16[80,1024]{1,0:T(8,128)(2,1)S(1)}, u32[]{:S(2)}, u32[]{:S(2)}) collective-permute-start(bf16[80,1024]{1,0:T(8,128)(2,1)S(1)} %get-tuple-element.25), channel_id=1, source_target_pairs={{0,8},{8,0},{16,24},{24,16},{1,9},{9,1},{17,25},{25,17},{2,10},{10... | collective-permute-start | bytes 491528 | tf_op jit(solution)/shard_map/ppermute | solution.py:38
  39.8 4.7 %collective-permute-start.12 = (f32[8,256]{1,0:T(8,128)S(1)}, f32[8,256]{1,0:T(8,128)S(1)}, u32[]{:S(2)}, u32[]{:S(2)}) collective-permute-start(f32[8,256]{1,0:T(8,128)S(1)} %fusion.4), channel_id=1, source_target_pairs={{0,16},{8,24},{16,0},{24,8},{1,17},{9,25},{17,1},{25,9},{2,18},{10... | collective-permute-start | bytes 24584 | tf_op jit(solution)/shard_map/ppermute | solution.py:38
  44.4 3.3 %collective-permute-start.13 = (f32[8,256]{1,0:T(8,128)S(1)}, f32[8,256]{1,0:T(8,128)S(1)}, u32[]{:S(2)}, u32[]{:S(2)}) collective-permute-start(f32[8,256]{1,0:T(8,128)S(1)} %add.36), channel_id=1, source_target_pairs={{0,8},{8,0},{16,24},{24,16},{1,9},{9,1},{17,25},{25,17},{2,10},{10... | collective-permute-start | bytes 24584 | tf_op jit(solution)/shard_map/ppermute | solution.py:38
  48.4 5.4 %collective-permute-start.7 = (bf16[40,1024]{1,0:T(8,128)(2,1)S(1)}, bf16[40,1024]{1,0:T(8,128)(2,1)S(1)}, u32[]{:S(2)}, u32[]{:S(2)}) collective-permute-start(bf16[40,1024]{1,0:T(8,128)(2,1)S(1)} %slice.94), channel_id=1, source_target_pairs={{0,16},{8,24},{16,0},{24,8},{1,17},{9,25},{17,1},{25,9},{2,18},{10... | collective-permute-start | bytes 245768 | tf_op jit(solution)/shard_map/ppermute | solution.py:38
  49.1 5.9 %collective-permute-start.5 = (bf16[40,1024]{1,0:T(8,128)(2,1)S(1)}, bf16[40,1024]{1,0:T(8,128)(2,1)S(1)}, u32[]{:S(2)}, u32[]{:S(2)}) collective-permute-start(bf16[40,1024]{1,0:T(8,128)(2,1)S(1)} %slice.95), channel_id=1, source_target_pairs={{0,16},{8,24},{16,0},{24,8},{1,17},{9,25},{17,1},{25,9},{2,18},{10... | collective-permute-start | bytes 245768 | tf_op jit(solution)/shard_map/ppermute | solution.py:38
  55.0 4.7 %collective-permute-start.8 = (bf16[4,40,256]{2,1,0:T(8,128)(2,1)S(1)}, bf16[4,40,256]{2,1,0:T(8,128)(2,1)S(1)}, u32[]{:S(2)}, u32[]{:S(2)}) collective-permute-start(bf16[4,40,256]{2,1,0:T(8,128)(2,1)S(1)} %get-tuple-element.31), channel_id=1, source_target_pairs={{0,1},{1,0},{2,3},{3,2},{4,5},{5,4},{6,7},{7,6},{8,9},{9,8},{10,11... | collective-permute-start | bytes 245768 | tf_op jit(solution)/shard_map/ppermute | solution.py:531
  59.8 4.5 %collective-permute-start.9 = (bf16[2,40,256]{2,1,0:T(8,128)(2,1)S(1)}, bf16[2,40,256]{2,1,0:T(8,128)(2,1)S(1)}, u32[]{:S(2)}, u32[]{:S(2)}) collective-permute-start(bf16[2,40,256]{2,1,0:T(8,128)(2,1)S(1)} %pad_maximum_fusion.4), channel_id=1, source_target_pairs={{0,2},{1,3},{2,0},{3,1},{4,6},{5,7},{6,4},{7,5},{8,10},{9,11},{10,... | collective-permute-start | bytes 122888 | tf_op jit(solution)/shard_map/ppermute | solution.py:531
  60.5 5.0 %collective-permute-start.10 = (bf16[2,40,256]{2,1,0:T(8,128)(2,1)S(1)}, bf16[2,40,256]{2,1,0:T(8,128)(2,1)S(1)}, u32[]{:S(2)}, u32[]{:S(2)}) collective-permute-start(bf16[2,40,256]{2,1,0:T(8,128)(2,1)S(1)} %pad_maximum_fusion.5), channel_id=1, source_target_pairs={{0,4},{1,5},{2,6},{3,7},{4,0},{5,1},{6,2},{7,3},{8,12},{9,13},{10,... | collective-permute-start | bytes 122888 | tf_op jit(solution)/shard_map/ppermute | solution.py:531
  63.2 5.8 %collective-permute-start.11 = (bf16[2,40,256]{2,1,0:T(8,128)(2,1)S(1)}, bf16[2,40,256]{2,1,0:T(8,128)(2,1)S(1)}, u32[]{:S(2)}, u32[]{:S(2)}) collective-permute-start(bf16[2,40,256]{2,1,0:T(8,128)(2,1)S(1)} %pad_maximum_fusion.6), channel_id=1, source_target_pairs={{0,6},{1,7},{2,4},{3,5},{4,2},{5,3},{6,0},{7,1},{8,14},{9,15},{10,... | collective-permute-start | bytes 122888 | tf_op jit(solution)/shard_map/ppermute | solution.py:531

commit v5 on v3

--- a/solution.py
+++ b/solution.py
@@ -218,11 +218,15 @@
         for number, (source, target) in enumerate(zip(sources, targets))
     ]
     pieces = sems.shape[0] - len(copies)
-    size = down_ref.shape[0] // pieces
+    half = down_ref.shape[0]
+    size = half // pieces
     for piece in range(pieces):
-        rows = pl.ds(piece * size, size)
         copies.append(
-            pltpu.make_async_copy(down_hbm.at[0, rows], down_ref.at[rows], sems.at[len(copies)])
+            pltpu.make_async_copy(
+                down_hbm.at[0, pl.ds(half + piece * size, size)],
+                down_ref.at[pl.ds(piece * size, size)],
+                sems.at[len(copies)],
+            )
         )
     for copy in copies:
         copy.start()
@@ -347,11 +351,10 @@
 
 def gate_pre_kernel(rows_ref, in_ref, down_hbm, out_ref, down_ref, sems):
     pieces = sems.shape[0]
-    half = down_ref.shape[0]
-    size = half // pieces
+    size = down_ref.shape[0] // pieces
     copies = [
         pltpu.make_async_copy(
-            down_hbm.at[0, pl.ds(half + piece * size, size)],
+            down_hbm.at[0, pl.ds(piece * size, size)],
             down_ref.at[pl.ds(piece * size, size)],
             sems.at[piece],
         )
@@ -535,7 +538,7 @@
     full_width = experts * width
     probs = router_probs.T
     route = expert_index.reshape(1, token_count)
-    send, mask, first_down = prelude(
+    send, mask, second_down = prelude(
         capacity, down_weight, route, probs, tokens, out_grad, expert_out
     )
     got = lax.all_to_all(send, "expert", split_axis=0, concat_axis=0, tiled=True)
@@ -550,7 +553,7 @@
     all_grads = gather_groups(all_grads, first)
     row_tokens = gather_groups(row_tokens, last)
     all_grads = gather_groups(all_grads, last).reshape(groups, capacity + 8, full_width)
-    gate_pre, second_down = hidden_pre(0, row_tokens, in_near, down_weight)
+    gate_pre, first_down = hidden_pre(0, row_tokens, in_near, down_weight)
     up_pre = hidden_pre(1, row_tokens, in_near)
     row_grads = all_grads[:, :capacity].reshape(groups * capacity, full_width)
     gate_dot = jnp.sum(got[:, 2 * capacity : 2 * capacity + 3].astype(jnp.float32), axis=(0, 1))
@@ -562,9 +565,7 @@
     more_kept, more_away = rest_back(gate_rows, up_rows, in_near)
     summed = kept + swap(away, 1).astype(jnp.float32)
     more = more_kept + swap(more_away, 1).astype(jnp.float32)
-    summed = reduce_groups(summed, 2).astype(jnp.bfloat16)
-    more = reduce_groups(more, 2).astype(jnp.bfloat16)
-    going = jnp.concatenate([summed, more], axis=1)
+    going = reduce_groups(jnp.concatenate([summed, more], axis=1), 2).astype(jnp.bfloat16)
     going = going.reshape(capacity, experts, width).transpose(1, 0, 2)
     returned = lax.all_to_all(going, "expert", split_axis=0, concat_axis=0, tiled=True)
     weight_grad = half_weight_grad(0, gate_grad, row_tokens)

time: 65.1 us -> 60.3 us (0.926)
  waiting for transfers between devices: 8.95 us -> 6.97 us
  starting transfers between devices: 12.3 us -> 10.4 us
  Pallas kernels: 20.8 us -> 20 us
    ppermute x10 -> x9, waiting for transfers between devices: 5.2 us -> 3.22 us  [swap(): return lax.ppermute(value, 'dp', [(i, i ^ distance) for i in range(size)])]
    ppermute x10 -> x9, starting transfers between devices: 6.99 us -> 5.03 us  [swap(): return lax.ppermute(value, 'dp', [(i, i ^ distance) for i in range(size)])]
    pallas_call x1, Pallas kernels: 2.53 us -> 1.72 us  [hidden_pre(): pl.pallas_call(gate_pre_kernel, in_specs=[near_spec] * 2 + [pl.BlockSpec(...]
  transfers between devices with their start and end apart: 11 -> 10, of which waited for: 4 -> 4; matrix products, arithmetic and copies ran while one was open for 3% -> 3% of each run, Pallas kernels for 22% -> 25%
where the time goes in v5:
time: 60.3 us; the launch traced here: 60 us
  Pallas kernels  20 us (33%)
  blocking collectives  18.6 us (31%)
  starting transfers between devices  10.4 us (17%)
  waiting for transfers between devices  6.97 us (12%)
  matrix products  1.39 us (2%)
  other arithmetic  0.98 us (2%)
  local copies, waits for them, and re-layouts  0.85 us (1%)
  between operations  0.85 us (1%)
    all_to_all x1, blocking collectives, aligned_device(): lax.all_to_all(send, 'expert', split_axis=0, concat_axis=0, tiled=True)  18.6 us
    pallas_call x2, Pallas kernels, half_weight_grad(): pl.pallas_call(half_kernel, grid=(hidden // block,), in_specs=[pl.BlockSp...  6.41 us
    all_to_all x1, starting transfers between devices, aligned_device(): lax.all_to_all(going, 'expert', split_axis=0, concat_axis=0, tiled=True)  5.34 us
    ppermute x9, starting transfers between devices, swap(): return lax.ppermute(value, 'dp', [(i, i ^ distance) for i in range(size)])  5.03 us
    pallas_call x1, Pallas kernels, fetch(): pl.pallas_call(partial(fetch_kernel, pieces), in_specs=[pl.BlockSpec(memo...  4.08 us
    all_to_all x1, waiting for transfers between devices, aligned_device(): lax.all_to_all(going, 'expert', split_axis=0, concat_axis=0, tiled=True)  3.75 us
    pallas_call x1, Pallas kernels, hidden_back(): pl.pallas_call(partial(hidden_back_kernel, width // 2), in_specs=[near_sp...  3.23 us
    ppermute x9, waiting for transfers between devices, swap(): return lax.ppermute(value, 'dp', [(i, i ^ distance) for i in range(size)])  3.22 us
  transfers between devices with their start and end apart: 10, of which 4 were waited for; matrix products, arithmetic and copies ran while one was open for 3% of the time, Pallas kernels for 25%

profile of v5, /device:TPU:0, one launch (start us, length us, event | category | flops | bytes accessed | tf_op | source)
XLA Modules:
  0.0 60.0 jit_solution(5371951840572252507)
XLA Ops:
  0.6 0.0 copy-start
  0.6 2.0 %prelude.1 = (bf16[8,88,256]{2,1,0:T(8,128)(2,1)S(1)}, bf16[320,256]{1,0:T(8,128)(2,1)S(1)}, bf16[640,2048]{1,0:T(8,128)(2,1)S(1)}) custom-call(s32[1,256]{1,0:T(1,128)} %bitcast.43, f32[8,256]{1,0:T(8,128)} %bitcast.42, bf16[256,256]{1,0:T(8,128)(2,1)} %tokens_hbm.1, bf16[256,256]{1,0:T(8,128)(2,1)} %grads_hbm.1, bf16[256,256]{1,0:T(8,128)(2,1)} %expert_out_hbm.1, ...), custom_call_target="tpu_custom_call" | custom-call | tf_op jit(solution)/shard_map/prelude/pallas_call | solution.py:292
  2.7 18.6 %all_to_all.10.after_ref = bf16[8,88,256]{2,1,0:T(8,128)(2,1)S(1)} all-to-all(bf16[8,88,256]{2,1,0:T(8,128)(2,1)S(1)} %get-tuple-element.17), channel_id=1, replica_groups=mesh['dp'=4,'expert'=8] {'expert'}, dimensions={0} | all-to-all | bytes 720896 | tf_op jit(solution)/shard_map/all_to_all | solution.py:544
  21.3 1.6 %collective-permute-start.2 = (bf16[40,2048]{1,0:T(8,128)(2,1)S(1)}, bf16[40,2048]{1,0:T(8,128)(2,1)S(1)}, u32[]{:S(2)}, u32[]{:S(2)}) collective-permute-start(bf16[40,2048]{1,0:T(8,128)(2,1)S(1)} %bitcast.37), channel_id=1, source_target_pairs={{0,16},{8,24},{16,0},{24,8},{1,17},{9,25},{17,1},{25,9},{2,18},{10... | collective-permute-start | bytes 491528 | tf_op jit(solution)/shard_map/ppermute | solution.py:38
  22.9 0.6 %collective-permute-start = (bf16[48,2048]{1,0:T(8,128)(2,1)S(1)}, bf16[48,2048]{1,0:T(8,128)(2,1)S(1)}, u32[]{:S(2)}, u32[]{:S(2)}) collective-permute-start(bf16[48,2048]{1,0:T(8,128)(2,1)S(1)} %bitcast.34), channel_id=1, source_target_pairs={{0,16},{8,24},{16,0},{24,8},{1,17},{9,25},{17,1},{25,9},{2,18},{10... | collective-permute-start | bytes 589832 | tf_op jit(solution)/shard_map/ppermute | solution.py:38
  23.5 4.1 %fetch.1.in_ref = bf16[1,2,1280,2048]{3,2,1,0:T(8,128)(2,1)S(1)} custom-call(bf16[1,2,1280,2048]{3,2,1,0:T(8,128)(2,1)} %source_ref.1, bf16[8,88,256]{2,1,0:T(8,128)(2,1)S(1)} %all_to_all.10.after_ref), custom_call_target="tpu_custom_call" | custom-call | bytes 10485760 | tf_op jit(solution)/shard_map/fetch/pallas_call | solution.py:328
  27.7 0.1 collective-permute-start.3
  27.7 1.4 %collective-permute-done = bf16[48,2048]{1,0:T(8,128)(2,1)S(1)} collective-permute-done((bf16[48,2048]{1,0:T(8,128)(2,1)S(1)}, bf16[48,2048]{1,0:T(8,128)(2,1)S(1)}, u32[]{:S(2)}, u32[]{:S(2)}) %collective-permute-start) | collective-permute-done | bytes 196640 | tf_op jit(solution)/shard_map/ppermute | solution.py:38
  29.2 0.1 collective-permute-start.1
  29.3 0.0 collective-permute-done.3
  29.4 1.7 %gate_pre.1 = (f32[1280,160]{1,0:T(8,128)S(1)}, bf16[640,2048]{1,0:T(8,128)(2,1)S(1)}) custom-call(bf16[160,2048]{1,0:T(8,128)(2,1)S(1)} %constant_dynamic-update-slice_fusion.rows_ref, bf16[1,2,1280,2048]{3,2,1,0:T(8,128)(2,1)S(1)} %fetch.1.in_ref, bf16[1,1280,2048]{2,1,0:T(8,128)(2,1)} %down_hbm.3), custom_call_target="tpu_custom_call" | custom-call | flops 838860800 | bytes 5242880 | tf_op jit(solution)/shard_map/gate_pre/pallas_call | solution.py:390
  31.1 1.5 %hidden_pre.1.up_pre_ref = f32[1280,160]{1,0:T(8,128)S(1)} custom-call(bf16[160,2048]{1,0:T(8,128)(2,1)S(1)} %constant_dynamic-update-slice_fusion.rows_ref, bf16[1,2,1280,2048]{3,2,1,0:T(8,128)(2,1)S(1)} %fetch.1.in_ref), custom_call_target="tpu_custom_call" | custom-call | flops 838860800 | bytes 5242880 | tf_op jit(solution)/shard_map/hidden_pre/pallas_call | solution.py:382
  32.7 0.1 pad_maximum_fusion
  32.8 0.1 slice.30
  32.8 3.2 %hidden_back.1 = (bf16[1280,160]{1,0:T(8,128)(2,1)S(1)}, bf16[1280,160]{1,0:T(8,128)(2,1)S(1)}, bf16[160,1280]{1,0:T(8,128)(2,1)S(1)}, bf16[160,1280]{1,0:T(8,12...) custom-call(bf16[160,2048]{1,0:T(8,128)(2,1)S(1)} %bitcast.31, ...), custom_call_target="tpu_custom_call" | custom-call | flops 1677721600 | bytes 10485760 | tf_op jit(solution)/shard_map/hidden_back/pallas_call | solution.py:459
  36.1 0.5 collective-permute-start.4
  36.6 1.0 %rest_back.1 = (f32[80,1024]{1,0:T(8,128)S(1)}, bf16[80,1024]{1,0:T(8,128)(2,1)S(1)}) custom-call(bf16[160,1280]{1,0:T(8,128)(2,1)S(1)} %get-tuple-element.23.gate_rows_ref, bf16[160,1280]{1,0:T(8,128)(2,1)S(1)} %get-tuple-element.24.up_rows_ref, bf16[1,2,1280,2048]{3,2,1,0:T(8,128)(2,1)S(1)} %fetch.1.in_ref), custom_call_target="tpu_custom_call" | custom-call | flops 838860800 | bytes 5242880 | tf_op jit(solution)/shard_map/rest_back/pallas_call | solution.py:485
  37.6 0.1 collective-permute-start.5
  37.8 0.1 multiply_reduce_fusion
  37.8 0.3 fusion.7
  38.2 0.9 %collective-permute-done.5 = bf16[80,1024]{1,0:T(8,128)(2,1)S(1)} collective-permute-done((bf16[80,1024]{1,0:T(8,128)(2,1)S(1)}, bf16[80,1024]{1,0:T(8,128)(2,1)S(1)}, u32[]{:S(2)}, u32[]{:S(2)}) %collective-permute-start.5) | collective-permute-done | bytes 163872 | tf_op jit(solution)/shard_map/ppermute | solution.py:38
  39.2 1.6 %collective-permute-start.6 = (bf16[40,2048]{1,0:T(8,128)(2,1)S(1)}, bf16[40,2048]{1,0:T(8,128)(2,1)S(1)}, u32[]{:S(2)}, u32[]{:S(2)}) collective-permute-start(bf16[40,2048]{1,0:T(8,128)(2,1)S(1)} %fusion.4), channel_id=1, source_target_pairs={{0,16},{8,24},{16,0},{24,8},{1,17},{9,25},{17,1},{25,9},{2,18},{10... | collective-permute-start | bytes 491528 | tf_op jit(solution)/shard_map/ppermute | solution.py:38
  40.7 0.2 fusion.6
  40.9 3.2 %weight_grad_half.2.refs_0_ = bf16[1,2,1280,2048]{3,2,1,0:T(8,128)(2,1)} custom-call(bf16[1280,160]{1,0:T(8,128)(2,1)S(1)} %get-tuple-element.28.grad_ref, bf16[160,2048]{1,0:T(8,128)(2,1)S(1)} %constant_dynamic-update-slice_fusion.rows_ref), custom_call_target="tpu_custom_call" | custom-call | flops 838860800 | bytes 5242880 | tf_op jit(solution)/shard_map/weight_grad_half/pallas_call | solution.py:512
  44.1 0.5 collective-permute-start.8
  44.6 0.8 %collective-permute-done.6 = bf16[40,2048]{1,0:T(8,128)(2,1)S(1)} collective-permute-done((bf16[40,2048]{1,0:T(8,128)(2,1)S(1)}, bf16[40,2048]{1,0:T(8,128)(2,1)S(1)}, u32[]{:S(2)}, u32[]{:S(2)}) %collective-permute-start.6) | collective-permute-done | bytes 163872 | tf_op jit(solution)/shard_map/ppermute | solution.py:38
  45.5 0.7 %copy.20 = bf16[5,8,8,256]{3,2,0,1:T(8,128)(2,1)} copy(bf16[5,8,8,256]{3,2,1,0:T(8,128)(2,1)S(1)} %bitcast.41) | data formatting | bytes 327680 | tf_op jit(solution)/shard_map/reshape | solution.py:569
  46.2 5.3 %all-to-all-start.1 = ((bf16[8,40,256]{2,1,0:T(8,128)(2,1)}), bf16[8,40,256]{2,1,0:T(8,128)(2,1)S(1)}, u32[]{:S(2)}, u32[]{:S(2)}) async-start(bf16[8,40,256]{2,1,0:T(8,128)(2,1)} %bitcast.30), calls=%async_computation.1 | async-start | bytes 327680 | tf_op jit(solution)/shard_map/all_to_all | solution.py:570
  51.5 3.2 %weight_grad_half.3 = bf16[1,2,1280,2048]{3,2,1,0:T(8,128)(2,1)} custom-call(bf16[1280,160]{1,0:T(8,128)(2,1)S(1)} %get-tuple-element.27.grad_ref, bf16[160,2048]{1,0:T(8,128)(2,1)S(1)} %constant_dynamic-update-slice_fusion.rows_ref, bf16[1,2,1280,2048]{3,2,1,0:T(8,128)(2,1)} %weight_grad_half.2.refs_0_), custom_call_target="tpu_custom_call", output_to_operand_aliasing={{}: (2, {})} | custom-call | flops 838860800 | bytes 5242880 | tf_op jit(solution)/shard_map/weight_grad_half/pallas_call | solution.py:512
  54.7 0.6 %add_bitcast_fusion = f32[256,8]{0,1:T(8,128)} fusion(f32[8,256]{1,0:T(8,128)S(1)} %add.32, f32[8,256]{1,0:T(8,128)S(1)} %collective-permute-done.8), kind=kLoop, calls=%fused_computation.21 | loop fusion | flops 2048 | bytes 24576 | tf_op jit(solution)/shard_map/transpose | solution.py:593
  55.3 3.8 %all-to-all-done.1 = bf16[8,40,256]{2,1,0:T(8,128)(2,1)S(1)} async-done(((bf16[8,40,256]{2,1,0:T(8,128)(2,1)}), bf16[8,40,256]{2,1,0:T(8,128)(2,1)S(1)}, u32[]{:S(2)}, u32[]{:S(2)}) %all-to-all-start.1) | async-done | bytes 163872 | tf_op jit(solution)/shard_map/all_to_all | solution.py:570
  59.1 0.9 %fusion = bf16[256,256]{1,0:T(8,128)(2,1)} fusion(f32[256,256]{1,0:T(8,128)S(1)} %fusion.7, bf16[320,256]{1,0:T(8,128)(2,1)S(1)} %get-tuple-element.16, bf16[320,256]{1,0:T(8,128)(2,1)S(1)} %bitcast.40), kind=kOutput, calls=%fused_computation.1 | convolution fusion | flops 42074112 | bytes 720896 | tf_op jit(solution)/shard_map/dot_general | solution.py:586
  (30 shorter events, 0.4 us)
Async XLA Ops:
  0.6 37.2 %copy-start = (bf16[256,8]{0,1:T(8,128)(2,1)S(1)}, bf16[256,8]{0,1:T(8,128)(2,1)}, u32[]{:S(2)}) copy-start(bf16[256,8]{0,1:T(8,128)(2,1)} %param.15) | copy-start | bytes 12292
  21.3 6.3 %collective-permute-start.2 = (bf16[40,2048]{1,0:T(8,128)(2,1)S(1)}, bf16[40,2048]{1,0:T(8,128)(2,1)S(1)}, u32[]{:S(2)}, u32[]{:S(2)}) collective-permute-start(bf16[40,2048]{1,0:T(8,128)(2,1)S(1)} %bitcast.37), channel_id=1, source_target_pairs={{0,16},{8,24},{16,0},{24,8},{1,17},{9,25},{17,1},{25,9},{2,18},{10... | collective-permute-start | bytes 491528 | tf_op jit(solution)/shard_map/ppermute | solution.py:38
  22.9 6.3 %collective-permute-start = (bf16[48,2048]{1,0:T(8,128)(2,1)S(1)}, bf16[48,2048]{1,0:T(8,128)(2,1)S(1)}, u32[]{:S(2)}, u32[]{:S(2)}) collective-permute-start(bf16[48,2048]{1,0:T(8,128)(2,1)S(1)} %bitcast.34), channel_id=1, source_target_pairs={{0,16},{8,24},{16,0},{24,8},{1,17},{9,25},{17,1},{25,9},{2,18},{10... | collective-permute-start | bytes 589832 | tf_op jit(solution)/shard_map/ppermute | solution.py:38
  27.7 1.7 %collective-permute-start.3 = (bf16[80,2048]{1,0:T(8,128)(2,1)S(1)}, bf16[80,2048]{1,0:T(8,128)(2,1)S(1)}, u32[]{:S(2)}, u32[]{:S(2)}) collective-permute-start(bf16[80,2048]{1,0:T(8,128)(2,1)S(1)} %pad_maximum_fusion.3), channel_id=1, source_target_pairs={{0,8},{8,0},{16,24},{24,16},{1,9},{9,1},{17,25},{25,17},{2,10},{10... | collective-permute-start | bytes 983048 | tf_op jit(solution)/shard_map/ppermute | solution.py:38
  29.2 3.4 %collective-permute-start.1 = (bf16[96,2048]{1,0:T(8,128)(2,1)S(1)}, bf16[96,2048]{1,0:T(8,128)(2,1)S(1)}, u32[]{:S(2)}, u32[]{:S(2)}) collective-permute-start(bf16[96,2048]{1,0:T(8,128)(2,1)S(1)} %pad_maximum_fusion.1), channel_id=1, source_target_pairs={{0,8},{8,0},{16,24},{24,16},{1,9},{9,1},{17,25},{25,17},{2,10},{10... | collective-permute-start | bytes 1179656 | tf_op jit(solution)/shard_map/ppermute | solution.py:38
  36.1 2.1 %collective-permute-start.4 = (bf16[80,1024]{1,0:T(8,128)(2,1)S(1)}, bf16[80,1024]{1,0:T(8,128)(2,1)S(1)}, u32[]{:S(2)}, u32[]{:S(2)}) collective-permute-start(bf16[80,1024]{1,0:T(8,128)(2,1)S(1)} %get-tuple-element.22), channel_id=1, source_target_pairs={{0,8},{8,0},{16,24},{24,16},{1,9},{9,1},{17,25},{25,17},{2,10},{10... | collective-permute-start | bytes 491528 | tf_op jit(solution)/shard_map/ppermute | solution.py:38
  36.6 1.2 %copy-start.2 = (f32[256,8]{0,1:T(8,128)S(1)}, f32[256,8]{0,1:T(8,128)}, u32[]{:S(2)}) copy-start(f32[256,8]{0,1:T(8,128)} %param.11) | copy-start | bytes 24580
  36.6 1.2 %copy-start.3 = (s32[256,1]{0,1:T(1,128)S(1)}, s32[256,1]{0,1:T(1,128)}, u32[]{:S(2)}) copy-start(s32[256,1]{0,1:T(1,128)} %param.12) | copy-start | bytes 3076
  37.6 3.1 %copy-start.1 = (bf16[256,256]{1,0:T(8,128)(2,1)S(1)}, bf16[256,256]{1,0:T(8,128)(2,1)}, u32[]{:S(2)}) copy-start(bf16[256,256]{1,0:T(8,128)(2,1)} %tokens_hbm.1) | copy-start | bytes 393220
  37.6 1.5 %collective-permute-start.5 = (bf16[80,1024]{1,0:T(8,128)(2,1)S(1)}, bf16[80,1024]{1,0:T(8,128)(2,1)S(1)}, u32[]{:S(2)}, u32[]{:S(2)}) collective-permute-start(bf16[80,1024]{1,0:T(8,128)(2,1)S(1)} %get-tuple-element.26), channel_id=1, source_target_pairs={{0,8},{8,0},{16,24},{24,16},{1,9},{9,1},{17,25},{25,17},{2,10},{10... | collective-permute-start | bytes 491528 | tf_op jit(solution)/shard_map/ppermute | solution.py:38
  39.2 6.3 %collective-permute-start.6 = (bf16[40,2048]{1,0:T(8,128)(2,1)S(1)}, bf16[40,2048]{1,0:T(8,128)(2,1)S(1)}, u32[]{:S(2)}, u32[]{:S(2)}) collective-permute-start(bf16[40,2048]{1,0:T(8,128)(2,1)S(1)} %fusion.4), channel_id=1, source_target_pairs={{0,16},{8,24},{16,0},{24,8},{1,17},{9,25},{17,1},{25,9},{2,18},{10... | collective-permute-start | bytes 491528 | tf_op jit(solution)/shard_map/ppermute | solution.py:38
  40.9 3.2 %collective-permute-start.7 = (f32[8,256]{1,0:T(8,128)S(1)}, f32[8,256]{1,0:T(8,128)S(1)}, u32[]{:S(2)}, u32[]{:S(2)}) collective-permute-start(f32[8,256]{1,0:T(8,128)S(1)} %fusion.6), channel_id=1, source_target_pairs={{0,8},{8,0},{16,24},{24,16},{1,9},{9,1},{17,25},{25,17},{2,10},{10... | collective-permute-start | bytes 24584 | tf_op jit(solution)/shard_map/ppermute | solution.py:38
  44.1 10.6 %collective-permute-start.8 = (f32[8,256]{1,0:T(8,128)S(1)}, f32[8,256]{1,0:T(8,128)S(1)}, u32[]{:S(2)}, u32[]{:S(2)}) collective-permute-start(f32[8,256]{1,0:T(8,128)S(1)} %add.32), channel_id=1, source_target_pairs={{0,16},{8,24},{16,0},{24,8},{1,17},{9,25},{17,1},{25,9},{2,18},{10... | collective-permute-start | bytes 24584 | tf_op jit(solution)/shard_map/ppermute | solution.py:38
  46.2 12.9 %all-to-all-start.1 = ((bf16[8,40,256]{2,1,0:T(8,128)(2,1)}), bf16[8,40,256]{2,1,0:T(8,128)(2,1)S(1)}, u32[]{:S(2)}, u32[]{:S(2)}) async-start(bf16[8,40,256]{2,1,0:T(8,128)(2,1)} %bitcast.30), calls=%async_computation.1 | async-start | bytes 327680 | tf_op jit(solution)/shard_map/all_to_all | solution.py:570

commit v6 on v5

--- a/solution.py
+++ b/solution.py
@@ -339,58 +339,72 @@
     )(far(weight), after)
 
 
-def pre_activation(which, rows_ref, in_ref, out_ref):
+def pre_activation(which, rows, in_ref, part):
+    return lax.dot_general(
+        in_ref[0, which, part], rows, contract_last, preferred_element_type=jnp.float32
+    )
+
+
+def up_pre_kernel(rows_ref, in_ref, gate_pre_ref, gate_factor_ref, up_factor_ref):
     rows = rows_ref[...]
-    size = in_ref.shape[2] // 2
-    for start in (0, size):
+    size = in_ref.shape[2] // 4
+    scale, cubic = math.sqrt(2 / math.pi), 0.044715
+    for start in range(0, 4 * size, size):
         part = slice(start, start + size)
-        out_ref[part] = lax.dot_general(
-            in_ref[0, which, part], rows, contract_last, preferred_element_type=jnp.float32
-        )
+        value = gate_pre_ref[part]
+        square = value * value
+        bend = jnp.tanh(scale * (value + cubic * (square * value)))
+        cdf = 0.5 * (1.0 + bend)
+        slope = cdf + (0.5 * scale) * value * (1.0 - bend * bend) * (1.0 + 3 * cubic * square)
+        up_factor_ref[part] = value * cdf
+        gate_factor_ref[part] = slope * pre_activation(1, rows, in_ref, part)
 
 
 def gate_pre_kernel(rows_ref, in_ref, down_hbm, out_ref, down_ref, sems):
     pieces = sems.shape[0]
-    size = down_ref.shape[0] // pieces
+    step = down_ref.shape[0] // pieces
     copies = [
         pltpu.make_async_copy(
-            down_hbm.at[0, pl.ds(piece * size, size)],
-            down_ref.at[pl.ds(piece * size, size)],
+            down_hbm.at[0, pl.ds(piece * step, step)],
+            down_ref.at[pl.ds(piece * step, step)],
             sems.at[piece],
         )
         for piece in range(pieces)
     ]
     for copy in copies:
         copy.start()
-    pre_activation(0, rows_ref, in_ref, out_ref)
+    rows = rows_ref[...]
+    size = in_ref.shape[2] // 2
+    for start in (0, size):
+        part = slice(start, start + size)
+        out_ref[part] = pre_activation(0, rows, in_ref, part)
     for copy in copies:
         copy.wait()
 
 
-def hidden_pre(which, rows, in_near, down_weight=None):
+def hidden_pre(rows, in_near, down_weight=None, gate_pre=None):
     count, width = rows.shape
     hidden = in_near.shape[2]
     near_spec = pl.BlockSpec(memory_space=pltpu.VMEM)
     out = pltpu.VMEM((hidden, count), jnp.float32)
     settings = dict(
+        out_specs=[near_spec] * 2,
         compiler_params=pltpu.CompilerParams(vmem_limit_bytes=8 << 20),
         cost_estimate=pl.CostEstimate(
             flops=2 * count * hidden * width, bytes_accessed=2 * hidden * width, transcendentals=0
         ),
     )
-    if down_weight is None:
+    if gate_pre is not None:
         return pl.pallas_call(
-            partial(pre_activation, which),
-            in_specs=[near_spec] * 2,
-            out_specs=near_spec,
-            out_shape=out,
-            name="hidden_pre",
+            up_pre_kernel,
+            in_specs=[near_spec] * 3,
+            out_shape=(out, out),
+            name="up_pre",
             **settings,
-        )(rows, near(in_near))
+        )(rows, near(in_near), near(gate_pre))
     return pl.pallas_call(
         gate_pre_kernel,
         in_specs=[near_spec] * 2 + [pl.BlockSpec(memory_space=pl.ANY)],
-        out_specs=[near_spec] * 2,
         out_shape=(out, pltpu.VMEM((hidden // 2, width), down_weight.dtype)),
         scratch_shapes=[pltpu.SemaphoreType.DMA((4,))],
         name="gate_pre",
@@ -415,8 +429,8 @@
 def hidden_back_kernel(
     block,
     rows_ref,
-    gate_pre_ref,
-    up_pre_ref,
+    gate_factor_ref,
+    up_factor_ref,
     in_ref,
     down_ref,
     other_ref,
@@ -429,19 +443,13 @@
 ):
     size = down_ref.shape[0]
     rows = rows_ref[...]
-    scale, cubic = math.sqrt(2 / math.pi), 0.044715
     for number, weight_ref in enumerate((down_ref, other_ref)):
         part = slice(number * size, (number + 1) * size)
         grad = lax.dot_general(
             weight_ref[...], rows, contract_last, preferred_element_type=jnp.float32
         )
-        value, up = gate_pre_ref[part], up_pre_ref[part]
-        square = value * value
-        bend = jnp.tanh(scale * (value + cubic * (square * value)))
-        cdf = 0.5 * (1.0 + bend)
-        slope = cdf + (0.5 * scale) * value * (1.0 - bend * bend) * (1.0 + 3 * cubic * square)
-        gate_ref[part] = (grad * up * slope).astype(jnp.bfloat16)
-        up_ref[part] = (grad * (value * cdf)).astype(jnp.bfloat16)
+        gate_ref[part] = (grad * gate_factor_ref[part]).astype(jnp.bfloat16)
+        up_ref[part] = (grad * up_factor_ref[part]).astype(jnp.bfloat16)
     gate_rows_ref[...] = gate_ref[...].T
     up_rows_ref[...] = up_ref[...].T
     input_grads((gate_rows_ref[...], up_rows_ref[...]), in_ref, 0, kept_ref, away_ref, block)
@@ -452,7 +460,7 @@
     input_grads((gate_rows_ref[...], up_rows_ref[...]), in_ref, first, kept_ref, away_ref, block)
 
 
-def hidden_back(rows, gate_pre, up_pre, in_near, downs):
+def hidden_back(rows, gate_factor, up_factor, in_near, downs):
     count, width = rows.shape
     hidden = in_near.shape[2]
     near_spec = pl.BlockSpec(memory_space=pltpu.VMEM)
@@ -475,7 +483,7 @@
             transcendentals=count * hidden,
         ),
         name="hidden_back",
-    )(rows, near(gate_pre), near(up_pre), near(in_near), *map(near, downs))
+    )(rows, near(gate_factor), near(up_factor), near(in_near), *map(near, downs))
 
 
 def rest_back(gate_rows, up_rows, in_near):
@@ -553,14 +561,14 @@
     all_grads = gather_groups(all_grads, first)
     row_tokens = gather_groups(row_tokens, last)
     all_grads = gather_groups(all_grads, last).reshape(groups, capacity + 8, full_width)
-    gate_pre, first_down = hidden_pre(0, row_tokens, in_near, down_weight)
-    up_pre = hidden_pre(1, row_tokens, in_near)
+    gate_pre, first_down = hidden_pre(row_tokens, in_near, down_weight)
+    gate_factor, up_factor = hidden_pre(row_tokens, in_near, gate_pre=gate_pre)
     row_grads = all_grads[:, :capacity].reshape(groups * capacity, full_width)
     gate_dot = jnp.sum(got[:, 2 * capacity : 2 * capacity + 3].astype(jnp.float32), axis=(0, 1))
     counts = jnp.sum(all_grads[:, capacity + 3, :experts].astype(jnp.float32), axis=0)
 
     gate_grad, up_grad, gate_rows, up_rows, kept, away = hidden_back(
-        row_grads, gate_pre, up_pre, in_near, (first_down, second_down)
+        row_grads, gate_factor, up_factor, in_near, (first_down, second_down)
     )
     more_kept, more_away = rest_back(gate_rows, up_rows, in_near)
     summed = kept + swap(away, 1).astype(jnp.float32)

time: 60.3 us -> 60.1 us (level)
    pallas_call x1, Pallas kernels: 3.23 us -> 2.58 us  [hidden_back(): pl.pallas_call(partial(hidden_back_kernel, width // 2), in_specs=[near_sp...]
where the time goes in v6:
time: 60.1 us; the launch traced here: 59.8 us
  Pallas kernels  19.8 us (33%)
  blocking collectives  18.6 us (31%)
  starting transfers between devices  10.3 us (17%)
  waiting for transfers between devices  6.98 us (12%)
  matrix products  1.39 us (2%)
  other arithmetic  0.98 us (2%)
  between operations  0.86 us (1%)
  local copies, waits for them, and re-layouts  0.84 us (1%)
    all_to_all x1, blocking collectives, aligned_device(): lax.all_to_all(send, 'expert', split_axis=0, concat_axis=0, tiled=True)  18.6 us
    pallas_call x2, Pallas kernels, half_weight_grad(): pl.pallas_call(half_kernel, grid=(hidden // block,), in_specs=[pl.BlockSp...  6.41 us
    all_to_all x1, starting transfers between devices, aligned_device(): lax.all_to_all(going, 'expert', split_axis=0, concat_axis=0, tiled=True)  5.31 us
    ppermute x9, starting transfers between devices, swap(): return lax.ppermute(value, 'dp', [(i, i ^ distance) for i in range(size)])  5.03 us
    pallas_call x1, Pallas kernels, fetch(): pl.pallas_call(partial(fetch_kernel, pieces), in_specs=[pl.BlockSpec(memo...  4.08 us
    all_to_all x1, waiting for transfers between devices, aligned_device(): lax.all_to_all(going, 'expert', split_axis=0, concat_axis=0, tiled=True)  3.75 us
    ppermute x9, waiting for transfers between devices, swap(): return lax.ppermute(value, 'dp', [(i, i ^ distance) for i in range(size)])  3.23 us
    pallas_call x1, Pallas kernels, hidden_back(): pl.pallas_call(partial(hidden_back_kernel, width // 2), in_specs=[near_sp...  2.58 us
  transfers between devices with their start and end apart: 10, of which 4 were waited for; matrix products, arithmetic and copies ran while one was open for 3% of the time, Pallas kernels for 25%

profile of v6, /device:TPU:0, one launch (start us, length us, event | category | flops | bytes accessed | tf_op | source)
XLA Modules:
  0.0 59.8 jit_solution(8250809824400031743)
XLA Ops:
  0.6 0.0 copy-start
  0.6 2.0 %prelude.1 = (bf16[8,88,256]{2,1,0:T(8,128)(2,1)S(1)}, bf16[320,256]{1,0:T(8,128)(2,1)S(1)}, bf16[640,2048]{1,0:T(8,128)(2,1)S(1)}) custom-call(s32[1,256]{1,0:T(1,128)} %bitcast.43, f32[8,256]{1,0:T(8,128)} %bitcast.42, bf16[256,256]{1,0:T(8,128)(2,1)} %tokens_hbm.1, bf16[256,256]{1,0:T(8,128)(2,1)} %grads_hbm.1, bf16[256,256]{1,0:T(8,128)(2,1)} %expert_out_hbm.1, ...), custom_call_target="tpu_custom_call" | custom-call | tf_op jit(solution)/shard_map/prelude/pallas_call | solution.py:292
  2.7 18.6 %all_to_all.10.after_ref = bf16[8,88,256]{2,1,0:T(8,128)(2,1)S(1)} all-to-all(bf16[8,88,256]{2,1,0:T(8,128)(2,1)S(1)} %get-tuple-element.19), channel_id=1, replica_groups=mesh['dp'=4,'expert'=8] {'expert'}, dimensions={0} | all-to-all | bytes 720896 | tf_op jit(solution)/shard_map/all_to_all | solution.py:552
  21.3 1.6 %collective-permute-start.2 = (bf16[40,2048]{1,0:T(8,128)(2,1)S(1)}, bf16[40,2048]{1,0:T(8,128)(2,1)S(1)}, u32[]{:S(2)}, u32[]{:S(2)}) collective-permute-start(bf16[40,2048]{1,0:T(8,128)(2,1)S(1)} %bitcast.37), channel_id=1, source_target_pairs={{0,16},{8,24},{16,0},{24,8},{1,17},{9,25},{17,1},{25,9},{2,18},{10... | collective-permute-start | bytes 491528 | tf_op jit(solution)/shard_map/ppermute | solution.py:38
  22.9 0.6 %collective-permute-start = (bf16[48,2048]{1,0:T(8,128)(2,1)S(1)}, bf16[48,2048]{1,0:T(8,128)(2,1)S(1)}, u32[]{:S(2)}, u32[]{:S(2)}) collective-permute-start(bf16[48,2048]{1,0:T(8,128)(2,1)S(1)} %bitcast.34), channel_id=1, source_target_pairs={{0,16},{8,24},{16,0},{24,8},{1,17},{9,25},{17,1},{25,9},{2,18},{10... | collective-permute-start | bytes 589832 | tf_op jit(solution)/shard_map/ppermute | solution.py:38
  23.5 4.1 %fetch.1.in_ref = bf16[1,2,1280,2048]{3,2,1,0:T(8,128)(2,1)S(1)} custom-call(bf16[1,2,1280,2048]{3,2,1,0:T(8,128)(2,1)} %source_ref.1, bf16[8,88,256]{2,1,0:T(8,128)(2,1)S(1)} %all_to_all.10.after_ref), custom_call_target="tpu_custom_call" | custom-call | bytes 10485760 | tf_op jit(solution)/shard_map/fetch/pallas_call | solution.py:328
  27.7 0.1 collective-permute-start.3
  27.7 1.4 %collective-permute-done = bf16[48,2048]{1,0:T(8,128)(2,1)S(1)} collective-permute-done((bf16[48,2048]{1,0:T(8,128)(2,1)S(1)}, bf16[48,2048]{1,0:T(8,128)(2,1)S(1)}, u32[]{:S(2)}, u32[]{:S(2)}) %collective-permute-start) | collective-permute-done | bytes 196640 | tf_op jit(solution)/shard_map/ppermute | solution.py:38
  29.2 0.1 collective-permute-start.1
  29.3 0.0 collective-permute-done.3
  29.4 1.7 %gate_pre.1 = (f32[1280,160]{1,0:T(8,128)S(1)}, bf16[640,2048]{1,0:T(8,128)(2,1)S(1)}) custom-call(bf16[160,2048]{1,0:T(8,128)(2,1)S(1)} %constant_dynamic-update-slice_fusion.rows_ref, bf16[1,2,1280,2048]{3,2,1,0:T(8,128)(2,1)S(1)} %fetch.1.in_ref, bf16[1,1280,2048]{2,1,0:T(8,128)(2,1)} %down_hbm.3), custom_call_target="tpu_custom_call" | custom-call | flops 838860800 | bytes 5242880 | tf_op jit(solution)/shard_map/gate_pre/pallas_call | solution.py:405
  31.1 2.0 %up_pre.1 = (f32[1280,160]{1,0:T(8,128)S(1)}, f32[1280,160]{1,0:T(8,128)S(1)}) custom-call(bf16[160,2048]{1,0:T(8,128)(2,1)S(1)} %constant_dynamic-update-slice_fusion.rows_ref, bf16[1,2,1280,2048]{3,2,1,0:T(8,128)(2,1)S(1)} %fetch.1.in_ref, f32[1280,160]{1,0:T(8,128)S(1)} %get-tuple-element.20.gate_pre_ref), custom_call_target="tpu_custom_call" | custom-call | flops 838860800 | bytes 5242880 | tf_op jit(solution)/shard_map/up_pre/pallas_call | solution.py:398
  33.1 0.1 pad_maximum_fusion
  33.3 2.6 %hidden_back.1 = (bf16[1280,160]{1,0:T(8,128)(2,1)S(1)}, bf16[1280,160]{1,0:T(8,128)(2,1)S(1)}, bf16[160,1280]{1,0:T(8,128)(2,1)S(1)}, bf16[160,1280]{1,0:T(8,12...) custom-call(bf16[160,2048]{1,0:T(8,128)(2,1)S(1)} %bitcast.31, ...), custom_call_target="tpu_custom_call" | custom-call | flops 1677721600 | bytes 10485760 | tf_op jit(solution)/shard_map/hidden_back/pallas_call | solution.py:467
  35.9 0.5 collective-permute-start.4
  36.4 1.0 %rest_back.1 = (f32[80,1024]{1,0:T(8,128)S(1)}, bf16[80,1024]{1,0:T(8,128)(2,1)S(1)}) custom-call(bf16[160,1280]{1,0:T(8,128)(2,1)S(1)} %get-tuple-element.27.gate_rows_ref, bf16[160,1280]{1,0:T(8,128)(2,1)S(1)} %get-tuple-element.28.up_rows_ref, bf16[1,2,1280,2048]{3,2,1,0:T(8,128)(2,1)S(1)} %fetch.1.in_ref), custom_call_target="tpu_custom_call" | custom-call | flops 838860800 | bytes 5242880 | tf_op jit(solution)/shard_map/rest_back/pallas_call | solution.py:493
  37.5 0.0 copy-start.1
  37.5 0.1 collective-permute-start.5
  37.6 0.1 multiply_reduce_fusion
  37.7 0.3 fusion.7
  38.0 0.9 %collective-permute-done.5 = bf16[80,1024]{1,0:T(8,128)(2,1)S(1)} collective-permute-done((bf16[80,1024]{1,0:T(8,128)(2,1)S(1)}, bf16[80,1024]{1,0:T(8,128)(2,1)S(1)}, u32[]{:S(2)}, u32[]{:S(2)}) %collective-permute-start.5) | collective-permute-done | bytes 163872 | tf_op jit(solution)/shard_map/ppermute | solution.py:38
  39.0 1.6 %collective-permute-start.6 = (bf16[40,2048]{1,0:T(8,128)(2,1)S(1)}, bf16[40,2048]{1,0:T(8,128)(2,1)S(1)}, u32[]{:S(2)}, u32[]{:S(2)}) collective-permute-start(bf16[40,2048]{1,0:T(8,128)(2,1)S(1)} %fusion.4), channel_id=1, source_target_pairs={{0,16},{8,24},{16,0},{24,8},{1,17},{9,25},{17,1},{25,9},{2,18},{10... | collective-permute-start | bytes 491528 | tf_op jit(solution)/shard_map/ppermute | solution.py:38
  40.5 0.2 fusion.6
  40.7 3.2 %weight_grad_half.2.refs_0_ = bf16[1,2,1280,2048]{3,2,1,0:T(8,128)(2,1)} custom-call(bf16[1280,160]{1,0:T(8,128)(2,1)S(1)} %get-tuple-element.32.grad_ref, bf16[160,2048]{1,0:T(8,128)(2,1)S(1)} %constant_dynamic-update-slice_fusion.rows_ref), custom_call_target="tpu_custom_call" | custom-call | flops 838860800 | bytes 5242880 | tf_op jit(solution)/shard_map/weight_grad_half/pallas_call | solution.py:520
  43.9 0.5 collective-permute-start.8
  44.5 0.8 %collective-permute-done.6 = bf16[40,2048]{1,0:T(8,128)(2,1)S(1)} collective-permute-done((bf16[40,2048]{1,0:T(8,128)(2,1)S(1)}, bf16[40,2048]{1,0:T(8,128)(2,1)S(1)}, u32[]{:S(2)}, u32[]{:S(2)}) %collective-permute-start.6) | collective-permute-done | bytes 163872 | tf_op jit(solution)/shard_map/ppermute | solution.py:38
  45.3 0.7 %copy.20 = bf16[5,8,8,256]{3,2,0,1:T(8,128)(2,1)} copy(bf16[5,8,8,256]{3,2,1,0:T(8,128)(2,1)S(1)} %bitcast.41) | data formatting | bytes 327680 | tf_op jit(solution)/shard_map/reshape | solution.py:577
  46.0 5.3 %all-to-all-start.1 = ((bf16[8,40,256]{2,1,0:T(8,128)(2,1)}), bf16[8,40,256]{2,1,0:T(8,128)(2,1)S(1)}, u32[]{:S(2)}, u32[]{:S(2)}) async-start(bf16[8,40,256]{2,1,0:T(8,128)(2,1)} %bitcast.30), calls=%async_computation.1 | async-start | bytes 327680 | tf_op jit(solution)/shard_map/all_to_all | solution.py:578
  51.3 3.2 %weight_grad_half.3 = bf16[1,2,1280,2048]{3,2,1,0:T(8,128)(2,1)} custom-call(bf16[1280,160]{1,0:T(8,128)(2,1)S(1)} %get-tuple-element.31.grad_ref, bf16[160,2048]{1,0:T(8,128)(2,1)S(1)} %constant_dynamic-update-slice_fusion.rows_ref, bf16[1,2,1280,2048]{3,2,1,0:T(8,128)(2,1)} %weight_grad_half.2.refs_0_), custom_call_target="tpu_custom_call", output_to_operand_aliasing={{}: (2, {})} | custom-call | flops 838860800 | bytes 5242880 | tf_op jit(solution)/shard_map/weight_grad_half/pallas_call | solution.py:520
  54.5 0.6 %add_bitcast_fusion = f32[256,8]{0,1:T(8,128)} fusion(f32[8,256]{1,0:T(8,128)S(1)} %add.32, f32[8,256]{1,0:T(8,128)S(1)} %collective-permute-done.8), kind=kLoop, calls=%fused_computation.21 | loop fusion | flops 2048 | bytes 24576 | tf_op jit(solution)/shard_map/transpose | solution.py:601
  55.1 3.8 %all-to-all-done.1 = bf16[8,40,256]{2,1,0:T(8,128)(2,1)S(1)} async-done(((bf16[8,40,256]{2,1,0:T(8,128)(2,1)}), bf16[8,40,256]{2,1,0:T(8,128)(2,1)S(1)}, u32[]{:S(2)}, u32[]{:S(2)}) %all-to-all-start.1) | async-done | bytes 163872 | tf_op jit(solution)/shard_map/all_to_all | solution.py:578
  58.9 0.9 %fusion = bf16[256,256]{1,0:T(8,128)(2,1)} fusion(f32[256,256]{1,0:T(8,128)S(1)} %fusion.7, bf16[320,256]{1,0:T(8,128)(2,1)S(1)} %get-tuple-element.18, bf16[320,256]{1,0:T(8,128)(2,1)S(1)} %bitcast.40), kind=kOutput, calls=%fused_computation.1 | convolution fusion | flops 42074112 | bytes 720896 | tf_op jit(solution)/shard_map/dot_general | solution.py:594
  (30 shorter events, 0.4 us)
Async XLA Ops:
  0.6 37.0 %copy-start = (bf16[256,8]{0,1:T(8,128)(2,1)S(1)}, bf16[256,8]{0,1:T(8,128)(2,1)}, u32[]{:S(2)}) copy-start(bf16[256,8]{0,1:T(8,128)(2,1)} %param.15) | copy-start | bytes 12292
  21.3 6.3 %collective-permute-start.2 = (bf16[40,2048]{1,0:T(8,128)(2,1)S(1)}, bf16[40,2048]{1,0:T(8,128)(2,1)S(1)}, u32[]{:S(2)}, u32[]{:S(2)}) collective-permute-start(bf16[40,2048]{1,0:T(8,128)(2,1)S(1)} %bitcast.37), channel_id=1, source_target_pairs={{0,16},{8,24},{16,0},{24,8},{1,17},{9,25},{17,1},{25,9},{2,18},{10... | collective-permute-start | bytes 491528 | tf_op jit(solution)/shard_map/ppermute | solution.py:38
  22.9 6.3 %collective-permute-start = (bf16[48,2048]{1,0:T(8,128)(2,1)S(1)}, bf16[48,2048]{1,0:T(8,128)(2,1)S(1)}, u32[]{:S(2)}, u32[]{:S(2)}) collective-permute-start(bf16[48,2048]{1,0:T(8,128)(2,1)S(1)} %bitcast.34), channel_id=1, source_target_pairs={{0,16},{8,24},{16,0},{24,8},{1,17},{9,25},{17,1},{25,9},{2,18},{10... | collective-permute-start | bytes 589832 | tf_op jit(solution)/shard_map/ppermute | solution.py:38
  27.7 1.7 %collective-permute-start.3 = (bf16[80,2048]{1,0:T(8,128)(2,1)S(1)}, bf16[80,2048]{1,0:T(8,128)(2,1)S(1)}, u32[]{:S(2)}, u32[]{:S(2)}) collective-permute-start(bf16[80,2048]{1,0:T(8,128)(2,1)S(1)} %pad_maximum_fusion.3), channel_id=1, source_target_pairs={{0,8},{8,0},{16,24},{24,16},{1,9},{9,1},{17,25},{25,17},{2,10},{10... | collective-permute-start | bytes 983048 | tf_op jit(solution)/shard_map/ppermute | solution.py:38
  29.2 3.9 %collective-permute-start.1 = (bf16[96,2048]{1,0:T(8,128)(2,1)S(1)}, bf16[96,2048]{1,0:T(8,128)(2,1)S(1)}, u32[]{:S(2)}, u32[]{:S(2)}) collective-permute-start(bf16[96,2048]{1,0:T(8,128)(2,1)S(1)} %pad_maximum_fusion.1), channel_id=1, source_target_pairs={{0,8},{8,0},{16,24},{24,16},{1,9},{9,1},{17,25},{25,17},{2,10},{10... | collective-permute-start | bytes 1179656 | tf_op jit(solution)/shard_map/ppermute | solution.py:38
  35.9 2.1 %collective-permute-start.4 = (bf16[80,1024]{1,0:T(8,128)(2,1)S(1)}, bf16[80,1024]{1,0:T(8,128)(2,1)S(1)}, u32[]{:S(2)}, u32[]{:S(2)}) collective-permute-start(bf16[80,1024]{1,0:T(8,128)(2,1)S(1)} %get-tuple-element.26), channel_id=1, source_target_pairs={{0,8},{8,0},{16,24},{24,16},{1,9},{9,1},{17,25},{25,17},{2,10},{10... | collective-permute-start | bytes 491528 | tf_op jit(solution)/shard_map/ppermute | solution.py:38
  36.4 1.1 %copy-start.2 = (f32[256,8]{0,1:T(8,128)S(1)}, f32[256,8]{0,1:T(8,128)}, u32[]{:S(2)}) copy-start(f32[256,8]{0,1:T(8,128)} %param.11) | copy-start | bytes 24580
  36.4 1.1 %copy-start.3 = (s32[256,1]{0,1:T(1,128)S(1)}, s32[256,1]{0,1:T(1,128)}, u32[]{:S(2)}) copy-start(s32[256,1]{0,1:T(1,128)} %param.12) | copy-start | bytes 3076
  37.5 3.1 %copy-start.1 = (bf16[256,256]{1,0:T(8,128)(2,1)S(1)}, bf16[256,256]{1,0:T(8,128)(2,1)}, u32[]{:S(2)}) copy-start(bf16[256,256]{1,0:T(8,128)(2,1)} %tokens_hbm.1) | copy-start | bytes 393220
  37.5 1.5 %collective-permute-start.5 = (bf16[80,1024]{1,0:T(8,128)(2,1)S(1)}, bf16[80,1024]{1,0:T(8,128)(2,1)S(1)}, u32[]{:S(2)}, u32[]{:S(2)}) collective-permute-start(bf16[80,1024]{1,0:T(8,128)(2,1)S(1)} %get-tuple-element.30), channel_id=1, source_target_pairs={{0,8},{8,0},{16,24},{24,16},{1,9},{9,1},{17,25},{25,17},{2,10},{10... | collective-permute-start | bytes 491528 | tf_op jit(solution)/shard_map/ppermute | solution.py:38
  39.0 6.3 %collective-permute-start.6 = (bf16[40,2048]{1,0:T(8,128)(2,1)S(1)}, bf16[40,2048]{1,0:T(8,128)(2,1)S(1)}, u32[]{:S(2)}, u32[]{:S(2)}) collective-permute-start(bf16[40,2048]{1,0:T(8,128)(2,1)S(1)} %fusion.4), channel_id=1, source_target_pairs={{0,16},{8,24},{16,0},{24,8},{1,17},{9,25},{17,1},{25,9},{2,18},{10... | collective-permute-start | bytes 491528 | tf_op jit(solution)/shard_map/ppermute | solution.py:38
  40.7 3.2 %collective-permute-start.7 = (f32[8,256]{1,0:T(8,128)S(1)}, f32[8,256]{1,0:T(8,128)S(1)}, u32[]{:S(2)}, u32[]{:S(2)}) collective-permute-start(f32[8,256]{1,0:T(8,128)S(1)} %fusion.6), channel_id=1, source_target_pairs={{0,8},{8,0},{16,24},{24,16},{1,9},{9,1},{17,25},{25,17},{2,10},{10... | collective-permute-start | bytes 24584 | tf_op jit(solution)/shard_map/ppermute | solution.py:38
  43.9 10.6 %collective-permute-start.8 = (f32[8,256]{1,0:T(8,128)S(1)}, f32[8,256]{1,0:T(8,128)S(1)}, u32[]{:S(2)}, u32[]{:S(2)}) collective-permute-start(f32[8,256]{1,0:T(8,128)S(1)} %add.32), channel_id=1, source_target_pairs={{0,16},{8,24},{16,0},{24,8},{1,17},{9,25},{17,1},{25,9},{2,18},{10... | collective-permute-start | bytes 24584 | tf_op jit(solution)/shard_map/ppermute | solution.py:38
  46.0 12.9 %all-to-all-start.1 = ((bf16[8,40,256]{2,1,0:T(8,128)(2,1)}), bf16[8,40,256]{2,1,0:T(8,128)(2,1)S(1)}, u32[]{:S(2)}, u32[]{:S(2)}) async-start(bf16[8,40,256]{2,1,0:T(8,128)(2,1)} %bitcast.30), calls=%async_computation.1 | async-start | bytes 327680 | tf_op jit(solution)/shard_map/all_to_all | solution.py:578

commit v7 on v6

--- a/solution.py
+++ b/solution.py
@@ -506,6 +506,22 @@
     )(near(gate_rows), near(up_rows), near(in_near))
 
 
+def finish_kernel(mask_ref, rows_ref, term_ref, out_ref):
+    combined = lax.dot_general(
+        mask_ref[...], rows_ref[...], contract_first, preferred_element_type=jnp.float32
+    )
+    out_ref[...] = (combined + term_ref[...]).astype(jnp.bfloat16)
+
+
+def finish(mask, rows, term):
+    return pl.pallas_call(
+        finish_kernel,
+        out_shape=jax.ShapeDtypeStruct(term.shape, jnp.bfloat16),
+        compiler_params=pltpu.CompilerParams(vmem_limit_bytes=4 << 20),
+        name="finish",
+    )(mask, rows, term)
+
+
 def half_kernel(grad_ref, rows_ref, *refs):
     refs[-1][0, 0] = jnp.dot(
         grad_ref[...], rows_ref[...], preferred_element_type=jnp.float32
@@ -591,13 +607,7 @@
     router_term = lax.dot_general(
         logit_grad, router_weight, (((0,), (1,)), ((), ())), preferred_element_type=jnp.float32
     )
-    combined = lax.dot_general(
-        mask,
-        returned.reshape(experts * capacity, width),
-        contract_first,
-        preferred_element_type=jnp.float32,
-    )
-    token_grad = (combined + router_term).astype(jnp.bfloat16)
+    token_grad = finish(mask, returned.reshape(experts * capacity, width), router_term)
     return (token_grad, weight_grad, router_grad.T)
 
 

time: 60.1 us -> 60.8 us (1.012)
  matrix products: 1.39 us -> 0.46 us
  Pallas kernels: 19.8 us -> 20.7 us
    dot_general x1 -> x0, matrix products: 0.92 us -> none  [aligned_device(): lax.dot_general(mask, returned.reshape(experts * capacity, width), contra...]
    pallas_call x0 -> x1, Pallas kernels: none -> 0.92 us  [finish(): pl.pallas_call(finish_kernel, out_shape=jax.ShapeDtypeStruct(term.shape,...]
where the time goes in v7:
time: 60.8 us; the launch traced here: 60.5 us
  Pallas kernels  20.7 us (34%)
  blocking collectives  18.6 us (31%)
  starting transfers between devices  10.8 us (18%)
  waiting for transfers between devices  7.16 us (12%)
  other arithmetic  0.98 us (2%)
  between operations  0.86 us (1%)
  local copies, waits for them, and re-layouts  0.85 us (1%)
    all_to_all x1, blocking collectives, aligned_device(): lax.all_to_all(send, 'expert', split_axis=0, concat_axis=0, tiled=True)  18.6 us
    pallas_call x2, Pallas kernels, half_weight_grad(): pl.pallas_call(half_kernel, grid=(hidden // block,), in_specs=[pl.BlockSp...  6.42 us
    ppermute x9, starting transfers between devices, swap(): return lax.ppermute(value, 'dp', [(i, i ^ distance) for i in range(size)])  5.51 us
    all_to_all x1, starting transfers between devices, aligned_device(): lax.all_to_all(going, 'expert', split_axis=0, concat_axis=0, tiled=True)  5.31 us
    pallas_call x1, Pallas kernels, fetch(): pl.pallas_call(partial(fetch_kernel, pieces), in_specs=[pl.BlockSpec(memo...  4.08 us
    all_to_all x1, waiting for transfers between devices, aligned_device(): lax.all_to_all(going, 'expert', split_axis=0, concat_axis=0, tiled=True)  3.75 us
    ppermute x9, waiting for transfers between devices, swap(): return lax.ppermute(value, 'dp', [(i, i ^ distance) for i in range(size)])  3.41 us
    pallas_call x1, Pallas kernels, hidden_back(): pl.pallas_call(partial(hidden_back_kernel, width // 2), in_specs=[near_sp...  2.57 us
  transfers between devices with their start and end apart: 10, of which 4 were waited for; matrix products, arithmetic and copies ran while one was open for 3% of the time, Pallas kernels for 25%

profile of v7, /device:TPU:0, one launch (start us, length us, event | category | flops | bytes accessed | tf_op | source)
XLA Modules:
  0.0 60.5 jit_solution(17801032919361167693)
XLA Ops:
  0.6 0.0 copy-start
  0.6 2.0 %prelude.1 = (bf16[8,88,256]{2,1,0:T(8,128)(2,1)S(1)}, bf16[320,256]{1,0:T(8,128)(2,1)S(1)}, bf16[640,2048]{1,0:T(8,128)(2,1)S(1)}) custom-call(s32[1,256]{1,0:T(1,128)} %bitcast.41, f32[8,256]{1,0:T(8,128)} %bitcast.40, bf16[256,256]{1,0:T(8,128)(2,1)} %tokens_hbm.1, bf16[256,256]{1,0:T(8,128)(2,1)} %grads_hbm.1, bf16[256,256]{1,0:T(8,128)(2,1)} %expert_out_hbm.1, ...), custom_call_target="tpu_custom_call" | custom-call | tf_op jit(solution)/shard_map/prelude/pallas_call | solution.py:292
  2.7 18.6 %all_to_all.10.after_ref = bf16[8,88,256]{2,1,0:T(8,128)(2,1)S(1)} all-to-all(bf16[8,88,256]{2,1,0:T(8,128)(2,1)S(1)} %get-tuple-element.19), channel_id=1, replica_groups=mesh['dp'=4,'expert'=8] {'expert'}, dimensions={0} | all-to-all | bytes 720896 | tf_op jit(solution)/shard_map/all_to_all | solution.py:568
  21.3 1.6 %collective-permute-start.2 = (bf16[40,2048]{1,0:T(8,128)(2,1)S(1)}, bf16[40,2048]{1,0:T(8,128)(2,1)S(1)}, u32[]{:S(2)}, u32[]{:S(2)}) collective-permute-start(bf16[40,2048]{1,0:T(8,128)(2,1)S(1)} %bitcast.36), channel_id=1, source_target_pairs={{0,16},{8,24},{16,0},{24,8},{1,17},{9,25},{17,1},{25,9},{2,18},{10... | collective-permute-start | bytes 491528 | tf_op jit(solution)/shard_map/ppermute | solution.py:38
  22.9 0.6 collective-permute-start
  23.5 4.1 %fetch.1.in_ref = bf16[1,2,1280,2048]{3,2,1,0:T(8,128)(2,1)S(1)} custom-call(bf16[1,2,1280,2048]{3,2,1,0:T(8,128)(2,1)} %source_ref.1, bf16[8,88,256]{2,1,0:T(8,128)(2,1)S(1)} %all_to_all.10.after_ref), custom_call_target="tpu_custom_call" | custom-call | bytes 10485760 | tf_op jit(solution)/shard_map/fetch/pallas_call | solution.py:328
  27.7 0.1 collective-permute-start.3
  27.7 1.4 %collective-permute-done = bf16[48,2048]{1,0:T(8,128)(2,1)S(1)} collective-permute-done((bf16[48,2048]{1,0:T(8,128)(2,1)S(1)}, bf16[48,2048]{1,0:T(8,128)(2,1)S(1)}, u32[]{:S(2)}, u32[]{:S(2)}) %collective-permute-start) | collective-permute-done | bytes 196640 | tf_op jit(solution)/shard_map/ppermute | solution.py:38
  29.2 0.1 collective-permute-start.1
  29.3 0.0 collective-permute-done.3
  29.4 1.7 %gate_pre.1 = (f32[1280,160]{1,0:T(8,128)S(1)}, bf16[640,2048]{1,0:T(8,128)(2,1)S(1)}) custom-call(bf16[160,2048]{1,0:T(8,128)(2,1)S(1)} %constant_dynamic-update-slice_fusion.rows_ref, bf16[1,2,1280,2048]{3,2,1,0:T(8,128)(2,1)S(1)} %fetch.1.in_ref, bf16[1,1280,2048]{2,1,0:T(8,128)(2,1)} %down_hbm.3), custom_call_target="tpu_custom_call" | custom-call | flops 838860800 | bytes 5242880 | tf_op jit(solution)/shard_map/gate_pre/pallas_call | solution.py:405
  31.1 2.0 %up_pre.1 = (f32[1280,160]{1,0:T(8,128)S(1)}, f32[1280,160]{1,0:T(8,128)S(1)}) custom-call(bf16[160,2048]{1,0:T(8,128)(2,1)S(1)} %constant_dynamic-update-slice_fusion.rows_ref, bf16[1,2,1280,2048]{3,2,1,0:T(8,128)(2,1)S(1)} %fetch.1.in_ref, f32[1280,160]{1,0:T(8,128)S(1)} %get-tuple-element.20.gate_pre_ref), custom_call_target="tpu_custom_call" | custom-call | flops 838860800 | bytes 5242880 | tf_op jit(solution)/shard_map/up_pre/pallas_call | solution.py:398
  33.1 0.1 pad_maximum_fusion
  33.3 2.6 %hidden_back.1 = (bf16[1280,160]{1,0:T(8,128)(2,1)S(1)}, bf16[1280,160]{1,0:T(8,128)(2,1)S(1)}, bf16[160,1280]{1,0:T(8,128)(2,1)S(1)}, bf16[160,1280]{1,0:T(8,12...) custom-call(bf16[160,2048]{1,0:T(8,128)(2,1)S(1)} %bitcast.29, ...), custom_call_target="tpu_custom_call" | custom-call | flops 1677721600 | bytes 10485760 | tf_op jit(solution)/shard_map/hidden_back/pallas_call | solution.py:467
  35.9 0.5 collective-permute-start.4
  36.5 0.1 multiply_reduce_fusion
  36.5 0.2 fusion.5
  36.7 0.1 collective-permute-start.7
  36.8 1.0 %rest_back.1 = (f32[80,1024]{1,0:T(8,128)S(1)}, bf16[80,1024]{1,0:T(8,128)(2,1)S(1)}) custom-call(bf16[160,1280]{1,0:T(8,128)(2,1)S(1)} %get-tuple-element.27.gate_rows_ref, bf16[160,1280]{1,0:T(8,128)(2,1)S(1)} %get-tuple-element.28.up_rows_ref, bf16[1,2,1280,2048]{3,2,1,0:T(8,128)(2,1)S(1)} %fetch.1.in_ref), custom_call_target="tpu_custom_call" | custom-call | flops 838860800 | bytes 5242880 | tf_op jit(solution)/shard_map/rest_back/pallas_call | solution.py:493
  37.8 0.5 collective-permute-start.5
  38.4 1.0 %collective-permute-done.5 = bf16[80,1024]{1,0:T(8,128)(2,1)S(1)} collective-permute-done((bf16[80,1024]{1,0:T(8,128)(2,1)S(1)}, bf16[80,1024]{1,0:T(8,128)(2,1)S(1)}, u32[]{:S(2)}, u32[]{:S(2)}) %collective-permute-start.5) | collective-permute-done | bytes 163872 | tf_op jit(solution)/shard_map/ppermute | solution.py:38
  39.4 1.5 %collective-permute-start.6 = (bf16[40,2048]{1,0:T(8,128)(2,1)S(1)}, bf16[40,2048]{1,0:T(8,128)(2,1)S(1)}, u32[]{:S(2)}, u32[]{:S(2)}) collective-permute-start(bf16[40,2048]{1,0:T(8,128)(2,1)S(1)} %fusion.3), channel_id=1, source_target_pairs={{0,16},{8,24},{16,0},{24,8},{1,17},{9,25},{17,1},{25,9},{2,18},{10... | collective-permute-start | bytes 491528 | tf_op jit(solution)/shard_map/ppermute | solution.py:38
  41.0 0.3 fusion.6.term_ref
  41.3 3.2 %weight_grad_half.2.refs_0_ = bf16[1,2,1280,2048]{3,2,1,0:T(8,128)(2,1)} custom-call(bf16[1280,160]{1,0:T(8,128)(2,1)S(1)} %get-tuple-element.32.grad_ref, bf16[160,2048]{1,0:T(8,128)(2,1)S(1)} %constant_dynamic-update-slice_fusion.rows_ref), custom_call_target="tpu_custom_call" | custom-call | flops 838860800 | bytes 5242880 | tf_op jit(solution)/shard_map/weight_grad_half/pallas_call | solution.py:536
  44.5 0.6 collective-permute-start.8
  45.0 0.9 %collective-permute-done.6 = bf16[40,2048]{1,0:T(8,128)(2,1)S(1)} collective-permute-done((bf16[40,2048]{1,0:T(8,128)(2,1)S(1)}, bf16[40,2048]{1,0:T(8,128)(2,1)S(1)}, u32[]{:S(2)}, u32[]{:S(2)}) %collective-permute-start.6) | collective-permute-done | bytes 163872 | tf_op jit(solution)/shard_map/ppermute | solution.py:38
  46.0 0.7 %copy.21 = bf16[5,8,8,256]{3,2,0,1:T(8,128)(2,1)} copy(bf16[5,8,8,256]{3,2,1,0:T(8,128)(2,1)S(1)} %bitcast.39) | data formatting | bytes 327680 | tf_op jit(solution)/shard_map/reshape | solution.py:593
  46.7 5.3 %all-to-all-start.1 = ((bf16[8,40,256]{2,1,0:T(8,128)(2,1)}), bf16[8,40,256]{2,1,0:T(8,128)(2,1)S(1)}, u32[]{:S(2)}, u32[]{:S(2)}) async-start(bf16[8,40,256]{2,1,0:T(8,128)(2,1)} %bitcast.28), calls=%async_computation.1 | async-start | bytes 327680 | tf_op jit(solution)/shard_map/all_to_all | solution.py:594
  52.0 3.2 %weight_grad_half.3 = bf16[1,2,1280,2048]{3,2,1,0:T(8,128)(2,1)} custom-call(bf16[1280,160]{1,0:T(8,128)(2,1)S(1)} %get-tuple-element.31.grad_ref, bf16[160,2048]{1,0:T(8,128)(2,1)S(1)} %constant_dynamic-update-slice_fusion.rows_ref, bf16[1,2,1280,2048]{3,2,1,0:T(8,128)(2,1)} %weight_grad_half.2.refs_0_), custom_call_target="tpu_custom_call", output_to_operand_aliasing={{}: (2, {})} | custom-call | flops 838860800 | bytes 5242880 | tf_op jit(solution)/shard_map/weight_grad_half/pallas_call | solution.py:536
  55.2 0.6 add_bitcast_fusion
  55.8 3.8 %all-to-all-done.1 = bf16[8,40,256]{2,1,0:T(8,128)(2,1)S(1)} async-done(((bf16[8,40,256]{2,1,0:T(8,128)(2,1)}), bf16[8,40,256]{2,1,0:T(8,128)(2,1)S(1)}, u32[]{:S(2)}, u32[]{:S(2)}) %all-to-all-start.1) | async-done | bytes 163872 | tf_op jit(solution)/shard_map/all_to_all | solution.py:594
  59.6 0.9 %finish.1 = bf16[256,256]{1,0:T(8,128)(2,1)} custom-call(bf16[320,256]{1,0:T(8,128)(2,1)S(1)} %get-tuple-element.18.mask_ref, bf16[320,256]{1,0:T(8,128)(2,1)S(1)} %bitcast.30, f32[256,256]{1,0:T(8,128)S(1)} %fusion.6.term_ref), custom_call_target="tpu_custom_call" | custom-call | tf_op jit(solution)/shard_map/finish/pallas_call | solution.py:517
  (30 shorter events, 0.4 us)
Async XLA Ops:
  0.6 40.3 %copy-start = (bf16[256,8]{0,1:T(8,128)(2,1)S(1)}, bf16[256,8]{0,1:T(8,128)(2,1)}, u32[]{:S(2)}) copy-start(bf16[256,8]{0,1:T(8,128)(2,1)} %param.15) | copy-start | bytes 12292
  21.3 6.3 %collective-permute-start.2 = (bf16[40,2048]{1,0:T(8,128)(2,1)S(1)}, bf16[40,2048]{1,0:T(8,128)(2,1)S(1)}, u32[]{:S(2)}, u32[]{:S(2)}) collective-permute-start(bf16[40,2048]{1,0:T(8,128)(2,1)S(1)} %bitcast.36), channel_id=1, source_target_pairs={{0,16},{8,24},{16,0},{24,8},{1,17},{9,25},{17,1},{25,9},{2,18},{10... | collective-permute-start | bytes 491528 | tf_op jit(solution)/shard_map/ppermute | solution.py:38
  22.9 6.3 %collective-permute-start = (bf16[48,2048]{1,0:T(8,128)(2,1)S(1)}, bf16[48,2048]{1,0:T(8,128)(2,1)S(1)}, u32[]{:S(2)}, u32[]{:S(2)}) collective-permute-start(bf16[48,2048]{1,0:T(8,128)(2,1)S(1)} %bitcast.33), channel_id=1, source_target_pairs={{0,16},{8,24},{16,0},{24,8},{1,17},{9,25},{17,1},{25,9},{2,18},{10... | collective-permute-start | bytes 589832 | tf_op jit(solution)/shard_map/ppermute | solution.py:38
  27.7 1.7 %collective-permute-start.3 = (bf16[80,2048]{1,0:T(8,128)(2,1)S(1)}, bf16[80,2048]{1,0:T(8,128)(2,1)S(1)}, u32[]{:S(2)}, u32[]{:S(2)}) collective-permute-start(bf16[80,2048]{1,0:T(8,128)(2,1)S(1)} %pad_maximum_fusion.3), channel_id=1, source_target_pairs={{0,8},{8,0},{16,24},{24,16},{1,9},{9,1},{17,25},{25,17},{2,10},{10... | collective-permute-start | bytes 983048 | tf_op jit(solution)/shard_map/ppermute | solution.py:38
  29.2 3.9 %collective-permute-start.1 = (bf16[96,2048]{1,0:T(8,128)(2,1)S(1)}, bf16[96,2048]{1,0:T(8,128)(2,1)S(1)}, u32[]{:S(2)}, u32[]{:S(2)}) collective-permute-start(bf16[96,2048]{1,0:T(8,128)(2,1)S(1)} %pad_maximum_fusion.1), channel_id=1, source_target_pairs={{0,8},{8,0},{16,24},{24,16},{1,9},{9,1},{17,25},{25,17},{2,10},{10... | collective-permute-start | bytes 1179656 | tf_op jit(solution)/shard_map/ppermute | solution.py:38
  33.3 3.1 %copy-start.2 = (f32[256,8]{0,1:T(8,128)S(1)}, f32[256,8]{0,1:T(8,128)}, u32[]{:S(2)}) copy-start(f32[256,8]{0,1:T(8,128)} %param.11) | copy-start | bytes 24580
  33.3 3.1 %copy-start.3 = (s32[256,1]{0,1:T(1,128)S(1)}, s32[256,1]{0,1:T(1,128)}, u32[]{:S(2)}) copy-start(s32[256,1]{0,1:T(1,128)} %param.12) | copy-start | bytes 3076
  33.3 3.2 %copy-start.1 = (bf16[256,256]{1,0:T(8,128)(2,1)S(1)}, bf16[256,256]{1,0:T(8,128)(2,1)}, u32[]{:S(2)}) copy-start(bf16[256,256]{1,0:T(8,128)(2,1)} %tokens_hbm.1) | copy-start | bytes 393220
  35.9 2.4 %collective-permute-start.4 = (bf16[80,1024]{1,0:T(8,128)(2,1)S(1)}, bf16[80,1024]{1,0:T(8,128)(2,1)S(1)}, u32[]{:S(2)}, u32[]{:S(2)}) collective-permute-start(bf16[80,1024]{1,0:T(8,128)(2,1)S(1)} %get-tuple-element.26), channel_id=1, source_target_pairs={{0,8},{8,0},{16,24},{24,16},{1,9},{9,1},{17,25},{25,17},{2,10},{10... | collective-permute-start | bytes 491528 | tf_op jit(solution)/shard_map/ppermute | solution.py:38
  36.7 7.8 %collective-permute-start.7 = (f32[8,256]{1,0:T(8,128)S(1)}, f32[8,256]{1,0:T(8,128)S(1)}, u32[]{:S(2)}, u32[]{:S(2)}) collective-permute-start(f32[8,256]{1,0:T(8,128)S(1)} %fusion.5), channel_id=1, source_target_pairs={{0,8},{8,0},{16,24},{24,16},{1,9},{9,1},{17,25},{25,17},{2,10},{10... | collective-permute-start | bytes 24584 | tf_op jit(solution)/shard_map/ppermute | solution.py:38
  37.8 1.6 %collective-permute-start.5 = (bf16[80,1024]{1,0:T(8,128)(2,1)S(1)}, bf16[80,1024]{1,0:T(8,128)(2,1)S(1)}, u32[]{:S(2)}, u32[]{:S(2)}) collective-permute-start(bf16[80,1024]{1,0:T(8,128)(2,1)S(1)} %get-tuple-element.30), channel_id=1, source_target_pairs={{0,8},{8,0},{16,24},{24,16},{1,9},{9,1},{17,25},{25,17},{2,10},{10... | collective-permute-start | bytes 491528 | tf_op jit(solution)/shard_map/ppermute | solution.py:38
  39.4 6.5 %collective-permute-start.6 = (bf16[40,2048]{1,0:T(8,128)(2,1)S(1)}, bf16[40,2048]{1,0:T(8,128)(2,1)S(1)}, u32[]{:S(2)}, u32[]{:S(2)}) collective-permute-start(bf16[40,2048]{1,0:T(8,128)(2,1)S(1)} %fusion.3), channel_id=1, source_target_pairs={{0,16},{8,24},{16,0},{24,8},{1,17},{9,25},{17,1},{25,9},{2,18},{10... | collective-permute-start | bytes 491528 | tf_op jit(solution)/shard_map/ppermute | solution.py:38
  44.5 10.7 %collective-permute-start.8 = (f32[8,256]{1,0:T(8,128)S(1)}, f32[8,256]{1,0:T(8,128)S(1)}, u32[]{:S(2)}, u32[]{:S(2)}) collective-permute-start(f32[8,256]{1,0:T(8,128)S(1)} %add.28), channel_id=1, source_target_pairs={{0,16},{8,24},{16,0},{24,8},{1,17},{9,25},{17,1},{25,9},{2,18},{10... | collective-permute-start | bytes 24584 | tf_op jit(solution)/shard_map/ppermute | solution.py:38
  46.7 12.9 %all-to-all-start.1 = ((bf16[8,40,256]{2,1,0:T(8,128)(2,1)}), bf16[8,40,256]{2,1,0:T(8,128)(2,1)S(1)}, u32[]{:S(2)}, u32[]{:S(2)}) async-start(bf16[8,40,256]{2,1,0:T(8,128)(2,1)} %bitcast.28), calls=%async_computation.1 | async-start | bytes 327680 | tf_op jit(solution)/shard_map/all_to_all | solution.py:594
